TPU v7x, 256 devices: a whole 4x4x8 slice. The times are simulated.
256 devices in a mesh: rows: 16 (over y_hi, x, core), feat: 16 (over y_lo, z).
Axes of the slice: x: 4, y: 4 (y_hi: 2, y_lo: 2; y = y_hi * 2 + y_lo), z: 8, core: 2. Of those that a mesh axis runs over, the one named last changes fastest.
Arguments:
- features: bfloat16 [3072, 16384], P('rows', 'feat'), may hold values from -0.5 to 0.5
- labels: int32 [3072], P('rows'), may hold values 0 or 1
- posterior: bfloat16 [16384], P('feat'), may hold values from -1 to 1
- prior_prec: float32 [16384], P('feat'), may hold values from 1 to 10
Outputs:
- hessian: float32 [16384, 16384], P('feat', 'rows')
- gradient: float32 [16384], P('feat')
All inputs are finite; a program needn't handle non-finite values. No bound on the sum of `labels` on one device may be relied on, other than what follows from the above.
Results may differ from a plain program's by a relative error of at most 0.003.
Values may be sent and summed in bfloat16 or wider, within the bound.
No kernel may reach another device: no remote copies, remote signals or barrier semaphores. Data moves between devices by JAX's collectives and lax.ppermute only.
A program may use at most 64 MiB of HBM per device.

v0:
```python
import jax
import jax.numpy as jnp
from jax import lax
from jax.sharding import PartitionSpec as P


def sent_to_all(x, axis):
    copies = jnp.broadcast_to(x, (lax.axis_size(axis), *x.shape))
    return lax.all_to_all(copies, axis, split_axis=0, concat_axis=0, tiled=True)


def over_copies(x, axis):
    return sent_to_all(x, axis).sum(axis=0)


def side_by_side(arrays, axis, dim, along):
    columns = [a.reshape(*a.shape[:along], -1) for a in arrays]
    both = jnp.concatenate(columns, axis=along)
    whole, at, finished = (lax.all_gather(both, axis, axis=dim, tiled=True), 0, [])
    for a, column in zip(arrays, columns):
        slab = whole[..., at : at + column.shape[along]]
        finished.append(slab.reshape(*slab.shape[:along], *a.shape[along:]))
        at += column.shape[along]
    return tuple(finished)


def per_device(features, labels, posterior, prior_prec):
    row_count = lax.axis_size("rows")
    feat_count = lax.axis_size("feat")
    row_index = lax.axis_index("rows")
    feat_index = lax.axis_index("feat")
    block_width = features.shape[1]
    col_width = block_width * feat_count // row_count
    partial_value = jnp.dot(features, posterior, preferred_element_type=jnp.float32)
    margins = over_copies(partial_value, "feat")
    chance = jax.nn.sigmoid(margins)
    weight = (chance * (1.0 - chance)).astype(jnp.bfloat16)
    residual = (labels.astype(jnp.float32) - chance).astype(jnp.bfloat16)
    all_rows, all_weight = side_by_side((features, weight), "rows", 0, 1)
    local_grad = jnp.dot(residual, features, preferred_element_type=jnp.float32)
    summed = over_copies(local_grad, "rows")
    gradient = summed - prior_prec * posterior.astype(jnp.float32)
    full_width = lax.all_gather(features, "feat", axis=1, tiled=True)
    column_rows = lax.all_to_all(full_width, "rows", split_axis=1, concat_axis=0, tiled=True)
    weighted = all_weight[:, None] * all_rows
    product = lax.dot_general(
        weighted, column_rows, (((0,), (0,)), ((), ())), preferred_element_type=jnp.float32
    )
    global_rows = feat_index * block_width + jnp.arange(block_width, dtype=jnp.int32)
    global_cols = row_index * col_width + jnp.arange(col_width, dtype=jnp.int32)
    on_diagonal = global_rows[:, None] == global_cols[None, :]
    hessian = product + jnp.where(on_diagonal, prior_prec[:, None], jnp.float32(0.0))
    return (hessian, gradient)


def solution(mesh):
    in_specs = (P("rows", "feat"), P("rows"), P("feat"), P("feat"))
    out_specs = (P("feat", "rows"), P("feat"))
    return jax.shard_map(
        per_device, mesh=mesh, in_specs=in_specs, out_specs=out_specs, check_vma=False
    )
```

profile of v0, /device:TPU:64, one launch (start us, length us, event | category | flops | bytes accessed | tf_op | source)
XLA Modules:
  0.0 238.3 jit_solution(10547593554285213768)
XLA Ops:
  7.2 0.0 all-gather.5.cloned.1.call-start
  7.2 0.7 all-gather.5.cloned.1.call-update
  7.9 0.0 all-gather.3.cloned.1.call-start
  7.9 0.7 reshape.56
  8.6 1.2 fusion.3
  9.9 15.3 %all_to_all.31 = f32[16,1,192]{2,1,0:T(1,128)S(1)} all-to-all(f32[16,1,192]{2,1,0:T(1,128)S(1)} %broadcast_in_dim.21), channel_id=1, replica_groups=mesh['rows'=16,'feat'=16] {'feat'}, dimensions={0} | all-to-all | bytes 24576 | tf_op jit(solution)/shard_map/all_to_all | solution.py:9
  25.2 0.7 subtract_convert_fusion
  25.9 0.2 copy.14
  26.0 1.8 pad_maximum_fusion
  27.8 0.0 all-gather.3.cloned.1.call-update
  27.9 1.2 fusion.4
  29.0 0.7 broadcast_in_dim.24
  29.7 6.7 %all-to-all-start.2 = ((f32[16,1,1024]{2,1,0:T(1,128)}), f32[16,1,1024]{2,1,0:T(1,128)S(1)}, u32[]{:S(2)}, u32[]{:S(2)}) async-start(f32[16,1,1024]{2,1,0:T(1,128)} %broadcast_in_dim.24), calls=%async_computation.2 | async-start | bytes 131072 | tf_op jit(solution)/shard_map/all_to_all | solution.py:9
  36.4 56.7 %all-gather.5.cloned.1.call-done = bf16[192,16384]{1,0:T(8,128)(2,1)} async-done(((bf16[192,1024]{1,0:T(8,128)(2,1)}), bf16[192,16384]{1,0:T(8,128)(2,1)}) %all-gather.5.cloned.1.call-update) | async-done | bytes 6291472 | tf_op jit(solution)/shard_map/all_gather | solution.py:43
  93.1 6.4 %copy.21 = bf16[24,16,8,1024]{3,2,0,1:T(8,128)(2,1)} copy(bf16[24,16,8,1024]{3,2,1,0:T(8,128)(2,1)} %bitcast.16) | data formatting | bytes 12582912 | tf_op jit(solution)/shard_map/all_to_all | solution.py:44
  99.5 0.0 all-to-all-done.2
  99.5 6.6 %all-to-all-start.1 = ((bf16[192,16,1024]{2,0,1:T(8,128)(2,1)}), bf16[192,16,1024]{2,0,1:T(8,128)(2,1)}, u32[]{:S(2)}, u32[]{:S(2)}) async-start(bf16[192,16,1024]{2,0,1:T(8,128)(2,1)} %bitcast.15), calls=%async_computation.1 | async-start | bytes 12582912 | tf_op jit(solution)/shard_map/all_to_all | solution.py:44
  106.1 0.1 reduce_sum.19
  106.2 0.0 copy-done
  106.2 0.6 multiply_subtract_fusion
  106.8 110.7 %all-gather.3.cloned.1.call-done = bf16[3072,1025]{1,0:T(8,128)(2,1)} async-done(((bf16[192,1025]{1,0:T(8,128)(2,1)}), bf16[3072,1025]{1,0:T(8,128)(2,1)}) %all-gather.3.cloned.1.call-update) | async-done | bytes 6297616 | tf_op jit(solution)/shard_map/all_gather | solution.py:19
  217.5 1.4 slice_reduce_fusion
  219.0 0.0 all-to-all-done.1
  219.0 12.5 %select_add_fusion = f32[1024,1024]{1,0:T(8,128)} fusion(bf16[3072,1024]{1,0:T(8,128)(2,1)} %bitcast.3, bf16[3072,1025]{1,0:T(8,128)(2,1)} %all-gather.3.cloned.1.call-done, bf16[3072]{0:T(1024)(128)(2,1)S(1)} %slice_reduce_fusion, f32[1024]{0:T(1024)S(1)} %copy-done.1, s32[1024]{0:T(1024)S(1)} %get-tuple-element.4, s32[1024]{0:T(1024)S(1)} %get-tuple-element.5), kind=kOutput, calls=%fused_computation.3 | convolution fusion | flops 6448742400 | bytes 16795648 | tf_op jit(solution)/shard_map/dot_general | solution.py:46
  (8 shorter events, 0.1 us)
Async XLA Ops:
  7.2 85.9 %all-gather.5.cloned.1.call-start = ((), (), s32[]{:S(2)}) async-start(), calls=%async_computation.4 | async-start | bytes 6684672 | tf_op jit(solution)/shard_map/all_gather | solution.py:43
  7.9 209.6 %all-gather.3.cloned.1.call-start = ((), (), s32[]{:S(2)}) async-start(), calls=%async_computation.3 | async-start | bytes 7520256 | tf_op jit(solution)/shard_map/all_gather | solution.py:19
  29.7 69.8 %all-to-all-start.2 = ((f32[16,1,1024]{2,1,0:T(1,128)}), f32[16,1,1024]{2,1,0:T(1,128)S(1)}, u32[]{:S(2)}, u32[]{:S(2)}) async-start(f32[16,1,1024]{2,1,0:T(1,128)} %broadcast_in_dim.24), calls=%async_computation.2 | async-start | bytes 131072 | tf_op jit(solution)/shard_map/all_to_all | solution.py:9
  99.5 6.7 %copy-start = (bf16[1024]{0:T(1024)(128)(2,1)S(1)}, bf16[1024]{0:T(1024)(128)(2,1)}, u32[]{:S(2)}) copy-start(bf16[1024]{0:T(1024)(128)(2,1)} %param.6) | copy-start | bytes 6148
  99.5 6.7 %copy-start.1 = (f32[1024]{0:T(1024)S(1)}, f32[1024]{0:T(1024)}, u32[]{:S(2)}) copy-start(f32[1024]{0:T(1024)} %param.7) | copy-start | bytes 12292
  99.5 119.4 %all-to-all-start.1 = ((bf16[192,16,1024]{2,0,1:T(8,128)(2,1)}), bf16[192,16,1024]{2,0,1:T(8,128)(2,1)}, u32[]{:S(2)}, u32[]{:S(2)}) async-start(bf16[192,16,1024]{2,0,1:T(8,128)(2,1)} %bitcast.15), calls=%async_computation.1 | async-start | bytes 12582912 | tf_op jit(solution)/shard_map/all_to_all | solution.py:44
Sparse Core Ops, SparseCore 0:
  9.8 83.2 all-gather.4
  96.4 121.0 all-gather.2
where the time goes:
time: 243 us; the launch traced here: 238 us
  waiting for transfers between devices  168 us (69%)
  blocking collectives  15.3 us (6%)
  matrix products  14.8 us (6%)
  between operations  14.1 us (6%)
  starting transfers between devices  13.4 us (6%)
  local copies, waits for them, and re-layouts  9.38 us (4%)
  other arithmetic  3.19 us (1%)
    all_gather x1, waiting for transfers between devices, side_by_side(): lax.all_gather(both, axis, axis=dim, tiled=True)  111 us
    all_gather x1, waiting for transfers between devices, per_device(): full_width = lax.all_gather(features, 'feat', axis=1, tiled=True)  56.7 us
    all_to_all x1, blocking collectives, sent_to_all(): return lax.all_to_all(copies, axis, split_axis=0, concat_axis=0, tiled=True)  15.3 us
    dot_general x1, matrix products, per_device(): lax.dot_general(weighted, column_rows, (((0,), (0,)), ((), ())), preferre...  12.5 us
    all_to_all x1, starting transfers between devices, sent_to_all(): return lax.all_to_all(copies, axis, split_axis=0, concat_axis=0, tiled=True)  6.74 us
    all_to_all x1, starting transfers between devices, per_device(): lax.all_to_all(full_width, 'rows', split_axis=1, concat_axis=0, tiled=True)  6.58 us
    all_to_all x1, local copies, waits for them, and re-layouts, per_device(): lax.all_to_all(full_width, 'rows', split_axis=1, concat_axis=0, tiled=True)  6.42 us
  transfers between devices with their start and end apart: 4, of which 2 were waited for; matrix products, arithmetic and copies ran while one was open for 6% of the time, Pallas kernels for 0%

commit v1 on v0

v1 whole, which is shorter than its diff:
```python
import jax
import jax.numpy as jnp
from jax import lax
from jax.sharding import PartitionSpec as P

SIZES = dict(yh=2, x=4, c=2, yl=2, z=8)


def place_of(index):
    r, f = divmod(index, 16)
    return dict(yh=r // 8, x=r // 2 % 4, c=r % 2, yl=f // 8, z=f % 8)


def index_of(p):
    return (p["yh"] * 8 + p["x"] * 2 + p["c"]) * 16 + p["yl"] * 8 + p["z"]


def permuted(x, move):
    pairs = []
    for i in range(256):
        p = place_of(i)
        pairs.append((i, index_of(move(p))))
    return lax.ppermute(x, ("rows", "feat"), pairs)


def shift(x, axis, by):
    def move(p):
        return {**p, axis: (p[axis] + by) % SIZES[axis]}

    return permuted(x, move)


def swap(x, axis, bit=1):
    def move(p):
        return {**p, axis: p[axis] ^ bit}

    return permuted(x, move)


def transposed(x):
    pairs = [(a * 16 + b, b * 16 + a) for a in range(16) for b in range(16)]
    return lax.ppermute(x, ("rows", "feat"), pairs)


BITS_FEAT = (("z", 1), ("z", 2), ("z", 4), ("yl", 1))
BITS_ROWS = (("c", 1), ("x", 1), ("x", 2), ("yh", 1))


def per_device(features, labels, posterior, prior_prec):
    n, width = features.shape
    a = n * 5 // 12
    row_index = lax.axis_index("rows")
    feat_index = lax.axis_index("feat")
    core, x, yh = row_index % 2, row_index // 2 % 4, row_index // 8
    z, yl = feat_index % 8, feat_index // 8

    margins = jnp.dot(features, posterior, preferred_element_type=jnp.float32)
    for axis, bit in BITS_FEAT:
        margins = margins + swap(margins, axis, bit)
    facts = jnp.stack([margins, labels.astype(jnp.float32)])
    facts = lax.dynamic_update_slice(
        jnp.zeros((16, 2, n), jnp.float32), facts[None], (row_index, 0, 0)
    )
    for axis, bit in BITS_ROWS:
        facts = facts + swap(facts, axis, bit)

    mine = transposed(features)
    first, second = mine[:a], mine[a:]
    first = jnp.stack([first, swap(first, "yl")])
    ups, downs = [first], [first]
    up_b, down_b = [second], [second]
    for k in range(1, 4):
        ups.append(shift(ups[-1], "z", 1))
        downs.append(shift(downs[-1], "z", -1))
        up_b.append(shift(up_b[-1], "z", 1))
        down_b.append(shift(down_b[-1], "z", -1))
    ups.append(shift(ups[-1], "z", 1))
    down_b.append(shift(down_b[-1], "z", -1))
    right = jnp.zeros((16, n, width), features.dtype)

    def at(yl_, z_):
        return ((z_ % 2) ^ core) * 8 + yl_ * 4 + z_ // 2

    def put(buffer, piece, yl_, z_, offset):
        return lax.dynamic_update_slice(buffer, piece[None], (at(yl_, z_), offset, 0))

    for k in range(5):
        held = [(ups[k], (z - k) % 8)]
        if 0 < k < 4:
            held.append((downs[k], (z + k) % 8))
        for pair, zz in held:
            right = put(right, pair[0], yl, zz, 0)
            right = put(right, pair[1], 1 - yl, zz, 0)
        held = [(down_b[k], (z + k) % 8)]
        if 0 < k < 4:
            held.append((up_b[k], (z - k) % 8))
        for piece, zz in held:
            right = put(right, piece, yl, zz, a)
            right = put(right, swap(piece, "yl"), 1 - yl, zz, a)

    across = swap(features, "yh")
    left_own, right_own = shift(features, "x", 1), shift(features, "x", -1)
    left_far, right_far = shift(across, "x", 1), shift(across, "x", -1)
    twice_own, twice_far = shift(left_own, "x", 1), shift(right_far, "x", -1)
    same_core = jnp.zeros((8, n, width), features.dtype)
    for piece, yh_, x_ in (
        (features, yh, x),
        (across, 1 - yh, x),
        (left_own, yh, (x + 3) % 4),
        (right_own, yh, (x + 1) % 4),
        (left_far, 1 - yh, (x + 3) % 4),
        (right_far, 1 - yh, (x + 1) % 4),
        (twice_own, yh, (x + 2) % 4),
        (twice_far, 1 - yh, (x + 2) % 4),
    ):
        same_core = lax.dynamic_update_slice(same_core, piece[None], (yh_ * 4 + x_, 0, 0))
    other_core = swap(same_core, "c")
    left = jnp.concatenate([same_core, other_core]).reshape(16 * n, width)

    by_core = facts.reshape(8, 2, 2, n).transpose(1, 2, 0, 3)
    by_core = jnp.where(core == 0, by_core, by_core[::-1])
    margins, label = by_core[:, 0].reshape(-1), by_core[:, 1].reshape(-1)
    chance = jax.nn.sigmoid(margins)
    weight = (chance * (1.0 - chance)).astype(jnp.bfloat16)
    residual = (label - chance).astype(jnp.bfloat16)

    gradient = jnp.dot(residual, left, preferred_element_type=jnp.float32)
    gradient = gradient - prior_prec * posterior.astype(jnp.float32)

    weighted = weight[:, None] * left
    product = lax.dot_general(
        weighted,
        right.reshape(16 * n, width),
        (((0,), (0,)), ((), ())),
        preferred_element_type=jnp.float32,
    )
    global_rows = feat_index * width + jnp.arange(width, dtype=jnp.int32)
    global_cols = row_index * width + jnp.arange(width, dtype=jnp.int32)
    on_diagonal = global_rows[:, None] == global_cols[None, :]
    hessian = product + jnp.where(on_diagonal, prior_prec[:, None], jnp.float32(0.0))
    return (hessian, gradient)


def solution(mesh):
    in_specs = (P("rows", "feat"), P("rows"), P("feat"), P("feat"))
    out_specs = (P("feat", "rows"), P("feat"))
    return jax.shard_map(
        per_device, mesh=mesh, in_specs=in_specs, out_specs=out_specs, check_vma=False
    )
```

time: 243 us -> 175 us (0.72)
  waiting for transfers between devices: 168 us -> 74.1 us
  starting transfers between devices: 13.4 us -> 64.5 us
  blocking collectives: 15.3 us -> 0 us
  between operations: 14.1 us -> 1.25 us
  other arithmetic: 3.19 us -> 8.71 us
  matrix products: 14.8 us -> 11 us
  local copies, waits for them, and re-layouts: 9.38 us -> 12.1 us
    all_gather x2 -> x0, waiting for transfers between devices: 167 us -> none  [the longest x1 111 us: side_by_side(): lax.all_gather(both, axis, axis=dim, tiled=True)]
    ppermute x0 -> x40, waiting for transfers between devices: none -> 74.1 us  [the longest x39 74.1 us: permuted(): return lax.ppermute(x, ('rows', 'feat'), pairs)]
    ppermute x0 -> x40, starting transfers between devices: none -> 64.5 us  [the longest x39 60.8 us: permuted(): return lax.ppermute(x, ('rows', 'feat'), pairs)]
    all_to_all x1 -> x0, blocking collectives: 15.3 us -> none  [sent_to_all(): return lax.all_to_all(copies, axis, split_axis=0, concat_axis=0, tiled=True)]
    all_to_all x2 -> x0, starting transfers between devices: 13.3 us -> none  [the longest x1 6.74 us: sent_to_all(): return lax.all_to_all(copies, axis, split_axis=0, concat_axis=0, tiled=True)]
    all_to_all x1 -> x0, local copies, waits for them, and re-layouts: 6.42 us -> none  [per_device(): lax.all_to_all(full_width, 'rows', split_axis=1, concat_axis=0, tiled=True)]
    add x1 -> x10, other arithmetic: 0.01 us -> 5.47 us  [the longest x4 4.86 us: per_device(): facts = facts + swap(facts, axis, bit)]
    dynamic_update_slice x0 -> x40, local copies, waits for them, and re-layouts: none -> 4.84 us  [the longest x8 4.23 us: per_device(): lax.dynamic_update_slice(same_core, piece[None], (yh_ * 4 + x_, 0, 0))]
  transfers between devices with their start and end apart: 4 -> 40, of which waited for: 2 -> 16; matrix products, arithmetic and copies ran while one was open for 6% -> 8% of each run, Pallas kernels for 0% -> 0%
where the time goes in v1:
time: 175 us; the launch traced here: 172 us
  waiting for transfers between devices  74.1 us (42%)
  starting transfers between devices  64.5 us (37%)
  local copies, waits for them, and re-layouts  12.1 us (7%)
  matrix products  11 us (6%)
  other arithmetic  8.71 us (5%)
    ppermute x39, waiting for transfers between devices, permuted(): return lax.ppermute(x, ('rows', 'feat'), pairs)  74.1 us
    ppermute x39, starting transfers between devices, permuted(): return lax.ppermute(x, ('rows', 'feat'), pairs)  60.8 us
    dot_general x1, matrix products, per_device(): lax.dot_general(weighted, right.reshape(16 * n, width), (((0,), (0,)), ((...  8.94 us
    unnamed x13, local copies, waits for them, and re-layouts  5.24 us
    add x4, other arithmetic, per_device(): facts = facts + swap(facts, axis, bit)  4.86 us
    dynamic_update_slice x8, local copies, waits for them, and re-layouts, per_device(): lax.dynamic_update_slice(same_core, piece[None], (yh_ * 4 + x_, 0, 0))  4.23 us
    ppermute x1, starting transfers between devices, transposed(): return lax.ppermute(x, ('rows', 'feat'), pairs)  3.75 us
  transfers between devices with their start and end apart: 40, of which 16 were waited for; matrix products, arithmetic and copies ran while one was open for 8% of the time, Pallas kernels for 0%

profile of v1, /device:TPU:64, one launch (start us, length us, event | category | flops | bytes accessed | tf_op | source)
XLA Modules:
  0.0 171.7 jit_solution(5668939179382053327)
XLA Ops:
  7.5 3.1 %collective-permute-done.1 = f32[192]{0:T(256)S(1)} collective-permute-done((f32[192]{0:T(256)S(1)}, f32[192]{0:T(256)S(1)}, u32[]{:S(2)}, u32[]{:S(2)}) %collective-permute-start.1) | collective-permute-done | bytes 800 | tf_op jit(solution)/shard_map/ppermute | solution.py:23
  10.6 5.4 %collective-permute-start.2 = (f32[192]{0:T(256)S(1)}, f32[192]{0:T(256)S(1)}, u32[]{:S(2)}, u32[]{:S(2)}) collective-permute-start(f32[192]{0:T(256)S(1)} %add.463), channel_id=1, source_target_pairs={{0,4},{1,5},{2,6},{3,7},{4,0},{5,1},{6,2},{7,3},{8,12},{9,13},{10,... | collective-permute-start | bytes 2312 | tf_op jit(solution)/shard_map/ppermute | solution.py:23
  21.8 3.8 %collective-permute-start.16 = (bf16[192,1024]{1,0:T(8,128)(2,1)}, bf16[192,1024]{1,0:T(8,128)(2,1)S(1)}, u32[]{:S(2)}, u32[]{:S(2)}) collective-permute-start(bf16[192,1024]{1,0:T(8,128)(2,1)} %param.4), channel_id=1, source_target_pairs={{0,0},{1,16},{2,32},{3,48},{4,64},{5,80},{6,96},{7,112},{8,128},{9... | collective-permute-start | bytes 1179656 | tf_op jit(solution)/shard_map/ppermute | solution.py:42
  25.5 3.2 %collective-permute-start.8 = (bf16[192,1024]{1,0:T(8,128)(2,1)}, bf16[192,1024]{1,0:T(8,128)(2,1)}, u32[]{:S(2)}, u32[]{:S(2)}) collective-permute-start(bf16[192,1024]{1,0:T(8,128)(2,1)} %param.4), channel_id=1, source_target_pairs={{0,128},{1,129},{2,130},{3,131},{4,132},{5,133},{6,134},{7,135},{8... | collective-permute-start | bytes 1179656 | tf_op jit(solution)/shard_map/ppermute | solution.py:23
  28.9 6.9 %collective-permute-start.10 = (bf16[192,1024]{1,0:T(8,128)(2,1)}, bf16[192,1024]{1,0:T(8,128)(2,1)}, u32[]{:S(2)}, u32[]{:S(2)}) collective-permute-start(bf16[192,1024]{1,0:T(8,128)(2,1)} %param.4), channel_id=1, source_target_pairs={{0,96},{1,97},{2,98},{3,99},{4,100},{5,101},{6,102},{7,103},{8,104... | collective-permute-start | bytes 1179656 | tf_op jit(solution)/shard_map/ppermute | solution.py:23
  38.5 17.6 %collective-permute-done.5 = f32[16,2,192]{2,1,0:T(2,128)} collective-permute-done((f32[16,2,192]{2,1,0:T(2,128)}, f32[16,2,192]{2,1,0:T(2,128)}, u32[]{:S(2)}, u32[]{:S(2)}) %collective-permute-start.5) | collective-permute-done | bytes 24608 | tf_op jit(solution)/shard_map/ppermute | solution.py:23
  57.6 5.7 %collective-permute-done.6 = f32[16,2,192]{2,1,0:T(2,128)} collective-permute-done((f32[16,2,192]{2,1,0:T(2,128)}, f32[16,2,192]{2,1,0:T(2,128)}, u32[]{:S(2)}, u32[]{:S(2)}) %collective-permute-start.6) | collective-permute-done | bytes 24608 | tf_op jit(solution)/shard_map/ppermute | solution.py:23
  64.7 2.9 %collective-permute-start.7 = (f32[16,2,192]{2,1,0:T(2,128)}, f32[16,2,192]{2,1,0:T(2,128)}, u32[]{:S(2)}, u32[]{:S(2)}) collective-permute-start(f32[16,2,192]{2,1,0:T(2,128)} %add.469), channel_id=1, source_target_pairs={{0,128},{1,129},{2,130},{3,131},{4,132},{5,133},{6,134},{7,135},{8... | collective-permute-start | bytes 73736 | tf_op jit(solution)/shard_map/ppermute | solution.py:23
  74.0 2.9 %collective-permute-start.18 = (bf16[112,1024]{1,0:T(8,128)(2,1)S(1)}, bf16[112,1024]{1,0:T(8,128)(2,1)S(1)}, u32[]{:S(2)}, u32[]{:S(2)}) collective-permute-start(bf16[112,1024]{1,0:T(8,128)(2,1)S(1)} %slice.74), channel_id=1, source_target_pairs={{0,8},{1,9},{2,10},{3,11},{4,12},{5,13},{6,14},{7,15},{8,0},{9,1},... | collective-permute-start | bytes 688136 | tf_op jit(solution)/shard_map/ppermute | solution.py:23
  77.0 2.5 %collective-permute-start.23 = (bf16[112,1024]{1,0:T(8,128)(2,1)S(1)}, bf16[112,1024]{1,0:T(8,128)(2,1)S(1)}, u32[]{:S(2)}, u32[]{:S(2)}) collective-permute-start(bf16[112,1024]{1,0:T(8,128)(2,1)S(1)} %slice.74), channel_id=1, source_target_pairs={{0,1},{1,2},{2,3},{3,4},{4,5},{5,6},{6,7},{7,0},{8,9},{9,10},{10,1... | collective-permute-start | bytes 688136 | tf_op jit(solution)/shard_map/ppermute | solution.py:23
  88.2 6.7 %collective-permute-done.11 = bf16[192,1024]{1,0:T(8,128)(2,1)S(1)} collective-permute-done((bf16[192,1024]{1,0:T(8,128)(2,1)}, bf16[192,1024]{1,0:T(8,128)(2,1)S(1)}, u32[]{:S(2)}, u32[]{:S(2)}) %collective-permute-start.11) | collective-permute-done | bytes 393248 | tf_op jit(solution)/shard_map/ppermute | solution.py:23
  94.9 2.9 %collective-permute-start.19 = (bf16[2,80,1024]{2,1,0:T(8,128)(2,1)S(1)}, bf16[2,80,1024]{2,1,0:T(8,128)(2,1)S(1)}, u32[]{:S(2)}, u32[]{:S(2)}) collective-permute-start(bf16[2,80,1024]{2,1,0:T(8,128)(2,1)S(1)} %pad_maximum_fusion.1), channel_id=1, source_target_pairs={{0,1},{1,2},{2,3},{3,4},{4,5},{5,6},{6,7},{7,0},{8,9},{9,10},{10,1... | collective-permute-start | bytes 983048 | tf_op jit(solution)/shard_map/ppermute | solution.py:23
  103.8 2.5 %collective-permute-start.29 = (bf16[112,1024]{1,0:T(8,128)(2,1)S(1)}, bf16[112,1024]{1,0:T(8,128)(2,1)S(1)}, u32[]{:S(2)}, u32[]{:S(2)}) collective-permute-start(bf16[112,1024]{1,0:T(8,128)(2,1)S(1)} %collective-permute-done.23), channel_id=1, source_target_pairs={{0,1},{1,2},{2,3},{3,4},{4,5},{5,6},{6,7},{7,0},{8,9},{9,10},{10,1... | collective-permute-start | bytes 688136 | tf_op jit(solution)/shard_map/ppermute | solution.py:23
  106.3 3.6 %collective-permute-done.27 = bf16[112,1024]{1,0:T(8,128)(2,1)S(1)} collective-permute-done((bf16[112,1024]{1,0:T(8,128)(2,1)S(1)}, bf16[112,1024]{1,0:T(8,128)(2,1)S(1)}, u32[]{:S(2)}, u32[]{:S(2)}) %collective-permute-start.27) | collective-permute-done | bytes 229408 | tf_op jit(solution)/shard_map/ppermute | solution.py:23
  112.2 3.2 %collective-permute-start.30 = (bf16[112,1024]{1,0:T(8,128)(2,1)S(1)}, bf16[112,1024]{1,0:T(8,128)(2,1)S(1)}, u32[]{:S(2)}, u32[]{:S(2)}) collective-permute-start(bf16[112,1024]{1,0:T(8,128)(2,1)S(1)} %collective-permute-done.29), channel_id=1, source_target_pairs={{0,8},{1,9},{2,10},{3,11},{4,12},{5,13},{6,14},{7,15},{8,0},{9,1},... | collective-permute-start | bytes 688136 | tf_op jit(solution)/shard_map/ppermute | solution.py:23
  115.5 2.6 %collective-permute-start.25 = (bf16[2,80,1024]{2,1,0:T(8,128)(2,1)S(1)}, bf16[2,80,1024]{2,1,0:T(8,128)(2,1)S(1)}, u32[]{:S(2)}, u32[]{:S(2)}) collective-permute-start(bf16[2,80,1024]{2,1,0:T(8,128)(2,1)S(1)} %collective-permute-done.19), channel_id=1, source_target_pairs={{0,1},{1,2},{2,3},{3,4},{4,5},{5,6},{6,7},{7,0},{8,9},{9,10},{10,1... | collective-permute-start | bytes 983048 | tf_op jit(solution)/shard_map/ppermute | solution.py:23
  122.7 4.4 %collective-permute-done.26 = bf16[2,80,1024]{2,1,0:T(8,128)(2,1)S(1)} collective-permute-done((bf16[2,80,1024]{2,1,0:T(8,128)(2,1)S(1)}, bf16[2,80,1024]{2,1,0:T(8,128)(2,1)S(1)}, u32[]{:S(2)}, u32[]{:S(2)}) %collective-permute-start.26) | collective-permute-done | bytes 327712 | tf_op jit(solution)/shard_map/ppermute | solution.py:23
  127.2 3.4 %collective-permute-start.31 = (bf16[2,80,1024]{2,1,0:T(8,128)(2,1)S(1)}, bf16[2,80,1024]{2,1,0:T(8,128)(2,1)S(1)}, u32[]{:S(2)}, u32[]{:S(2)}) collective-permute-start(bf16[2,80,1024]{2,1,0:T(8,128)(2,1)S(1)} %collective-permute-done.25), channel_id=1, source_target_pairs={{0,1},{1,2},{2,3},{3,4},{4,5},{5,6},{6,7},{7,0},{8,9},{9,10},{10,1... | collective-permute-start | bytes 983048 | tf_op jit(solution)/shard_map/ppermute | solution.py:23
  132.6 5.9 %collective-permute-done.38 = bf16[112,1024]{1,0:T(8,128)(2,1)S(1)} collective-permute-done((bf16[112,1024]{1,0:T(8,128)(2,1)S(1)}, bf16[112,1024]{1,0:T(8,128)(2,1)S(1)}, u32[]{:S(2)}, u32[]{:S(2)}) %collective-permute-start.38) | collective-permute-done | bytes 229408 | tf_op jit(solution)/shard_map/ppermute | solution.py:23
  140.6 7.1 %collective-permute-done.32 = bf16[2,80,1024]{2,1,0:T(8,128)(2,1)S(1)} collective-permute-done((bf16[2,80,1024]{2,1,0:T(8,128)(2,1)S(1)}, bf16[2,80,1024]{2,1,0:T(8,128)(2,1)S(1)}, u32[]{:S(2)}, u32[]{:S(2)}) %collective-permute-start.32) | collective-permute-done | bytes 327712 | tf_op jit(solution)/shard_map/ppermute | solution.py:23
  147.6 3.0 %collective-permute-start.37 = (bf16[2,80,1024]{2,1,0:T(8,128)(2,1)S(1)}, bf16[2,80,1024]{2,1,0:T(8,128)(2,1)S(1)}, u32[]{:S(2)}, u32[]{:S(2)}) collective-permute-start(bf16[2,80,1024]{2,1,0:T(8,128)(2,1)S(1)} %collective-permute-done.31), channel_id=1, source_target_pairs={{0,1},{1,2},{2,3},{3,4},{4,5},{5,6},{6,7},{7,0},{8,9},{9,10},{10,1... | collective-permute-start | bytes 983048 | tf_op jit(solution)/shard_map/ppermute | solution.py:23
  150.8 5.8 %collective-permute-done.37 = bf16[2,80,1024]{2,1,0:T(8,128)(2,1)S(1)} collective-permute-done((bf16[2,80,1024]{2,1,0:T(8,128)(2,1)S(1)}, bf16[2,80,1024]{2,1,0:T(8,128)(2,1)S(1)}, u32[]{:S(2)}, u32[]{:S(2)}) %collective-permute-start.37) | collective-permute-done | bytes 327712 | tf_op jit(solution)/shard_map/ppermute | solution.py:23
  156.7 2.7 %copy-done = bf16[16,192,1024]{2,1,0:T(8,128)(2,1)} copy-done((bf16[16,192,1024]{2,1,0:T(8,128)(2,1)}, bf16[16,192,1024]{2,1,0:T(8,128)(2,1)S(1)}, u32[]{:S(2)}) %copy-start) | copy-done | bytes 6291480
  162.7 8.9 %bitcast_add_fusion = f32[1024,1024]{1,0:T(8,128)} fusion(bf16[16,192,1024]{2,1,0:T(8,128)(2,1)S(1)} %copy-done.1, bf16[16,192]{1,0:T(8,128)(2,1)S(1)} %fusion.5, f32[1024]{0:T(1024)S(1)} %copy-done.4, s32[1024]{0:T(1024)S(1)} %iota_add_fusion, s32[1024]{0:T(1024)S(1)} %copy-done.5, bf16[8,192,1024]{2,1,0:T(8,128)(2,1)S(1)} %collective-permute-done.15, ...), kind=kOutput, calls=%fused_computation.3 | convolution fusion | flops 6451888128 | bytes 16795648 | tf_op jit(solution)/shard_map/dot_general | solution.py:131
  (137 shorter events, 53.8 us)
Async XLA Ops:
  21.7 14.2 %collective-permute-start.4 = (f32[16,2,192]{2,1,0:T(2,128)S(1)}, f32[16,2,192]{2,1,0:T(2,128)}, u32[]{:S(2)}, u32[]{:S(2)}) collective-permute-start(f32[16,2,192]{2,1,0:T(2,128)S(1)} %constant_dynamic-update-slice_fusion.3), channel_id=1, source_target_pairs={{0,16},{1,17},{2,18},{3,19},{4,20},{5,21},{6,22},{7,23},{8,24},{9,... | collective-permute-start | bytes 73736 | tf_op jit(solution)/shard_map/ppermute | solution.py:23
  21.8 52.2 %collective-permute-start.16 = (bf16[192,1024]{1,0:T(8,128)(2,1)}, bf16[192,1024]{1,0:T(8,128)(2,1)S(1)}, u32[]{:S(2)}, u32[]{:S(2)}) collective-permute-start(bf16[192,1024]{1,0:T(8,128)(2,1)} %param.4), channel_id=1, source_target_pairs={{0,0},{1,16},{2,32},{3,48},{4,64},{5,80},{6,96},{7,112},{8,128},{9... | collective-permute-start | bytes 1179656 | tf_op jit(solution)/shard_map/ppermute | solution.py:42
  25.5 51.4 %collective-permute-start.8 = (bf16[192,1024]{1,0:T(8,128)(2,1)}, bf16[192,1024]{1,0:T(8,128)(2,1)}, u32[]{:S(2)}, u32[]{:S(2)}) collective-permute-start(bf16[192,1024]{1,0:T(8,128)(2,1)} %param.4), channel_id=1, source_target_pairs={{0,128},{1,129},{2,130},{3,131},{4,132},{5,133},{6,134},{7,135},{8... | collective-permute-start | bytes 1179656 | tf_op jit(solution)/shard_map/ppermute | solution.py:23
  28.7 51.9 %collective-permute-start.9 = (bf16[192,1024]{1,0:T(8,128)(2,1)}, bf16[192,1024]{1,0:T(8,128)(2,1)}, u32[]{:S(2)}, u32[]{:S(2)}) collective-permute-start(bf16[192,1024]{1,0:T(8,128)(2,1)} %param.4), channel_id=1, source_target_pairs={{0,32},{1,33},{2,34},{3,35},{4,36},{5,37},{6,38},{7,39},{8,40},{9,... | collective-permute-start | bytes 1179656 | tf_op jit(solution)/shard_map/ppermute | solution.py:23
  28.9 53.0 %collective-permute-start.10 = (bf16[192,1024]{1,0:T(8,128)(2,1)}, bf16[192,1024]{1,0:T(8,128)(2,1)}, u32[]{:S(2)}, u32[]{:S(2)}) collective-permute-start(bf16[192,1024]{1,0:T(8,128)(2,1)} %param.4), channel_id=1, source_target_pairs={{0,96},{1,97},{2,98},{3,99},{4,100},{5,101},{6,102},{7,103},{8,104... | collective-permute-start | bytes 1179656 | tf_op jit(solution)/shard_map/ppermute | solution.py:23
  37.1 19.0 %collective-permute-start.5 = (f32[16,2,192]{2,1,0:T(2,128)}, f32[16,2,192]{2,1,0:T(2,128)}, u32[]{:S(2)}, u32[]{:S(2)}) collective-permute-start(f32[16,2,192]{2,1,0:T(2,128)} %constant_dynamic-update-slice_fusion.2), channel_id=1, source_target_pairs={{0,32},{1,33},{2,34},{3,35},{4,36},{5,37},{6,38},{7,39},{8,40},{9,... | collective-permute-start | bytes 73736 | tf_op jit(solution)/shard_map/ppermute | solution.py:23
  74.0 13.3 %collective-permute-start.18 = (bf16[112,1024]{1,0:T(8,128)(2,1)S(1)}, bf16[112,1024]{1,0:T(8,128)(2,1)S(1)}, u32[]{:S(2)}, u32[]{:S(2)}) collective-permute-start(bf16[112,1024]{1,0:T(8,128)(2,1)S(1)} %slice.74), channel_id=1, source_target_pairs={{0,8},{1,9},{2,10},{3,11},{4,12},{5,13},{6,14},{7,15},{8,0},{9,1},... | collective-permute-start | bytes 688136 | tf_op jit(solution)/shard_map/ppermute | solution.py:23
  77.0 20.9 %collective-permute-start.21 = (bf16[112,1024]{1,0:T(8,128)(2,1)S(1)}, bf16[112,1024]{1,0:T(8,128)(2,1)S(1)}, u32[]{:S(2)}, u32[]{:S(2)}) collective-permute-start(bf16[112,1024]{1,0:T(8,128)(2,1)S(1)} %slice.74), channel_id=1, source_target_pairs={{0,7},{1,0},{2,1},{3,2},{4,3},{5,4},{6,5},{7,6},{8,15},{9,8},{10,9... | collective-permute-start | bytes 688136 | tf_op jit(solution)/shard_map/ppermute | solution.py:23
  77.0 23.3 %collective-permute-start.23 = (bf16[112,1024]{1,0:T(8,128)(2,1)S(1)}, bf16[112,1024]{1,0:T(8,128)(2,1)S(1)}, u32[]{:S(2)}, u32[]{:S(2)}) collective-permute-start(bf16[112,1024]{1,0:T(8,128)(2,1)S(1)} %slice.74), channel_id=1, source_target_pairs={{0,1},{1,2},{2,3},{3,4},{4,5},{5,6},{6,7},{7,0},{8,9},{9,10},{10,1... | collective-permute-start | bytes 688136 | tf_op jit(solution)/shard_map/ppermute | solution.py:23
  81.9 13.1 %collective-permute-start.11 = (bf16[192,1024]{1,0:T(8,128)(2,1)}, bf16[192,1024]{1,0:T(8,128)(2,1)S(1)}, u32[]{:S(2)}, u32[]{:S(2)}) collective-permute-start(bf16[192,1024]{1,0:T(8,128)(2,1)} %collective-permute-done.8), channel_id=1, source_target_pairs={{0,32},{1,33},{2,34},{3,35},{4,36},{5,37},{6,38},{7,39},{8,40},{9,... | collective-permute-start | bytes 1179656 | tf_op jit(solution)/shard_map/ppermute | solution.py:23
  86.0 12.0 %collective-permute-start.12 = (bf16[192,1024]{1,0:T(8,128)(2,1)}, bf16[192,1024]{1,0:T(8,128)(2,1)S(1)}, u32[]{:S(2)}, u32[]{:S(2)}) collective-permute-start(bf16[192,1024]{1,0:T(8,128)(2,1)} %collective-permute-done.8), channel_id=1, source_target_pairs={{0,96},{1,97},{2,98},{3,99},{4,100},{5,101},{6,102},{7,103},{8,104... | collective-permute-start | bytes 1179656 | tf_op jit(solution)/shard_map/ppermute | solution.py:23
  87.4 12.9 %collective-permute-start.13 = (bf16[192,1024]{1,0:T(8,128)(2,1)}, bf16[192,1024]{1,0:T(8,128)(2,1)S(1)}, u32[]{:S(2)}, u32[]{:S(2)}) collective-permute-start(bf16[192,1024]{1,0:T(8,128)(2,1)} %collective-permute-done.9), channel_id=1, source_target_pairs={{0,32},{1,33},{2,34},{3,35},{4,36},{5,37},{6,38},{7,39},{8,40},{9,... | collective-permute-start | bytes 1179656 | tf_op jit(solution)/shard_map/ppermute | solution.py:23
  97.9 13.3 %collective-permute-start.20 = (bf16[2,80,1024]{2,1,0:T(8,128)(2,1)S(1)}, bf16[2,80,1024]{2,1,0:T(8,128)(2,1)S(1)}, u32[]{:S(2)}, u32[]{:S(2)}) collective-permute-start(bf16[2,80,1024]{2,1,0:T(8,128)(2,1)S(1)} %pad_maximum_fusion.1), channel_id=1, source_target_pairs={{0,7},{1,0},{2,1},{3,2},{4,3},{5,4},{6,5},{7,6},{8,15},{9,8},{10,9... | collective-permute-start | bytes 983048 | tf_op jit(solution)/shard_map/ppermute | solution.py:23
  98.0 14.2 %collective-permute-start.22 = (bf16[112,1024]{1,0:T(8,128)(2,1)S(1)}, bf16[112,1024]{1,0:T(8,128)(2,1)S(1)}, u32[]{:S(2)}, u32[]{:S(2)}) collective-permute-start(bf16[112,1024]{1,0:T(8,128)(2,1)S(1)} %collective-permute-done.21), channel_id=1, source_target_pairs={{0,8},{1,9},{2,10},{3,11},{4,12},{5,13},{6,14},{7,15},{8,0},{9,1},... | collective-permute-start | bytes 688136 | tf_op jit(solution)/shard_map/ppermute | solution.py:23
  100.2 9.7 %collective-permute-start.27 = (bf16[112,1024]{1,0:T(8,128)(2,1)S(1)}, bf16[112,1024]{1,0:T(8,128)(2,1)S(1)}, u32[]{:S(2)}, u32[]{:S(2)}) collective-permute-start(bf16[112,1024]{1,0:T(8,128)(2,1)S(1)} %collective-permute-done.21), channel_id=1, source_target_pairs={{0,7},{1,0},{2,1},{3,2},{4,3},{5,4},{6,5},{7,6},{8,15},{9,8},{10,9... | collective-permute-start | bytes 688136 | tf_op jit(solution)/shard_map/ppermute | solution.py:23
  100.3 15.2 %collective-permute-start.24 = (bf16[112,1024]{1,0:T(8,128)(2,1)S(1)}, bf16[112,1024]{1,0:T(8,128)(2,1)S(1)}, u32[]{:S(2)}, u32[]{:S(2)}) collective-permute-start(bf16[112,1024]{1,0:T(8,128)(2,1)S(1)} %collective-permute-done.23), channel_id=1, source_target_pairs={{0,8},{1,9},{2,10},{3,11},{4,12},{5,13},{6,14},{7,15},{8,0},{9,1},... | collective-permute-start | bytes 688136 | tf_op jit(solution)/shard_map/ppermute | solution.py:23
  111.2 16.0 %collective-permute-start.28 = (bf16[112,1024]{1,0:T(8,128)(2,1)S(1)}, bf16[112,1024]{1,0:T(8,128)(2,1)S(1)}, u32[]{:S(2)}, u32[]{:S(2)}) collective-permute-start(bf16[112,1024]{1,0:T(8,128)(2,1)S(1)} %collective-permute-done.27), channel_id=1, source_target_pairs={{0,8},{1,9},{2,10},{3,11},{4,12},{5,13},{6,14},{7,15},{8,0},{9,1},... | collective-permute-start | bytes 688136 | tf_op jit(solution)/shard_map/ppermute | solution.py:23
  112.2 18.5 %collective-permute-start.30 = (bf16[112,1024]{1,0:T(8,128)(2,1)S(1)}, bf16[112,1024]{1,0:T(8,128)(2,1)S(1)}, u32[]{:S(2)}, u32[]{:S(2)}) collective-permute-start(bf16[112,1024]{1,0:T(8,128)(2,1)S(1)} %collective-permute-done.29), channel_id=1, source_target_pairs={{0,8},{1,9},{2,10},{3,11},{4,12},{5,13},{6,14},{7,15},{8,0},{9,1},... | collective-permute-start | bytes 688136 | tf_op jit(solution)/shard_map/ppermute | solution.py:23
  118.1 12.7 %collective-permute-start.35 = (bf16[112,1024]{1,0:T(8,128)(2,1)S(1)}, bf16[112,1024]{1,0:T(8,128)(2,1)S(1)}, u32[]{:S(2)}, u32[]{:S(2)}) collective-permute-start(bf16[112,1024]{1,0:T(8,128)(2,1)S(1)} %collective-permute-done.29), channel_id=1, source_target_pairs={{0,1},{1,2},{2,3},{3,4},{4,5},{5,6},{6,7},{7,0},{8,9},{9,10},{10,1... | collective-permute-start | bytes 688136 | tf_op jit(solution)/shard_map/ppermute | solution.py:23
  122.7 28.0 %collective-permute-start.34 = (bf16[112,1024]{1,0:T(8,128)(2,1)S(1)}, bf16[112,1024]{1,0:T(8,128)(2,1)S(1)}, u32[]{:S(2)}, u32[]{:S(2)}) collective-permute-start(bf16[112,1024]{1,0:T(8,128)(2,1)S(1)} %collective-permute-done.33), channel_id=1, source_target_pairs={{0,8},{1,9},{2,10},{3,11},{4,12},{5,13},{6,14},{7,15},{8,0},{9,1},... | collective-permute-start | bytes 688136 | tf_op jit(solution)/shard_map/ppermute | solution.py:23
  127.2 32.2 %collective-permute-start.15 = (bf16[8,192,1024]{2,1,0:T(8,128)(2,1)S(1)}, bf16[8,192,1024]{2,1,0:T(8,128)(2,1)S(1)}, u32[]{:S(2)}, u32[]{:S(2)}) collective-permute-start(bf16[8,192,1024]{2,1,0:T(8,128)(2,1)S(1)} %bitcast_dynamic-update-slice_fusion), channel_id=1, source_target_pairs={{0,16},{1,17},{2,18},{3,19},{4,20},{5,21},{6,22},{7,23},{8,24},{9,... | collective-permute-start | bytes 9437192 | tf_op jit(solution)/shard_map/ppermute | solution.py:23
  127.2 11.6 %collective-permute-start.31 = (bf16[2,80,1024]{2,1,0:T(8,128)(2,1)S(1)}, bf16[2,80,1024]{2,1,0:T(8,128)(2,1)S(1)}, u32[]{:S(2)}, u32[]{:S(2)}) collective-permute-start(bf16[2,80,1024]{2,1,0:T(8,128)(2,1)S(1)} %collective-permute-done.25), channel_id=1, source_target_pairs={{0,1},{1,2},{2,3},{3,4},{4,5},{5,6},{6,7},{7,0},{8,9},{9,10},{10,1... | collective-permute-start | bytes 983048 | tf_op jit(solution)/shard_map/ppermute | solution.py:23
  130.8 19.9 %collective-permute-start.36 = (bf16[112,1024]{1,0:T(8,128)(2,1)S(1)}, bf16[112,1024]{1,0:T(8,128)(2,1)S(1)}, u32[]{:S(2)}, u32[]{:S(2)}) collective-permute-start(bf16[112,1024]{1,0:T(8,128)(2,1)S(1)} %collective-permute-done.35), channel_id=1, source_target_pairs={{0,8},{1,9},{2,10},{3,11},{4,12},{5,13},{6,14},{7,15},{8,0},{9,1},... | collective-permute-start | bytes 688136 | tf_op jit(solution)/shard_map/ppermute | solution.py:23
  138.8 17.8 %collective-permute-start.39 = (bf16[112,1024]{1,0:T(8,128)(2,1)S(1)}, bf16[112,1024]{1,0:T(8,128)(2,1)S(1)}, u32[]{:S(2)}, u32[]{:S(2)}) collective-permute-start(bf16[112,1024]{1,0:T(8,128)(2,1)S(1)} %collective-permute-done.38), channel_id=1, source_target_pairs={{0,8},{1,9},{2,10},{3,11},{4,12},{5,13},{6,14},{7,15},{8,0},{9,1},... | collective-permute-start | bytes 688136 | tf_op jit(solution)/shard_map/ppermute | solution.py:23
  (22 other events, 120.3 us)

commit v2 on v0

v2 whole, which is shorter than its diff:
```python
import jax
import jax.numpy as jnp
from jax import lax
from jax.experimental import pallas as pl
from jax.experimental.pallas import tpu as pltpu
from jax.sharding import PartitionSpec as P

SIZES = dict(yh=2, x=4, c=2, yl=2, z=8)


def place_of(index):
    r, f = divmod(index, 16)
    return dict(yh=r // 8, x=r // 2 % 4, c=r % 2, yl=f // 8, z=f % 8)


def index_of(p):
    return (p["yh"] * 8 + p["x"] * 2 + p["c"]) * 16 + p["yl"] * 8 + p["z"]


def permuted(x, move):
    pairs = [(i, index_of(move(place_of(i)))) for i in range(256)]
    return lax.ppermute(x, ("rows", "feat"), pairs)


def shift(x, axis, by):
    return permuted(x, lambda p: {**p, axis: (p[axis] + by) % SIZES[axis]})


def swap(x, axis):
    return shift(x, axis, 1)


def spread(p):
    flip = p["x"] if p["z"] % 2 == 0 else -p["x"] % 4
    z = (p["z"] + flip + 4 * p["c"]) % 8
    return dict(yh=p["yl"], x=p["z"] // 2, c=p["z"] % 2, yl=p["yh"], z=z)


def from_all(x, axis):
    copies = jnp.broadcast_to(x, (16, *x.shape))
    return lax.all_to_all(copies, axis, split_axis=0, concat_axis=0, tiled=True)


def together(*arrays):
    return lax.optimization_barrier(arrays)


def prepare_kernel(at_ref, row_ref, *refs):
    same, other = refs[0:2], refs[2:4]
    weights, residuals = refs[4:6], refs[6:8]
    out_ref, grad_ref = refs[8:]
    g = pl.program_id(0)
    n = same[0].shape[1]
    parts = []
    total = jnp.zeros(grad_ref.shape, jnp.float32)
    for i in range(2):
        block = jnp.where(at_ref[2 * g + i] < 8, same[i][0], other[i][0])
        total = total + jnp.dot(
            residuals[i][0], block, preferred_element_type=jnp.float32
        )
        parts.append(block.T.astype(jnp.float32) * weights[i][0])
    out_ref[...] = jnp.concatenate(parts, axis=1).astype(jnp.bfloat16)

    @pl.when(g == 0)
    def _():
        grad_ref[...] = jnp.zeros_like(grad_ref)

    grad_ref[...] += total


def prepare(at, row, same, other, weight, residual):
    _, n, width = same.shape

    def block(i):
        return pl.BlockSpec((1, n, width), lambda g, at, row: (at[2 * g + i] % 8, 0, 0))

    def line(i):
        return pl.BlockSpec((1, 1, n), lambda g, at, row: (row[2 * g + i], 0, 0))

    return pl.pallas_call(
        prepare_kernel,
        grid_spec=pltpu.PrefetchScalarGridSpec(
            num_scalar_prefetch=2,
            grid=(8,),
            in_specs=[block(0), block(1)] * 2 + [line(0), line(1)] * 2,
            out_specs=[
                pl.BlockSpec((width, 2 * n), lambda g, at, row: (0, g)),
                pl.BlockSpec((1, width), lambda g, at, row: (0, 0)),
            ],
        ),
        out_shape=[
            jax.ShapeDtypeStruct((width, 16 * n), jnp.bfloat16),
            jax.ShapeDtypeStruct((1, width), jnp.float32),
        ],
        compiler_params=pltpu.CompilerParams(vmem_limit_bytes=20 * 2**20),
        cost_estimate=pl.CostEstimate(
            flops=32 * n * width, bytes_accessed=96 * n * width, transcendentals=0
        ),
        name="prepare",
    )(at, row, same, same, other, other, weight, weight, residual, residual)


def gram_kernel(slots, first, n, count, has_acc, *refs):
    left_ref = refs[0]
    pieces = refs[1 : 1 + count]
    rest = refs[1 + count :]
    if has_acc:
        diag_ref, acc_ref, out_ref, lbuf, rbuf, obuf, lsem, rsem, asem, osem = rest
    else:
        out_ref, lbuf, rbuf, obuf, lsem, rsem, osem = rest
    width = obuf.shape[0]
    depth = rbuf.shape[0]
    tile = min(256, width)
    tiles = width // tile
    copies = []
    for i, (slot, offset, operand, source, rows) in enumerate(slots):
        copies.append(
            pltpu.make_async_copy(
                pieces[operand].at[pl.ds(source, rows)],
                rbuf.at[pl.ds((slot - first) * n + offset, rows)],
                rsem.at[i],
            )
        )
    lefts, accs, outs = [], [], []
    for m in range(tiles):
        ms = pl.ds(m * tile, tile)
        lefts.append(
            pltpu.make_async_copy(
                left_ref.at[ms, pl.ds(first * n, depth)], lbuf.at[ms], lsem.at[m]
            )
        )
        if has_acc:
            accs.append(pltpu.make_async_copy(acc_ref.at[ms], obuf.at[ms], asem.at[m]))
        outs.append(pltpu.make_async_copy(obuf.at[ms], out_ref.at[ms], osem.at[m]))
    lefts[0].start()
    for c in copies:
        c.start()
    for m in range(tiles):
        if m:
            lefts[m].start()
        if has_acc:
            accs[m].start()
    for c in copies:
        c.wait()
    for m in range(tiles):
        ms = pl.ds(m * tile, tile)
        lefts[m].wait()
        part = jnp.dot(lbuf[ms, :], rbuf[...], preferred_element_type=jnp.float32)
        if has_acc:
            accs[m].wait()
            obuf[ms, :] = obuf[ms, :] + part
            row = lax.broadcasted_iota(jnp.int32, (tile, tile), 0)
            col = lax.broadcasted_iota(jnp.int32, (tile, tile), 1)
            extra = jnp.where(row == col, diag_ref[:, ms], 0.0)
            obuf[ms, ms] = obuf[ms, ms] + extra
        else:
            obuf[ms, :] = part
        outs[m].start()
    for c in outs:
        c.wait()


def gram(left, slots, pieces, diag=None, acc=None):
    width = left.shape[0]
    n = left.shape[1] // 16
    first = min(slot[0] for slot in slots)
    depth = n * (1 + max(slot[0] for slot in slots) - first)
    used = sorted({slot[2] for slot in slots})
    slots = [(s, o, used.index(p), r, k) for s, o, p, r, k in slots]
    pieces = [pieces[p] for p in used]
    has_acc = acc is not None
    tiles = width // min(256, width)
    anywhere = pl.BlockSpec(memory_space=pl.ANY)
    operands = [left, *pieces]
    in_specs = [anywhere] * len(operands)
    if has_acc:
        operands += [diag, acc]
        in_specs += [pl.BlockSpec(memory_space=pltpu.VMEM), anywhere]
    sems = [pltpu.SemaphoreType.DMA((k,)) for k in [tiles, len(slots)]]
    sems += [pltpu.SemaphoreType.DMA((tiles,))] * (1 + has_acc)
    return pl.pallas_call(
        lambda *refs: gram_kernel(slots, first, n, len(pieces), has_acc, *refs),
        out_shape=jax.ShapeDtypeStruct((width, width), jnp.float32),
        in_specs=in_specs,
        out_specs=anywhere,
        scratch_shapes=[
            pltpu.VMEM((width, depth), jnp.bfloat16),
            pltpu.VMEM((depth, width), jnp.bfloat16),
            pltpu.VMEM((width, width), jnp.float32),
            *sems,
        ],
        compiler_params=pltpu.CompilerParams(vmem_limit_bytes=24 * 2**20),
        cost_estimate=pl.CostEstimate(
            flops=2 * depth * width * width,
            bytes_accessed=4 * depth * width + 4 * width * width,
            transcendentals=0,
        ),
        name="gram",
    )(*operands)


def per_device(features, labels, posterior, prior_prec):
    n, width = features.shape
    a = n * 5 // 12 // 16 * 16
    b = n - a
    row_index = lax.axis_index("rows")
    feat_index = lax.axis_index("feat")
    core, x, yh = row_index % 2, row_index // 2 % 4, row_index // 8
    z, yl = feat_index % 8, feat_index // 8

    slots, pieces, at, row = [], [], [], []

    def put(operand, *parts):
        for slot, offset, source, rows in parts:
            slots.append((slot, offset, len(pieces), source, rows))
        pieces.append(operand)

    def locate(yl_, z_):
        d = (z_ - row_index) % 8
        x_ = jnp.where(core == 0, d % 4, -d % 4)
        c_ = d // 4
        at.append((c_ ^ core) * 8 + (yl_ ^ yh) * 4 + (x_ - x) % 4)
        row.append(yl_ * 8 + x_ * 2 + c_)

    for by in (0, -1, 1, -2, 2, -3, 3, 4):
        locate(yl, (z + by) % 8)
        locate(1 - yl, (z + by) % 8)
    at = jnp.stack(at).astype(jnp.int32)
    row = jnp.stack(row).astype(jnp.int32)

    mine = permuted(features, spread)
    across = swap(features, "yh")
    margins = jnp.dot(features, posterior, preferred_element_type=jnp.float32)
    margins = from_all(margins, "feat").sum(axis=0)
    mine, across, margins = together(mine, across, margins)

    up1, down1 = shift(mine, "z", 1), shift(mine, "z", -1)
    mine_y = swap(mine, "yl")
    left1, right1 = shift(features, "x", 1), shift(features, "x", -1)
    facts = from_all(jnp.stack([margins, labels.astype(jnp.float32)]), "rows")
    up1, down1, mine_y, left1, right1, facts = together(
        up1, down1, mine_y, left1, right1, facts
    )
    put(mine, (0, 0, 0, n))
    put(mine_y, (1, 0, 0, n))

    other_a = mine_y[:a]
    up2 = shift(jnp.concatenate([up1, other_a]), "z", 1)
    down2 = shift(jnp.concatenate([down1, other_a]), "z", -1)
    swapped1 = swap(jnp.concatenate([up1[a:], down1[a:]]), "yl")
    left2, right2 = shift(across, "x", 1), shift(across, "x", -1)
    up2, down2, swapped1, left2, right2 = together(
        up2, down2, swapped1, left2, right2
    )
    put(up1, (2, 0, 0, n))
    put(down1, (4, 0, 0, n))
    put(swapped1, (3, a, 0, b), (5, a, b, b))

    up3, down3 = shift(up2, "z", 1), shift(down2, "z", -1)
    swapped2 = swap(jnp.concatenate([up2[a:n], down2[a:n]]), "yl")
    twice_own, twice_far = shift(left1, "x", 1), shift(right2, "x", -1)
    up3, down3, swapped2, twice_own, twice_far = together(
        up3, down3, swapped2, twice_own, twice_far
    )
    put(up2, (6, 0, 0, n), (3, 0, n, a))
    put(down2, (8, 0, 0, n), (5, 0, n, a))
    put(swapped2, (7, a, 0, b), (9, a, b, b))

    up4 = shift(jnp.concatenate([up3[:a], up3[n:]]), "z", 1)
    down4 = shift(down3[a:], "z", -1)
    swapped3 = swap(jnp.concatenate([up3[a:n], down3[a:n]]), "yl")
    same = [features, right1, twice_own, left1, across, right2, twice_far, left2]
    same = jnp.stack(same)
    other = swap(same, "c")
    up4, down4, swapped3, other = together(up4, down4, swapped3, other)
    put(up3, (10, 0, 0, n), (7, 0, n, a))
    put(down3, (12, 0, 0, n), (9, 0, n, a))
    put(swapped3, (11, a, 0, b), (13, a, b, b))

    up5 = shift(up4[a:], "z", 1)
    swapped4 = swap(down4[:b], "yl")
    put(up4, (14, 0, 0, a), (11, 0, a, a))
    put(down4, (14, a, 0, b), (13, 0, b, a))
    put(up5, (15, 0, 0, a))
    put(swapped4, (15, a, 0, b))

    chance = jax.nn.sigmoid(facts[:, :1])
    weight = (chance * (1.0 - chance)).astype(jnp.bfloat16).astype(jnp.float32)
    residual = (facts[:, 1:] - chance).astype(jnp.bfloat16)
    left, gradient = prepare(at, row, same, other, weight, residual)
    gradient = gradient[0] - prior_prec * posterior.astype(jnp.float32)

    diag = jnp.where(row_index == feat_index, prior_prec, 0.0)[None, :]
    early = [slot for slot in slots if slot[0] < 10]
    late = [slot for slot in slots if slot[0] >= 10]
    acc = gram(left, early, pieces)
    hessian = gram(left, late, pieces, diag, acc)
    return (hessian, gradient)


def solution(mesh):
    in_specs = (P("rows", "feat"), P("rows"), P("feat"), P("feat"))
    out_specs = (P("feat", "rows"), P("feat"))
    return jax.shard_map(
        per_device, mesh=mesh, in_specs=in_specs, out_specs=out_specs, check_vma=False
    )
```

time: 243 us -> 128 us (0.53); the launches traced: 238 us -> 127 us
  waiting for transfers between devices: 168 us -> 42.9 us
  starting transfers between devices: 13.4 us -> 45 us
  Pallas kernels: 0 us -> 25.8 us
  blocking collectives: 15.3 us -> 0 us
  matrix products: 14.8 us -> 1.19 us
  between operations: 14.1 us -> 2.27 us
    all_gather x2 -> x0, waiting for transfers between devices: 167 us -> none  [the longest x1 111 us: side_by_side(): lax.all_gather(both, axis, axis=dim, tiled=True)]
    ppermute x0 -> x23, starting transfers between devices: none -> 31.6 us  [permuted(): return lax.ppermute(x, ('rows', 'feat'), pairs)]
    ppermute x0 -> x23, waiting for transfers between devices: none -> 29.9 us  [permuted(): return lax.ppermute(x, ('rows', 'feat'), pairs)]
    pallas_call x0 -> x3, Pallas kernels: none -> 25.8 us  [the longest x2 16.9 us: gram(): pl.pallas_call(lambda *refs: gram_kernel(slots, first, n, len(pieces), ha...]
    all_to_all x1 -> x0, blocking collectives: 15.3 us -> none  [sent_to_all(): return lax.all_to_all(copies, axis, split_axis=0, concat_axis=0, tiled=True)]
    dot_general x3 -> x1, matrix products: 14.8 us -> 1.19 us  [per_device(): margins = jnp.dot(features, posterior, preferred_element_type=jnp.float32)]
    all_to_all x2, waiting for transfers between devices: 0.01 us -> 13 us  [from_all(): return lax.all_to_all(copies, axis, split_axis=0, concat_axis=0, tiled=True)]
    all_to_all x1 -> x0, local copies, waits for them, and re-layouts: 6.42 us -> none  [per_device(): lax.all_to_all(full_width, 'rows', split_axis=1, concat_axis=0, tiled=True)]
  transfers between devices with their start and end apart: 4 -> 25, of which waited for: 2 -> 10; matrix products, arithmetic and copies ran while one was open for 6% -> 7% of each run, Pallas kernels for 0% -> 14%
where the time goes in v2:
time: 128 us; the launch traced here: 127 us
  starting transfers between devices  45 us (35%)
  waiting for transfers between devices  42.9 us (34%)
  Pallas kernels  25.8 us (20%)
  local copies, waits for them, and re-layouts  8.4 us (7%)
  between operations  2.27 us (2%)
  other arithmetic  1.61 us (1%)
    ppermute x23, starting transfers between devices, permuted(): return lax.ppermute(x, ('rows', 'feat'), pairs)  31.6 us
    ppermute x23, waiting for transfers between devices, permuted(): return lax.ppermute(x, ('rows', 'feat'), pairs)  29.9 us
    pallas_call x2, Pallas kernels, gram(): pl.pallas_call(lambda *refs: gram_kernel(slots, first, n, len(pieces), ha...  16.9 us
    all_to_all x2, starting transfers between devices, from_all(): return lax.all_to_all(copies, axis, split_axis=0, concat_axis=0, tiled=True)  13.4 us
    all_to_all x2, waiting for transfers between devices, from_all(): return lax.all_to_all(copies, axis, split_axis=0, concat_axis=0, tiled=True)  13 us
    pallas_call x1, Pallas kernels, prepare(): pl.pallas_call(prepare_kernel, grid_spec=pltpu.PrefetchScalarGridSpec(num...  8.84 us
    unnamed x64, local copies, waits for them, and re-layouts  3.81 us
  transfers between devices with their start and end apart: 25, of which 10 were waited for; matrix products, arithmetic and copies ran while one was open for 7% of the time, Pallas kernels for 14%

profile of v2, /device:TPU:64, one launch (start us, length us, event | category | flops | bytes accessed | tf_op | source)
XLA Modules:
  0.0 127.1 jit_solution(10821577455239812159)
XLA Ops:
  0.6 3.3 %collective-permute-start.1 = (bf16[192,1024]{1,0:T(8,128)(2,1)}, bf16[192,1024]{1,0:T(8,128)(2,1)S(1)}, u32[]{:S(2)}, u32[]{:S(2)}) collective-permute-start(bf16[192,1024]{1,0:T(8,128)(2,1)} %param.4), channel_id=1, source_target_pairs={{0,128},{1,129},{2,130},{3,131},{4,132},{5,133},{6,134},{7,135},{8... | collective-permute-start | bytes 1179656 | tf_op jit(solution)/shard_map/ppermute | solution.py:22
  3.9 3.4 %collective-permute-start = (bf16[192,1024]{1,0:T(8,128)(2,1)}, bf16[192,1024]{1,0:T(8,128)(2,1)S(1)}, u32[]{:S(2)}, u32[]{:S(2)}) collective-permute-start(bf16[192,1024]{1,0:T(8,128)(2,1)} %param.4), channel_id=1, source_target_pairs={{0,0},{1,17},{2,34},{3,51},{4,68},{5,85},{6,102},{7,119},{8,128},{... | collective-permute-start | bytes 1179656 | tf_op jit(solution)/shard_map/ppermute | solution.py:22
  9.8 9.7 %all-to-all-start = ((f32[16,1,192]{2,1,0:T(1,128)}), f32[16,1,192]{2,1,0:T(1,128)S(1)}, u32[]{:S(2)}, u32[]{:S(2)}) async-start(f32[16,1,192]{2,1,0:T(1,128)} %broadcast_in_dim.13), calls=%async_computation | async-start | bytes 32768 | tf_op jit(solution)/shard_map/all_to_all | solution.py:41
  19.5 1.9 %collective-permute-start.6 = (bf16[192,1024]{1,0:T(8,128)(2,1)}, bf16[192,1024]{1,0:T(8,128)(2,1)S(1)}, u32[]{:S(2)}, u32[]{:S(2)}) collective-permute-start(bf16[192,1024]{1,0:T(8,128)(2,1)} %param.4), channel_id=1, source_target_pairs={{0,96},{1,97},{2,98},{3,99},{4,100},{5,101},{6,102},{7,103},{8,104... | collective-permute-start | bytes 1179656 | tf_op jit(solution)/shard_map/ppermute | solution.py:22
  21.5 5.4 %all-to-all-done = f32[16,1,192]{2,1,0:T(1,128)S(1)} async-done(((f32[16,1,192]{2,1,0:T(1,128)}), f32[16,1,192]{2,1,0:T(1,128)S(1)}, u32[]{:S(2)}, u32[]{:S(2)}) %all-to-all-start) | async-done | bytes 12320 | tf_op jit(solution)/shard_map/all_to_all | solution.py:41
  29.2 2.0 %collective-permute-start.2 = (bf16[192,1024]{1,0:T(8,128)(2,1)S(1)}, bf16[192,1024]{1,0:T(8,128)(2,1)S(1)}, u32[]{:S(2)}, u32[]{:S(2)}) collective-permute-start(bf16[192,1024]{1,0:T(8,128)(2,1)S(1)} %collective-permute-done.refs_1_), channel_id=1, source_target_pairs={{0,1},{1,2},{2,3},{3,4},{4,5},{5,6},{6,7},{7,0},{8,9},{9,10},{10,1... | collective-permute-start | bytes 1179656 | tf_op jit(solution)/shard_map/ppermute | solution.py:22
  32.5 3.7 %all-to-all-start.1 = ((f32[16,2,192]{2,1,0:T(2,128)}), f32[16,2,192]{2,1,0:T(2,128)S(1)}, u32[]{:S(2)}, u32[]{:S(2)}) async-start(f32[16,2,192]{2,1,0:T(2,128)} %broadcast_in_dim.14), calls=%async_computation.1 | async-start | bytes 65536 | tf_op jit(solution)/shard_map/all_to_all | solution.py:41
  36.3 7.6 %all-to-all-done.1 = f32[16,2,192]{2,1,0:T(2,128)S(1)} async-done(((f32[16,2,192]{2,1,0:T(2,128)}), f32[16,2,192]{2,1,0:T(2,128)S(1)}, u32[]{:S(2)}, u32[]{:S(2)}) %all-to-all-start.1) | async-done | bytes 24608 | tf_op jit(solution)/shard_map/all_to_all | solution.py:41
  45.6 1.6 %collective-permute-start.7 = (bf16[272,1024]{1,0:T(8,128)(2,1)S(1)}, bf16[272,1024]{1,0:T(8,128)(2,1)S(1)}, u32[]{:S(2)}, u32[]{:S(2)}) collective-permute-start(bf16[272,1024]{1,0:T(8,128)(2,1)S(1)} %get-tuple-element.57), channel_id=1, source_target_pairs={{0,1},{1,2},{2,3},{3,4},{4,5},{5,6},{6,7},{7,0},{8,9},{9,10},{10,1... | collective-permute-start | bytes 1671176 | tf_op jit(solution)/shard_map/ppermute | solution.py:22
  49.9 8.5 %collective-permute-done.11 = bf16[192,1024]{1,0:T(8,128)(2,1)S(1)} collective-permute-done((bf16[192,1024]{1,0:T(8,128)(2,1)S(1)}, bf16[192,1024]{1,0:T(8,128)(2,1)S(1)}, u32[]{:S(2)}, u32[]{:S(2)}) %collective-permute-start.11) | collective-permute-done | bytes 393248 | tf_op jit(solution)/shard_map/ppermute | solution.py:22
  60.6 2.9 %collective-permute-start.12 = (bf16[272,1024]{1,0:T(8,128)(2,1)S(1)}, bf16[272,1024]{1,0:T(8,128)(2,1)S(1)}, u32[]{:S(2)}, u32[]{:S(2)}) collective-permute-start(bf16[272,1024]{1,0:T(8,128)(2,1)S(1)} %collective-permute-done.7.refs_6_), channel_id=1, source_target_pairs={{0,1},{1,2},{2,3},{3,4},{4,5},{5,6},{6,7},{7,0},{8,9},{9,10},{10,1... | collective-permute-start | bytes 1671176 | tf_op jit(solution)/shard_map/ppermute | solution.py:22
  64.9 1.7 %collective-permute-start.14 = (bf16[224,1024]{1,0:T(8,128)(2,1)S(1)}, bf16[224,1024]{1,0:T(8,128)(2,1)S(1)}, u32[]{:S(2)}, u32[]{:S(2)}) collective-permute-start(bf16[224,1024]{1,0:T(8,128)(2,1)S(1)} %pad_maximum_fusion.3), channel_id=1, source_target_pairs={{0,8},{1,9},{2,10},{3,11},{4,12},{5,13},{6,14},{7,15},{8,0},{9,1},... | collective-permute-start | bytes 1376264 | tf_op jit(solution)/shard_map/ppermute | solution.py:22
  67.7 1.6 %collective-permute-done.15 = bf16[192,1024]{1,0:T(8,128)(2,1)S(1)} collective-permute-done((bf16[192,1024]{1,0:T(8,128)(2,1)S(1)}, bf16[192,1024]{1,0:T(8,128)(2,1)S(1)}, u32[]{:S(2)}, u32[]{:S(2)}) %collective-permute-start.15) | collective-permute-done | bytes 393248 | tf_op jit(solution)/shard_map/ppermute | solution.py:22
  69.3 3.9 %collective-permute-done.16 = bf16[192,1024]{1,0:T(8,128)(2,1)S(1)} collective-permute-done((bf16[192,1024]{1,0:T(8,128)(2,1)S(1)}, bf16[192,1024]{1,0:T(8,128)(2,1)S(1)}, u32[]{:S(2)}, u32[]{:S(2)}) %collective-permute-start.16) | collective-permute-done | bytes 393248 | tf_op jit(solution)/shard_map/ppermute | solution.py:22
  73.2 2.7 %collective-permute-done.14.refs_8_ = bf16[224,1024]{1,0:T(8,128)(2,1)S(1)} collective-permute-done((bf16[224,1024]{1,0:T(8,128)(2,1)S(1)}, bf16[224,1024]{1,0:T(8,128)(2,1)S(1)}, u32[]{:S(2)}, u32[]{:S(2)}) %collective-permute-start.14) | collective-permute-done | bytes 458784 | tf_op jit(solution)/shard_map/ppermute | solution.py:22
  75.9 1.6 %collective-permute-done.13.refs_10_.refs_2_ = bf16[272,1024]{1,0:T(8,128)(2,1)S(1)} collective-permute-done((bf16[272,1024]{1,0:T(8,128)(2,1)S(1)}, bf16[272,1024]{1,0:T(8,128)(2,1)S(1)}, u32[]{:S(2)}, u32[]{:S(2)}) %collective-permute-start.13) | collective-permute-done | bytes 557088 | tf_op jit(solution)/shard_map/ppermute | solution.py:22
  83.2 3.0 %collective-permute-start.17 = (bf16[160,1024]{1,0:T(8,128)(2,1)S(1)}, bf16[160,1024]{1,0:T(8,128)(2,1)S(1)}, u32[]{:S(2)}, u32[]{:S(2)}) collective-permute-start(bf16[160,1024]{1,0:T(8,128)(2,1)S(1)} %pad_maximum_fusion.5), channel_id=1, source_target_pairs={{0,1},{1,2},{2,3},{3,4},{4,5},{5,6},{6,7},{7,0},{8,9},{9,10},{10,1... | collective-permute-start | bytes 983048 | tf_op jit(solution)/shard_map/ppermute | solution.py:22
  86.4 6.4 %collective-permute-done.17.refs_4_ = bf16[160,1024]{1,0:T(8,128)(2,1)S(1)} collective-permute-done((bf16[160,1024]{1,0:T(8,128)(2,1)S(1)}, bf16[160,1024]{1,0:T(8,128)(2,1)S(1)}, u32[]{:S(2)}, u32[]{:S(2)}) %collective-permute-start.17) | collective-permute-done | bytes 327712 | tf_op jit(solution)/shard_map/ppermute | solution.py:22
  92.7 3.6 %collective-permute-done.18.refs_5_ = bf16[192,1024]{1,0:T(8,128)(2,1)S(1)} collective-permute-done((bf16[192,1024]{1,0:T(8,128)(2,1)S(1)}, bf16[192,1024]{1,0:T(8,128)(2,1)S(1)}, u32[]{:S(2)}, u32[]{:S(2)}) %collective-permute-start.18) | collective-permute-done | bytes 393248 | tf_op jit(solution)/shard_map/ppermute | solution.py:22
  96.4 2.2 %collective-permute-start.21 = (bf16[80,1024]{1,0:T(8,128)(2,1)S(1)}, bf16[80,1024]{1,0:T(8,128)(2,1)S(1)}, u32[]{:S(2)}, u32[]{:S(2)}) collective-permute-start(bf16[80,1024]{1,0:T(8,128)(2,1)S(1)} %slice.54), channel_id=1, source_target_pairs={{0,1},{1,2},{2,3},{3,4},{4,5},{5,6},{6,7},{7,0},{8,9},{9,10},{10,1... | collective-permute-start | bytes 491528 | tf_op jit(solution)/shard_map/ppermute | solution.py:22
  98.6 1.8 %collective-permute-start.22 = (bf16[112,1024]{1,0:T(8,128)(2,1)S(1)}, bf16[112,1024]{1,0:T(8,128)(2,1)S(1)}, u32[]{:S(2)}, u32[]{:S(2)}) collective-permute-start(bf16[112,1024]{1,0:T(8,128)(2,1)S(1)} %slice.55), channel_id=1, source_target_pairs={{0,8},{1,9},{2,10},{3,11},{4,12},{5,13},{6,14},{7,15},{8,0},{9,1},... | collective-permute-start | bytes 688136 | tf_op jit(solution)/shard_map/ppermute | solution.py:22
  100.4 8.8 %prepare.1 = (bf16[1024,3072]{1,0:T(8,128)(2,1)S(1)}, f32[1,1024]{1,0:T(1,128)S(1)}) custom-call(s32[16]{0:T(128)S(1)} %stack.154.at_ref, s32[16]{0:T(128)S(1)} %stack.171.row_ref, bf16[8,192,1024]{2,1,0:T(8,128)(2,1)S(1)} %bitcast_dynamic-update-slice_fusion.refs_0_.refs_1_, bf16[8,192,1024]{2,1,0:T(8,128)(2,1)S(1)} %bitcast_dynamic-update-slice_fusion.refs_0_.refs_1_, ...), custom_call_target="tpu_custom_call" | custom-call | flops 6291456 | bytes 18874368 | tf_op jit(solution)/shard_map/prepare/pallas_call | solution.py:80
  109.4 9.0 %gram.2.refs_9_ = f32[1024,1024]{1,0:T(8,128)S(1)} custom-call(bf16[1024,3072]{1,0:T(8,128)(2,1)S(1)} %get-tuple-element.45.refs_0_, bf16[192,1024]{1,0:T(8,128)(2,1)S(1)} %copy-done.17, bf16[192,1024]{1,0:T(8,128)(2,1)S(1)} %copy-done.11, bf16[192,1024]{1,0:T(8,128)(2,1)S(1)} %copy-done.5, bf16[192,1024]{1,0:T(8,128)(2,1)S(1)} %collective-permute-done.3.refs_4_, ...), custom_call_target="tpu_custom_call" | custom-call | flops 4026531840 | bytes 12058624 | tf_op jit(solution)/shard_map/gram/pallas_call | solution.py:181
  119.0 7.9 %gram.3 = f32[1024,1024]{1,0:T(8,128)} custom-call(bf16[1024,3072]{1,0:T(8,128)(2,1)S(1)} %get-tuple-element.45.refs_0_, bf16[272,1024]{1,0:T(8,128)(2,1)S(1)} %copy-done.3, bf16[272,1024]{1,0:T(8,128)(2,1)S(1)} %copy-done.1, bf16[224,1024]{1,0:T(8,128)(2,1)S(1)} %collective-permute-done.19.refs_3_, bf16[160,1024]{1,0:T(8,128)(2,1)S(1)} %collective-permute-done.17.refs_4_, ...), custom_call_target="tpu_custom_call" | custom-call | flops 2415919104 | bytes 8912896 | tf_op jit(solution)/shard_map/gram/pallas_call | solution.py:181
  (121 shorter events, 20.5 us)
Async XLA Ops:
  0.6 26.3 %collective-permute-start.1 = (bf16[192,1024]{1,0:T(8,128)(2,1)}, bf16[192,1024]{1,0:T(8,128)(2,1)S(1)}, u32[]{:S(2)}, u32[]{:S(2)}) collective-permute-start(bf16[192,1024]{1,0:T(8,128)(2,1)} %param.4), channel_id=1, source_target_pairs={{0,128},{1,129},{2,130},{3,131},{4,132},{5,133},{6,134},{7,135},{8... | collective-permute-start | bytes 1179656 | tf_op jit(solution)/shard_map/ppermute | solution.py:22
  3.9 23.1 %collective-permute-start = (bf16[192,1024]{1,0:T(8,128)(2,1)}, bf16[192,1024]{1,0:T(8,128)(2,1)S(1)}, u32[]{:S(2)}, u32[]{:S(2)}) collective-permute-start(bf16[192,1024]{1,0:T(8,128)(2,1)} %param.4), channel_id=1, source_target_pairs={{0,0},{1,17},{2,34},{3,51},{4,68},{5,85},{6,102},{7,119},{8,128},{... | collective-permute-start | bytes 1179656 | tf_op jit(solution)/shard_map/ppermute | solution.py:22
  9.8 17.1 %all-to-all-start = ((f32[16,1,192]{2,1,0:T(1,128)}), f32[16,1,192]{2,1,0:T(1,128)S(1)}, u32[]{:S(2)}, u32[]{:S(2)}) async-start(f32[16,1,192]{2,1,0:T(1,128)} %broadcast_in_dim.13), calls=%async_computation | async-start | bytes 32768 | tf_op jit(solution)/shard_map/all_to_all | solution.py:41
  19.5 16.7 %collective-permute-start.6 = (bf16[192,1024]{1,0:T(8,128)(2,1)}, bf16[192,1024]{1,0:T(8,128)(2,1)S(1)}, u32[]{:S(2)}, u32[]{:S(2)}) collective-permute-start(bf16[192,1024]{1,0:T(8,128)(2,1)} %param.4), channel_id=1, source_target_pairs={{0,96},{1,97},{2,98},{3,99},{4,100},{5,101},{6,102},{7,103},{8,104... | collective-permute-start | bytes 1179656 | tf_op jit(solution)/shard_map/ppermute | solution.py:22
  21.4 14.8 %collective-permute-start.5 = (bf16[192,1024]{1,0:T(8,128)(2,1)}, bf16[192,1024]{1,0:T(8,128)(2,1)S(1)}, u32[]{:S(2)}, u32[]{:S(2)}) collective-permute-start(bf16[192,1024]{1,0:T(8,128)(2,1)} %param.4), channel_id=1, source_target_pairs={{0,32},{1,33},{2,34},{3,35},{4,36},{5,37},{6,38},{7,39},{8,40},{9,... | collective-permute-start | bytes 1179656 | tf_op jit(solution)/shard_map/ppermute | solution.py:22
  27.7 16.1 %collective-permute-start.4 = (bf16[192,1024]{1,0:T(8,128)(2,1)S(1)}, bf16[192,1024]{1,0:T(8,128)(2,1)S(1)}, u32[]{:S(2)}, u32[]{:S(2)}) collective-permute-start(bf16[192,1024]{1,0:T(8,128)(2,1)S(1)} %collective-permute-done.refs_1_), channel_id=1, source_target_pairs={{0,8},{1,9},{2,10},{3,11},{4,12},{5,13},{6,14},{7,15},{8,0},{9,1},... | collective-permute-start | bytes 1179656 | tf_op jit(solution)/shard_map/ppermute | solution.py:22
  29.2 14.7 %collective-permute-start.3 = (bf16[192,1024]{1,0:T(8,128)(2,1)S(1)}, bf16[192,1024]{1,0:T(8,128)(2,1)S(1)}, u32[]{:S(2)}, u32[]{:S(2)}) collective-permute-start(bf16[192,1024]{1,0:T(8,128)(2,1)S(1)} %collective-permute-done.refs_1_), channel_id=1, source_target_pairs={{0,7},{1,0},{2,1},{3,2},{4,3},{5,4},{6,5},{7,6},{8,15},{9,8},{10,9... | collective-permute-start | bytes 1179656 | tf_op jit(solution)/shard_map/ppermute | solution.py:22
  29.2 14.7 %collective-permute-start.2 = (bf16[192,1024]{1,0:T(8,128)(2,1)S(1)}, bf16[192,1024]{1,0:T(8,128)(2,1)S(1)}, u32[]{:S(2)}, u32[]{:S(2)}) collective-permute-start(bf16[192,1024]{1,0:T(8,128)(2,1)S(1)} %collective-permute-done.refs_1_), channel_id=1, source_target_pairs={{0,1},{1,2},{2,3},{3,4},{4,5},{5,6},{6,7},{7,0},{8,9},{9,10},{10,1... | collective-permute-start | bytes 1179656 | tf_op jit(solution)/shard_map/ppermute | solution.py:22
  32.5 11.3 %all-to-all-start.1 = ((f32[16,2,192]{2,1,0:T(2,128)}), f32[16,2,192]{2,1,0:T(2,128)S(1)}, u32[]{:S(2)}, u32[]{:S(2)}) async-start(f32[16,2,192]{2,1,0:T(2,128)} %broadcast_in_dim.14), calls=%async_computation.1 | async-start | bytes 65536 | tf_op jit(solution)/shard_map/all_to_all | solution.py:41
  44.6 16.0 %collective-permute-start.8 = (bf16[272,1024]{1,0:T(8,128)(2,1)S(1)}, bf16[272,1024]{1,0:T(8,128)(2,1)S(1)}, u32[]{:S(2)}, u32[]{:S(2)}) collective-permute-start(bf16[272,1024]{1,0:T(8,128)(2,1)S(1)} %get-tuple-element.56), channel_id=1, source_target_pairs={{0,7},{1,0},{2,1},{3,2},{4,3},{5,4},{6,5},{7,6},{8,15},{9,8},{10,9... | collective-permute-start | bytes 1671176 | tf_op jit(solution)/shard_map/ppermute | solution.py:22
  45.6 15.0 %collective-permute-start.7 = (bf16[272,1024]{1,0:T(8,128)(2,1)S(1)}, bf16[272,1024]{1,0:T(8,128)(2,1)S(1)}, u32[]{:S(2)}, u32[]{:S(2)}) collective-permute-start(bf16[272,1024]{1,0:T(8,128)(2,1)S(1)} %get-tuple-element.57), channel_id=1, source_target_pairs={{0,1},{1,2},{2,3},{3,4},{4,5},{5,6},{6,7},{7,0},{8,9},{9,10},{10,1... | collective-permute-start | bytes 1671176 | tf_op jit(solution)/shard_map/ppermute | solution.py:22
  47.2 13.4 %collective-permute-start.9 = (bf16[224,1024]{1,0:T(8,128)(2,1)S(1)}, bf16[224,1024]{1,0:T(8,128)(2,1)S(1)}, u32[]{:S(2)}, u32[]{:S(2)}) collective-permute-start(bf16[224,1024]{1,0:T(8,128)(2,1)S(1)} %pad_maximum_fusion.2), channel_id=1, source_target_pairs={{0,8},{1,9},{2,10},{3,11},{4,12},{5,13},{6,14},{7,15},{8,0},{9,1},... | collective-permute-start | bytes 1376264 | tf_op jit(solution)/shard_map/ppermute | solution.py:22
  47.8 10.6 %collective-permute-start.11 = (bf16[192,1024]{1,0:T(8,128)(2,1)S(1)}, bf16[192,1024]{1,0:T(8,128)(2,1)S(1)}, u32[]{:S(2)}, u32[]{:S(2)}) collective-permute-start(bf16[192,1024]{1,0:T(8,128)(2,1)S(1)} %copy-done.19), channel_id=1, source_target_pairs={{0,96},{1,97},{2,98},{3,99},{4,100},{5,101},{6,102},{7,103},{8,104... | collective-permute-start | bytes 1179656 | tf_op jit(solution)/shard_map/ppermute | solution.py:22
  49.0 11.5 %collective-permute-start.10 = (bf16[192,1024]{1,0:T(8,128)(2,1)S(1)}, bf16[192,1024]{1,0:T(8,128)(2,1)S(1)}, u32[]{:S(2)}, u32[]{:S(2)}) collective-permute-start(bf16[192,1024]{1,0:T(8,128)(2,1)S(1)} %copy-done.19), channel_id=1, source_target_pairs={{0,32},{1,33},{2,34},{3,35},{4,36},{5,37},{6,38},{7,39},{8,40},{9,... | collective-permute-start | bytes 1179656 | tf_op jit(solution)/shard_map/ppermute | solution.py:22
  58.4 10.9 %collective-permute-start.15 = (bf16[192,1024]{1,0:T(8,128)(2,1)S(1)}, bf16[192,1024]{1,0:T(8,128)(2,1)S(1)}, u32[]{:S(2)}, u32[]{:S(2)}) collective-permute-start(bf16[192,1024]{1,0:T(8,128)(2,1)S(1)} %copy-done.21), channel_id=1, source_target_pairs={{0,32},{1,33},{2,34},{3,35},{4,36},{5,37},{6,38},{7,39},{8,40},{9,... | collective-permute-start | bytes 1179656 | tf_op jit(solution)/shard_map/ppermute | solution.py:22
  60.6 15.3 %collective-permute-start.12 = (bf16[272,1024]{1,0:T(8,128)(2,1)S(1)}, bf16[272,1024]{1,0:T(8,128)(2,1)S(1)}, u32[]{:S(2)}, u32[]{:S(2)}) collective-permute-start(bf16[272,1024]{1,0:T(8,128)(2,1)S(1)} %collective-permute-done.7.refs_6_), channel_id=1, source_target_pairs={{0,1},{1,2},{2,3},{3,4},{4,5},{5,6},{6,7},{7,0},{8,9},{9,10},{10,1... | collective-permute-start | bytes 1671176 | tf_op jit(solution)/shard_map/ppermute | solution.py:22
  63.6 14.0 %collective-permute-start.13 = (bf16[272,1024]{1,0:T(8,128)(2,1)S(1)}, bf16[272,1024]{1,0:T(8,128)(2,1)S(1)}, u32[]{:S(2)}, u32[]{:S(2)}) collective-permute-start(bf16[272,1024]{1,0:T(8,128)(2,1)S(1)} %collective-permute-done.8.refs_7_), channel_id=1, source_target_pairs={{0,7},{1,0},{2,1},{3,2},{4,3},{5,4},{6,5},{7,6},{8,15},{9,8},{10,9... | collective-permute-start | bytes 1671176 | tf_op jit(solution)/shard_map/ppermute | solution.py:22
  63.6 9.6 %collective-permute-start.16 = (bf16[192,1024]{1,0:T(8,128)(2,1)S(1)}, bf16[192,1024]{1,0:T(8,128)(2,1)S(1)}, u32[]{:S(2)}, u32[]{:S(2)}) collective-permute-start(bf16[192,1024]{1,0:T(8,128)(2,1)S(1)} %collective-permute-done.11), channel_id=1, source_target_pairs={{0,96},{1,97},{2,98},{3,99},{4,100},{5,101},{6,102},{7,103},{8,104... | collective-permute-start | bytes 1179656 | tf_op jit(solution)/shard_map/ppermute | solution.py:22
  64.9 11.0 %collective-permute-start.14 = (bf16[224,1024]{1,0:T(8,128)(2,1)S(1)}, bf16[224,1024]{1,0:T(8,128)(2,1)S(1)}, u32[]{:S(2)}, u32[]{:S(2)}) collective-permute-start(bf16[224,1024]{1,0:T(8,128)(2,1)S(1)} %pad_maximum_fusion.3), channel_id=1, source_target_pairs={{0,8},{1,9},{2,10},{3,11},{4,12},{5,13},{6,14},{7,15},{8,0},{9,1},... | collective-permute-start | bytes 1376264 | tf_op jit(solution)/shard_map/ppermute | solution.py:22
  78.4 18.0 %collective-permute-start.20 = (bf16[8,192,1024]{2,1,0:T(8,128)(2,1)S(1)}, bf16[8,192,1024]{2,1,0:T(8,128)(2,1)}, u32[]{:S(2)}, u32[]{:S(2)}) collective-permute-start(bf16[8,192,1024]{2,1,0:T(8,128)(2,1)S(1)} %bitcast_dynamic-update-slice_fusion.refs_0_.refs_1_), channel_id=1, source_target_pairs={{0,16},{1,17},{2,18},{3,19},{4,20},{5,21},{6,22},{7,23},{8,24},{9,... | collective-permute-start | bytes 9437192 | tf_op jit(solution)/shard_map/ppermute | solution.py:22
  81.5 14.8 %collective-permute-start.19 = (bf16[224,1024]{1,0:T(8,128)(2,1)S(1)}, bf16[224,1024]{1,0:T(8,128)(2,1)S(1)}, u32[]{:S(2)}, u32[]{:S(2)}) collective-permute-start(bf16[224,1024]{1,0:T(8,128)(2,1)S(1)} %pad_maximum_fusion.4), channel_id=1, source_target_pairs={{0,8},{1,9},{2,10},{3,11},{4,12},{5,13},{6,14},{7,15},{8,0},{9,1},... | collective-permute-start | bytes 1376264 | tf_op jit(solution)/shard_map/ppermute | solution.py:22
  86.3 10.1 %collective-permute-start.18 = (bf16[192,1024]{1,0:T(8,128)(2,1)S(1)}, bf16[192,1024]{1,0:T(8,128)(2,1)S(1)}, u32[]{:S(2)}, u32[]{:S(2)}) collective-permute-start(bf16[192,1024]{1,0:T(8,128)(2,1)S(1)} %slice.49), channel_id=1, source_target_pairs={{0,7},{1,0},{2,1},{3,2},{4,3},{5,4},{6,5},{7,6},{8,15},{9,8},{10,9... | collective-permute-start | bytes 1179656 | tf_op jit(solution)/shard_map/ppermute | solution.py:22
  96.4 22.7 %collective-permute-start.21 = (bf16[80,1024]{1,0:T(8,128)(2,1)S(1)}, bf16[80,1024]{1,0:T(8,128)(2,1)S(1)}, u32[]{:S(2)}, u32[]{:S(2)}) collective-permute-start(bf16[80,1024]{1,0:T(8,128)(2,1)S(1)} %slice.54), channel_id=1, source_target_pairs={{0,1},{1,2},{2,3},{3,4},{4,5},{5,6},{6,7},{7,0},{8,9},{9,10},{10,1... | collective-permute-start | bytes 491528 | tf_op jit(solution)/shard_map/ppermute | solution.py:22
  98.6 20.4 %collective-permute-start.22 = (bf16[112,1024]{1,0:T(8,128)(2,1)S(1)}, bf16[112,1024]{1,0:T(8,128)(2,1)S(1)}, u32[]{:S(2)}, u32[]{:S(2)}) collective-permute-start(bf16[112,1024]{1,0:T(8,128)(2,1)S(1)} %slice.55), channel_id=1, source_target_pairs={{0,8},{1,9},{2,10},{3,11},{4,12},{5,13},{6,14},{7,15},{8,0},{9,1},... | collective-permute-start | bytes 688136 | tf_op jit(solution)/shard_map/ppermute | solution.py:22
  (29 other events, 273.7 us)

commit v3 on v2

v3 whole, which is shorter than its diff:
```python
import jax
import jax.numpy as jnp
from jax import lax
from jax.experimental import pallas as pl
from jax.experimental.pallas import tpu as pltpu
from jax.sharding import PartitionSpec as P

SIZES = dict(yh=2, x=4, c=2, yl=2, z=8)


def place_of(index):
    r, f = divmod(index, 16)
    return dict(yh=r // 8, x=r // 2 % 4, c=r % 2, yl=f // 8, z=f % 8)


def index_of(p):
    return (p["yh"] * 8 + p["x"] * 2 + p["c"]) * 16 + p["yl"] * 8 + p["z"]


def permuted(x, move):
    pairs = [(i, index_of(move(place_of(i)))) for i in range(256)]
    return lax.ppermute(x, ("rows", "feat"), pairs)


def shift(x, axis, by):
    return permuted(x, lambda p: {**p, axis: (p[axis] + by) % SIZES[axis]})


def swap(x, axis):
    return shift(x, axis, 1)


def spread(p):
    flip = p["x"] if p["z"] % 2 == 0 else -p["x"] % 4
    z = (p["z"] + flip + 4 * p["c"]) % 8
    return dict(yh=p["yl"], x=p["z"] // 2, c=p["z"] % 2, yl=p["yh"], z=z)


def from_all(x, axis):
    copies = jnp.broadcast_to(x, (16, *x.shape))
    return lax.all_to_all(copies, axis, split_axis=0, concat_axis=0, tiled=True)


def together(*arrays):
    return lax.optimization_barrier(arrays)


def prepare_kernel(slot_ref, row_ref, *refs):
    same, other = refs[:2]
    weight_ref, residual_ref, prior_ref, point_ref = refs[2:6]
    out_ref, grad_ref, lbuf, obuf, lsem, osem = refs[6:]
    _, n, width = same.shape
    copies = []
    for i in range(16):
        start = pl.multiple_of(slot_ref[i] * n, 16)
        copies.append(
            pltpu.make_async_copy(
                (same if i < 8 else other).at[i % 8],
                lbuf.at[pl.ds(start, n)],
                lsem.at[i],
            )
        )
    for c in copies:
        c.start()
    for c in copies:
        c.wait()
    total = jnp.zeros(grad_ref.shape, jnp.float32)
    outs = []
    for g in range(8):
        block = lbuf[2 * g * n : 2 * (g + 1) * n, :]
        lines = [residual_ref[row_ref[2 * g + i]] for i in range(2)]
        total = total + jnp.dot(
            jnp.concatenate(lines, axis=1), block, preferred_element_type=jnp.float32
        )
        scales = [weight_ref[row_ref[2 * g + i]] for i in range(2)]
        turned = block.T.astype(jnp.float32) * jnp.concatenate(scales, axis=1)
        columns = pl.ds(2 * g * n, 2 * n)
        obuf[:, columns] = turned.astype(jnp.bfloat16)
        outs.append(
            pltpu.make_async_copy(
                obuf.at[:, columns], out_ref.at[:, columns], osem.at[g]
            )
        )
        outs[-1].start()
    grad_ref[...] = total - prior_ref[...] * point_ref[...].astype(jnp.float32)
    for c in outs:
        c.wait()


def prepare(slot, row, same, other, weight, residual, prior, point):
    _, n, width = same.shape
    smem = pl.BlockSpec(memory_space=pltpu.SMEM)
    vmem = pl.BlockSpec(memory_space=pltpu.VMEM)
    anywhere = pl.BlockSpec(memory_space=pl.ANY)
    return pl.pallas_call(
        prepare_kernel,
        in_specs=[smem, smem] + [anywhere] * 2 + [vmem] * 4,
        out_specs=[pl.BlockSpec(memory_space=pltpu.HBM), vmem],
        out_shape=[
            jax.ShapeDtypeStruct((width, 16 * n), jnp.bfloat16),
            jax.ShapeDtypeStruct((1, width), jnp.float32),
        ],
        scratch_shapes=[
            pltpu.VMEM((16 * n, width), jnp.bfloat16),
            pltpu.VMEM((width, 16 * n), jnp.bfloat16),
            pltpu.SemaphoreType.DMA((16,)),
            pltpu.SemaphoreType.DMA((8,)),
        ],
        compiler_params=pltpu.CompilerParams(vmem_limit_bytes=60 * 2**20),
        cost_estimate=pl.CostEstimate(flops=1, bytes_accessed=1, transcendentals=0),
        name="prepare",
    )(slot, row, same, other, weight, residual, prior, point)


def gram_kernel(slots, first, n, count, has_acc, has_diag, *refs):
    left_ref = refs[0]
    pieces = refs[1 : 1 + count]
    rest = refs[1 + count :]
    if has_acc:
        acc_ref, rest = rest[0], rest[1:]
    if has_diag:
        diag_ref, rest = rest[0], rest[1:]
    out_ref, lbuf, rbuf, obuf, lsem, rsem, asem, osem = rest
    width = obuf.shape[0]
    depth = rbuf.shape[0]
    tile = min(256, width)
    tiles = width // tile
    copies = []
    for i, (slot, offset, operand, source, rows) in enumerate(slots):
        copies.append(
            pltpu.make_async_copy(
                pieces[operand].at[pl.ds(source, rows)],
                rbuf.at[pl.ds((slot - first) * n + offset, rows)],
                rsem.at[i],
            )
        )
    lefts, accs, outs = [], [], []
    for m in range(tiles):
        ms = pl.ds(m * tile, tile)
        lefts.append(
            pltpu.make_async_copy(
                left_ref.at[ms, pl.ds(first * n, depth)], lbuf.at[ms], lsem.at[m]
            )
        )
        if has_acc:
            accs.append(pltpu.make_async_copy(acc_ref.at[ms], obuf.at[ms], asem.at[m]))
        outs.append(pltpu.make_async_copy(obuf.at[ms], out_ref.at[ms], osem.at[m]))
    lefts[0].start()
    for c in copies:
        c.start()
    for m in range(tiles):
        if m:
            lefts[m].start()
        if has_acc:
            accs[m].start()
    for c in copies:
        c.wait()
    for m in range(tiles):
        ms = pl.ds(m * tile, tile)
        lefts[m].wait()
        part = jnp.dot(lbuf[ms, :], rbuf[...], preferred_element_type=jnp.float32)
        if has_acc:
            accs[m].wait()
            obuf[ms, :] = obuf[ms, :] + part
        else:
            obuf[ms, :] = part
        if has_diag:
            row = lax.broadcasted_iota(jnp.int32, (tile, tile), 0)
            col = lax.broadcasted_iota(jnp.int32, (tile, tile), 1)
            extra = jnp.where(row == col, diag_ref[:, ms], 0.0)
            obuf[ms, ms] = obuf[ms, ms] + extra
        outs[m].start()
    for c in outs:
        c.wait()


def gram(left, slots, pieces, acc=None, diag=None):
    width = left.shape[0]
    n = left.shape[1] // 16
    first = min(slot[0] for slot in slots)
    depth = n * (1 + max(slot[0] for slot in slots) - first)
    used = sorted({slot[2] for slot in slots})
    slots = [(s, o, used.index(p), r, k) for s, o, p, r, k in slots]
    pieces = [pieces[p] for p in used]
    has_acc, has_diag = acc is not None, diag is not None
    tiles = width // min(256, width)
    anywhere = pl.BlockSpec(memory_space=pl.ANY)
    operands = [left, *pieces]
    far = pl.BlockSpec(memory_space=pltpu.HBM)
    in_specs = [far] + [anywhere] * len(pieces)
    if has_acc:
        operands.append(acc)
        in_specs.append(far)
    if has_diag:
        operands.append(diag)
        in_specs.append(pl.BlockSpec(memory_space=pltpu.VMEM))
    sems = [pltpu.SemaphoreType.DMA((k,)) for k in [tiles, len(slots)]]
    sems += [pltpu.SemaphoreType.DMA((tiles,))] * 2
    return pl.pallas_call(
        lambda *refs: gram_kernel(slots, first, n, len(pieces), has_acc, has_diag, *refs),
        out_shape=jax.ShapeDtypeStruct((width, width), jnp.float32),
        in_specs=in_specs,
        out_specs=far,
        scratch_shapes=[
            pltpu.VMEM((width, depth), jnp.bfloat16),
            pltpu.VMEM((depth, width), jnp.bfloat16),
            pltpu.VMEM((width, width), jnp.float32),
            *sems,
        ],
        compiler_params=pltpu.CompilerParams(vmem_limit_bytes=60 * 2**20),
        cost_estimate=pl.CostEstimate(flops=1, bytes_accessed=1, transcendentals=0),
        name="gram",
    )(*operands)


def per_device(features, labels, posterior, prior_prec):
    n, width = features.shape
    a = n * 5 // 12 // 16 * 16
    b = n - a
    row_index = lax.axis_index("rows")
    feat_index = lax.axis_index("feat")
    core, x, yh = row_index % 2, row_index // 2 % 4, row_index // 8
    z, yl = feat_index % 8, feat_index // 8

    slots, pieces, row = [], [], []

    def put(operand, *parts):
        for slot, offset, source, rows in parts:
            slots.append((slot, offset, len(pieces), source, rows))
        pieces.append(operand)

    for by in (0, -1, 1, -2, 2, -3, 3, 4):
        for yl_ in (yl, 1 - yl):
            d = ((z + by) - row_index) % 8
            x_ = jnp.where(core == 0, d % 4, -d % 4)
            row.append(yl_ * 8 + x_ * 2 + d // 4)
    row = jnp.stack(row).astype(jnp.int32)

    def slot_of(other, dy, dx):
        c_, x_ = core ^ other, (x + dx) % 4
        d = c_ * 4 + jnp.where(core == 0, x_, -x_ % 4)
        by = (d + row_index - z + 3) % 8 - 3
        rank = jnp.where(by < 0, -2 * by - 1, 2 * by)
        rank = jnp.where(by == 4, 7, rank)
        return 2 * rank + (yh ^ dy ^ yl)

    order = [(0, 0), (0, 1), (0, 3), (1, 0), (1, 1), (1, 3), (0, 2), (1, 2)]
    slot = [slot_of(other, dy, dx) for other in range(2) for dy, dx in order]
    slot = jnp.stack(slot).astype(jnp.int32)

    mine = permuted(features, spread)
    partial = jnp.dot(features, posterior, preferred_element_type=jnp.float32)
    across = swap(features, "yh")
    left1, right1 = shift(features, "x", 1), shift(features, "x", -1)
    margins = from_all(partial, "feat").sum(axis=0)
    across, left1, right1, margins, mine = together(
        across, left1, right1, margins, mine
    )

    up1, down1 = shift(mine, "z", 1), shift(mine, "z", -1)
    mine_y = swap(mine, "yl")
    left2, right2 = shift(across, "x", 1), shift(across, "x", -1)
    facts = jnp.stack([margins, labels.astype(jnp.float32)])
    facts = from_all(facts, "rows")
    up1, down1, mine_y, left2, right2, facts = together(
        up1, down1, mine_y, left2, right2, facts
    )
    put(mine, (0, 0, 0, n))
    put(mine_y, (1, 0, 0, n))

    other_a = mine_y[:a]
    up2 = shift(jnp.concatenate([up1[:a], other_a, up1[a:]]), "z", 1)
    down2 = shift(jnp.concatenate([down1, other_a]), "z", -1)
    swapped1 = swap(jnp.concatenate([up1[a:], down1[a:]]), "yl")
    twice_own, twice_far = shift(left1, "x", 1), shift(right2, "x", -1)
    up2, down2, swapped1, twice_own, twice_far = together(
        up2, down2, swapped1, twice_own, twice_far
    )
    put(up1, (2, 0, 0, n))
    put(down1, (4, 0, 0, n))
    put(swapped1, (3, a, 0, b), (5, a, b, b))

    up3, down3 = shift(up2, "z", 1), shift(down2, "z", -1)
    swap_u2, swap_d2 = swap(up2[2 * a :], "yl"), swap(down2[a:n], "yl")
    same = [features, right1, left1, across, right2, left2, twice_own, twice_far]
    same = jnp.stack(same)
    other = swap(same, "c")
    chance = jax.nn.sigmoid(facts[:, :1])
    weight = (chance * (1.0 - chance)).astype(jnp.bfloat16).astype(jnp.float32)
    residual = (facts[:, 1:] - chance).astype(jnp.bfloat16)
    left, gradient = prepare(
        slot, row, same, other, weight, residual, prior_prec[None], posterior[None]
    )
    up3, down3, swap_u2, swap_d2, left = together(up3, down3, swap_u2, swap_d2, left)
    put(up2, (6, 0, 0, a), (3, 0, a, a), (6, a, 2 * a, b))
    put(down2, (8, 0, 0, n), (5, 0, n, a))
    put(swap_u2, (7, a, 0, b))
    put(swap_d2, (9, a, 0, b))

    up4 = shift(up3[: 2 * a], "z", 1)
    down4 = shift(down3[a:], "z", -1)
    swap_u3, swap_d3 = swap(up3[2 * a :], "yl"), swap(down3[a:n], "yl")
    put(up3, (10, 0, 0, a), (7, 0, a, a), (10, a, 2 * a, b))
    put(down3, (12, 0, 0, n), (9, 0, n, a))
    put(swap_u3, (11, a, 0, b))
    put(swap_d3, (13, a, 0, b))
    acc = gram(left, [slot for slot in slots if slot[0] < 10], pieces)
    up4, down4, swap_u3, swap_d3, acc = together(up4, down4, swap_u3, swap_d3, acc)

    up5 = shift(up4[a:], "z", 1)
    swapped4 = swap(down4[:b], "yl")
    pieces[-2:] = [swap_u3, swap_d3]
    put(up4, (14, 0, 0, a), (11, 0, a, a))
    put(down4, (14, a, 0, b), (13, 0, b, a))
    acc = gram(left, [slot for slot in slots if 10 <= slot[0] < 14], pieces, acc)
    put(up5, (15, 0, 0, a))
    put(swapped4, (15, a, 0, b))

    diag = jnp.where(row_index == feat_index, prior_prec, 0.0)[None, :]
    last = [slot for slot in slots if slot[0] >= 14]
    hessian = gram(left, last, pieces, acc, diag)
    return (hessian, gradient[0])


def solution(mesh):
    in_specs = (P("rows", "feat"), P("rows"), P("feat"), P("feat"))
    out_specs = (P("feat", "rows"), P("feat"))
    return jax.shard_map(
        per_device, mesh=mesh, in_specs=in_specs, out_specs=out_specs, check_vma=False
    )
```

time: 128 us -> 117 us (0.914)
  waiting for transfers between devices: 42.9 us -> 18.1 us
  local copies, waits for them, and re-layouts: 8.4 us -> 14.1 us
  Pallas kernels: 25.8 us -> 30.3 us
  starting transfers between devices: 45 us -> 48 us
    ppermute x23 -> x25, waiting for transfers between devices: 29.9 us -> 12.1 us  [permuted(): return lax.ppermute(x, ('rows', 'feat'), pairs)]
    all_to_all x2, waiting for transfers between devices: 13 us -> 6.05 us  [from_all(): return lax.all_to_all(copies, axis, split_axis=0, concat_axis=0, tiled=True)]
    unnamed x64 -> x44, local copies, waits for them, and re-layouts: 3.81 us -> 10.1 us
    pallas_call x2 -> x3, Pallas kernels: 16.9 us -> 22 us  [gram(): pl.pallas_call(lambda *refs: gram_kernel(slots, first, n, len(pieces), ha...]
    ppermute x23 -> x25, starting transfers between devices: 31.6 us -> 34.5 us  [permuted(): return lax.ppermute(x, ('rows', 'feat'), pairs)]
    slice x5 -> x7, local copies, waits for them, and re-layouts: 3.02 us -> 0.12 us  [the longest x2 0.03 us: per_device(): swap_u2, swap_d2 = (swap(up2[2 * a:], 'yl'), swap(down2[a:n], 'yl'))]
  transfers between devices with their start and end apart: 25 -> 27, of which waited for: 10 -> 10; matrix products, arithmetic and copies ran while one was open for 7% -> 12% of each run, Pallas kernels for 14% -> 21%
where the time goes in v3:
time: 117 us; the launch traced here: 116 us
  starting transfers between devices  48 us (41%)
  Pallas kernels  30.3 us (26%)
  waiting for transfers between devices  18.1 us (15%)
  local copies, waits for them, and re-layouts  14.1 us (12%)
  other arithmetic  2.7 us (2%)
  matrix products  1.19 us (1%)
    ppermute x25, starting transfers between devices, permuted(): return lax.ppermute(x, ('rows', 'feat'), pairs)  34.5 us
    pallas_call x3, Pallas kernels, gram(): pl.pallas_call(lambda *refs: gram_kernel(slots, first, n, len(pieces), ha...  22 us
    all_to_all x2, starting transfers between devices, from_all(): return lax.all_to_all(copies, axis, split_axis=0, concat_axis=0, tiled=True)  13.4 us
    ppermute x25, waiting for transfers between devices, permuted(): return lax.ppermute(x, ('rows', 'feat'), pairs)  12.1 us
    unnamed x44, local copies, waits for them, and re-layouts  10.1 us
    pallas_call x1, Pallas kernels, prepare(): pl.pallas_call(prepare_kernel, in_specs=[smem, smem] + [anywhere] * 2 + [...  8.3 us
    all_to_all x2, waiting for transfers between devices, from_all(): return lax.all_to_all(copies, axis, split_axis=0, concat_axis=0, tiled=True)  6.05 us
  transfers between devices with their start and end apart: 27, of which 10 were waited for; matrix products, arithmetic and copies ran while one was open for 12% of the time, Pallas kernels for 21%

profile of v3, /device:TPU:64, one launch (start us, length us, event | category | flops | bytes accessed | tf_op | source)
XLA Modules:
  0.0 115.5 jit_solution(16246088751426709272)
XLA Ops:
  0.6 3.3 %collective-permute-start = (bf16[192,1024]{1,0:T(8,128)(2,1)}, bf16[192,1024]{1,0:T(8,128)(2,1)S(1)}, u32[]{:S(2)}, u32[]{:S(2)}) collective-permute-start(bf16[192,1024]{1,0:T(8,128)(2,1)} %param.4), channel_id=1, source_target_pairs={{0,128},{1,129},{2,130},{3,131},{4,132},{5,133},{6,134},{7,135},{8... | collective-permute-start | bytes 1179656 | tf_op jit(solution)/shard_map/ppermute | solution.py:22
  3.9 1.5 %collective-permute-start.1 = (bf16[192,1024]{1,0:T(8,128)(2,1)}, bf16[192,1024]{1,0:T(8,128)(2,1)}, u32[]{:S(2)}, u32[]{:S(2)}) collective-permute-start(bf16[192,1024]{1,0:T(8,128)(2,1)} %param.4), channel_id=1, source_target_pairs={{0,32},{1,33},{2,34},{3,35},{4,36},{5,37},{6,38},{7,39},{8,40},{9,... | collective-permute-start | bytes 1179656 | tf_op jit(solution)/shard_map/ppermute | solution.py:22
  5.4 1.7 %collective-permute-start.2 = (bf16[192,1024]{1,0:T(8,128)(2,1)}, bf16[192,1024]{1,0:T(8,128)(2,1)S(1)}, u32[]{:S(2)}, u32[]{:S(2)}) collective-permute-start(bf16[192,1024]{1,0:T(8,128)(2,1)} %param.4), channel_id=1, source_target_pairs={{0,96},{1,97},{2,98},{3,99},{4,100},{5,101},{6,102},{7,103},{8,104... | collective-permute-start | bytes 1179656 | tf_op jit(solution)/shard_map/ppermute | solution.py:22
  7.1 2.2 %collective-permute-start.3 = (bf16[192,1024]{1,0:T(8,128)(2,1)}, bf16[192,1024]{1,0:T(8,128)(2,1)}, u32[]{:S(2)}, u32[]{:S(2)}) collective-permute-start(bf16[192,1024]{1,0:T(8,128)(2,1)} %param.4), channel_id=1, source_target_pairs={{0,0},{1,17},{2,34},{3,51},{4,68},{5,85},{6,102},{7,119},{8,128},{... | collective-permute-start | bytes 1179656 | tf_op jit(solution)/shard_map/ppermute | solution.py:22
  11.8 9.7 %all-to-all-start = ((f32[16,1,192]{2,1,0:T(1,128)}), f32[16,1,192]{2,1,0:T(1,128)S(1)}, u32[]{:S(2)}, u32[]{:S(2)}) async-start(f32[16,1,192]{2,1,0:T(1,128)} %broadcast_in_dim.19), calls=%async_computation | async-start | bytes 32768 | tf_op jit(solution)/shard_map/all_to_all | solution.py:41
  21.5 1.8 %bitcast_dynamic-update-slice_fusion.7 = bf16[8,192,1024]{2,1,0:T(8,128)(2,1)} fusion(bf16[192,1024]{1,0:T(8,128)(2,1)} %param.4), kind=kLoop, calls=%fused_computation.10 | loop fusion | bytes 786432
  24.0 3.8 %all-to-all-done = f32[16,1,192]{2,1,0:T(1,128)S(1)} async-done(((f32[16,1,192]{2,1,0:T(1,128)}), f32[16,1,192]{2,1,0:T(1,128)S(1)}, u32[]{:S(2)}, u32[]{:S(2)}) %all-to-all-start) | async-done | bytes 12320 | tf_op jit(solution)/shard_map/all_to_all | solution.py:41
  31.1 2.7 %collective-permute-start.8 = (bf16[192,1024]{1,0:T(8,128)(2,1)S(1)}, bf16[192,1024]{1,0:T(8,128)(2,1)S(1)}, u32[]{:S(2)}, u32[]{:S(2)}) collective-permute-start(bf16[192,1024]{1,0:T(8,128)(2,1)S(1)} %collective-permute-done), channel_id=1, source_target_pairs={{0,96},{1,97},{2,98},{3,99},{4,100},{5,101},{6,102},{7,103},{8,104... | collective-permute-start | bytes 1179656 | tf_op jit(solution)/shard_map/ppermute | solution.py:22
  34.5 3.8 %all-to-all-start.1 = ((f32[16,2,192]{2,1,0:T(2,128)}), f32[16,2,192]{2,1,0:T(2,128)S(1)}, u32[]{:S(2)}, u32[]{:S(2)}) async-start(f32[16,2,192]{2,1,0:T(2,128)} %broadcast_in_dim.20), calls=%async_computation.1 | async-start | bytes 65536 | tf_op jit(solution)/shard_map/all_to_all | solution.py:41
  39.0 1.8 %bitcast_dynamic-update-slice_fusion.5 = bf16[8,192,1024]{2,1,0:T(8,128)(2,1)} fusion(bf16[8,192,1024]{2,1,0:T(8,128)(2,1)} %bitcast_dynamic-update-slice_fusion.6, bf16[192,1024]{1,0:T(8,128)(2,1)} %collective-permute-done.1), kind=kLoop, calls=%fused_computation.8 | loop fusion | bytes 786432
  41.5 1.9 %collective-permute-start.12 = (bf16[192,1024]{1,0:T(8,128)(2,1)}, bf16[192,1024]{1,0:T(8,128)(2,1)}, u32[]{:S(2)}, u32[]{:S(2)}) collective-permute-start(bf16[192,1024]{1,0:T(8,128)(2,1)} %collective-permute-done.1), channel_id=1, source_target_pairs={{0,32},{1,33},{2,34},{3,35},{4,36},{5,37},{6,38},{7,39},{8,40},{9,... | collective-permute-start | bytes 1179656 | tf_op jit(solution)/shard_map/ppermute | solution.py:22
  43.5 2.2 %all-to-all-done.1 = f32[16,2,192]{2,1,0:T(2,128)S(1)} async-done(((f32[16,2,192]{2,1,0:T(2,128)}), f32[16,2,192]{2,1,0:T(2,128)S(1)}, u32[]{:S(2)}, u32[]{:S(2)}) %all-to-all-start.1) | async-done | bytes 24608 | tf_op jit(solution)/shard_map/all_to_all | solution.py:41
  45.9 1.5 %collective-permute-start.10 = (bf16[272,1024]{1,0:T(8,128)(2,1)S(1)}, bf16[272,1024]{1,0:T(8,128)(2,1)S(1)}, u32[]{:S(2)}, u32[]{:S(2)}) collective-permute-start(bf16[272,1024]{1,0:T(8,128)(2,1)S(1)} %get-tuple-element.60), channel_id=1, source_target_pairs={{0,7},{1,0},{2,1},{3,2},{4,3},{5,4},{6,5},{7,6},{8,15},{9,8},{10,9... | collective-permute-start | bytes 1671176 | tf_op jit(solution)/shard_map/ppermute | solution.py:22
  52.1 2.4 %collective-permute-done.12 = bf16[192,1024]{1,0:T(8,128)(2,1)} collective-permute-done((bf16[192,1024]{1,0:T(8,128)(2,1)}, bf16[192,1024]{1,0:T(8,128)(2,1)}, u32[]{:S(2)}, u32[]{:S(2)}) %collective-permute-start.12) | collective-permute-done | bytes 393248 | tf_op jit(solution)/shard_map/ppermute | solution.py:22
  54.5 5.0 %collective-permute-done.13 = bf16[192,1024]{1,0:T(8,128)(2,1)S(1)} collective-permute-done((bf16[192,1024]{1,0:T(8,128)(2,1)S(1)}, bf16[192,1024]{1,0:T(8,128)(2,1)S(1)}, u32[]{:S(2)}, u32[]{:S(2)}) %collective-permute-start.13) | collective-permute-done | bytes 393248 | tf_op jit(solution)/shard_map/ppermute | solution.py:22
  60.7 2.1 %collective-permute-done.9.refs_6_ = bf16[272,1024]{1,0:T(8,128)(2,1)S(1)} collective-permute-done((bf16[272,1024]{1,0:T(8,128)(2,1)S(1)}, bf16[272,1024]{1,0:T(8,128)(2,1)S(1)}, u32[]{:S(2)}, u32[]{:S(2)}) %collective-permute-start.9) | collective-permute-done | bytes 557088 | tf_op jit(solution)/shard_map/ppermute | solution.py:22
  62.7 2.0 %bitcast_dynamic-update-slice_fusion.1 = bf16[8,192,1024]{2,1,0:T(8,128)(2,1)} fusion(bf16[8,192,1024]{2,1,0:T(8,128)(2,1)} %bitcast_dynamic-update-slice_fusion.2, bf16[192,1024]{1,0:T(8,128)(2,1)} %collective-permute-done.12), kind=kLoop, calls=%fused_computation.4 | loop fusion | bytes 786432
  72.8 8.3 %prepare.1 = (bf16[1024,3072]{1,0:T(8,128)(2,1)}, f32[1,1024]{1,0:T(1,128)}) custom-call(s32[16]{0:T(128)} %stack.157.slot_ref, s32[16]{0:T(128)} %stack.174.row_ref, bf16[8,192,1024]{2,1,0:T(8,128)(2,1)} %bitcast_dynamic-update-slice_fusion.refs_0_, bf16[8,192,1024]{2,1,0:T(8,128)(2,1)} %collective-permute-done.18.refs_1_, f32[16,1,192]{2,1,0:T(1,128)} %fusion.1.refs_2_, ...), custom_call_target="tpu_custom_call" | custom-call | flops 1 | bytes 1 | tf_op jit(solution)/shard_map/prepare/pallas_call | solution.py:95
  82.2 2.4 %collective-permute-start.20 = (bf16[192,1024]{1,0:T(8,128)(2,1)S(1)}, bf16[192,1024]{1,0:T(8,128)(2,1)S(1)}, u32[]{:S(2)}, u32[]{:S(2)}) collective-permute-start(bf16[192,1024]{1,0:T(8,128)(2,1)S(1)} %slice.52), channel_id=1, source_target_pairs={{0,7},{1,0},{2,1},{3,2},{4,3},{5,4},{6,5},{7,6},{8,15},{9,8},{10,9... | collective-permute-start | bytes 1179656 | tf_op jit(solution)/shard_map/ppermute | solution.py:22
  86.1 1.4 %collective-permute-start.22 = (bf16[112,1024]{1,0:T(8,128)(2,1)S(1)}, bf16[112,1024]{1,0:T(8,128)(2,1)S(1)}, u32[]{:S(2)}, u32[]{:S(2)}) collective-permute-start(bf16[112,1024]{1,0:T(8,128)(2,1)S(1)} %slice.54), channel_id=1, source_target_pairs={{0,8},{1,9},{2,10},{3,11},{4,12},{5,13},{6,14},{7,15},{8,0},{9,1},... | collective-permute-start | bytes 688136 | tf_op jit(solution)/shard_map/ppermute | solution.py:22
  87.6 9.1 %gram.3.refs_7_ = f32[1024,1024]{1,0:T(8,128)} custom-call(bf16[1024,3072]{1,0:T(8,128)(2,1)} %get-tuple-element.46.refs_0_, bf16[192,1024]{1,0:T(8,128)(2,1)} %collective-permute-done.3.refs_1_, bf16[192,1024]{1,0:T(8,128)(2,1)} %copy-done.8, bf16[192,1024]{1,0:T(8,128)(2,1)} %copy-done.5, bf16[192,1024]{1,0:T(8,128)(2,1)} %copy-done.3, ...), custom_call_target="tpu_custom_call" | custom-call | flops 1 | bytes 1 | tf_op jit(solution)/shard_map/gram/pallas_call | solution.py:199
  97.8 3.2 %collective-permute-start.23 = (bf16[80,1024]{1,0:T(8,128)(2,1)S(1)}, bf16[80,1024]{1,0:T(8,128)(2,1)S(1)}, u32[]{:S(2)}, u32[]{:S(2)}) collective-permute-start(bf16[80,1024]{1,0:T(8,128)(2,1)S(1)} %slice.55), channel_id=1, source_target_pairs={{0,1},{1,2},{2,3},{3,4},{4,5},{5,6},{6,7},{7,0},{8,9},{9,10},{10,1... | collective-permute-start | bytes 491528 | tf_op jit(solution)/shard_map/ppermute | solution.py:22
  101.7 6.5 %gram.4.refs_5_ = f32[1024,1024]{1,0:T(8,128)} custom-call(bf16[1024,3072]{1,0:T(8,128)(2,1)} %get-tuple-element.46.refs_0_, bf16[272,1024]{1,0:T(8,128)(2,1)} %copy-done.1, bf16[272,1024]{1,0:T(8,128)(2,1)} %copy-done, bf16[112,1024]{1,0:T(8,128)(2,1)} %copy-done.10, bf16[112,1024]{1,0:T(8,128)(2,1)} %copy-done.11, bf16[160,1024]{1,0:T(8,128)(2,1)} %copy-done.4, ...), custom_call_target="tpu_custom_call" | custom-call | flops 1 | bytes 1 | tf_op jit(solution)/shard_map/gram/pallas_call | solution.py:199
  109.0 6.3 %gram.5 = f32[1024,1024]{1,0:T(8,128)} custom-call(bf16[1024,3072]{1,0:T(8,128)(2,1)} %get-tuple-element.46.refs_0_, bf16[160,1024]{1,0:T(8,128)(2,1)} %copy-done.4, bf16[192,1024]{1,0:T(8,128)(2,1)} %copy-done.2, bf16[80,1024]{1,0:T(8,128)(2,1)} %copy-done.15, bf16[112,1024]{1,0:T(8,128)(2,1)} %copy-done.12, f32[1024,1024]{1,0:T(8,128)} %gram.4.refs_5_, ...), custom_call_target="tpu_custom_call" | custom-call | flops 1 | bytes 1 | tf_op jit(solution)/shard_map/gram/pallas_call | solution.py:199
  (105 shorter events, 27.7 us)
Async XLA Ops:
  0.6 27.2 %collective-permute-start = (bf16[192,1024]{1,0:T(8,128)(2,1)}, bf16[192,1024]{1,0:T(8,128)(2,1)S(1)}, u32[]{:S(2)}, u32[]{:S(2)}) collective-permute-start(bf16[192,1024]{1,0:T(8,128)(2,1)} %param.4), channel_id=1, source_target_pairs={{0,128},{1,129},{2,130},{3,131},{4,132},{5,133},{6,134},{7,135},{8... | collective-permute-start | bytes 1179656 | tf_op jit(solution)/shard_map/ppermute | solution.py:22
  3.9 23.9 %collective-permute-start.1 = (bf16[192,1024]{1,0:T(8,128)(2,1)}, bf16[192,1024]{1,0:T(8,128)(2,1)}, u32[]{:S(2)}, u32[]{:S(2)}) collective-permute-start(bf16[192,1024]{1,0:T(8,128)(2,1)} %param.4), channel_id=1, source_target_pairs={{0,32},{1,33},{2,34},{3,35},{4,36},{5,37},{6,38},{7,39},{8,40},{9,... | collective-permute-start | bytes 1179656 | tf_op jit(solution)/shard_map/ppermute | solution.py:22
  5.4 22.5 %collective-permute-start.2 = (bf16[192,1024]{1,0:T(8,128)(2,1)}, bf16[192,1024]{1,0:T(8,128)(2,1)S(1)}, u32[]{:S(2)}, u32[]{:S(2)}) collective-permute-start(bf16[192,1024]{1,0:T(8,128)(2,1)} %param.4), channel_id=1, source_target_pairs={{0,96},{1,97},{2,98},{3,99},{4,100},{5,101},{6,102},{7,103},{8,104... | collective-permute-start | bytes 1179656 | tf_op jit(solution)/shard_map/ppermute | solution.py:22
  7.1 20.7 %collective-permute-start.3 = (bf16[192,1024]{1,0:T(8,128)(2,1)}, bf16[192,1024]{1,0:T(8,128)(2,1)}, u32[]{:S(2)}, u32[]{:S(2)}) collective-permute-start(bf16[192,1024]{1,0:T(8,128)(2,1)} %param.4), channel_id=1, source_target_pairs={{0,0},{1,17},{2,34},{3,51},{4,68},{5,85},{6,102},{7,119},{8,128},{... | collective-permute-start | bytes 1179656 | tf_op jit(solution)/shard_map/ppermute | solution.py:22
  11.8 16.0 %all-to-all-start = ((f32[16,1,192]{2,1,0:T(1,128)}), f32[16,1,192]{2,1,0:T(1,128)S(1)}, u32[]{:S(2)}, u32[]{:S(2)}) async-start(f32[16,1,192]{2,1,0:T(1,128)} %broadcast_in_dim.19), calls=%async_computation | async-start | bytes 32768 | tf_op jit(solution)/shard_map/all_to_all | solution.py:41
  27.9 13.7 %collective-permute-start.4 = (bf16[192,1024]{1,0:T(8,128)(2,1)}, bf16[192,1024]{1,0:T(8,128)(2,1)S(1)}, u32[]{:S(2)}, u32[]{:S(2)}) collective-permute-start(bf16[192,1024]{1,0:T(8,128)(2,1)} %collective-permute-done.3.refs_1_), channel_id=1, source_target_pairs={{0,1},{1,2},{2,3},{3,4},{4,5},{5,6},{6,7},{7,0},{8,9},{9,10},{10,1... | collective-permute-start | bytes 1179656 | tf_op jit(solution)/shard_map/ppermute | solution.py:22
  28.6 17.1 %collective-permute-start.5 = (bf16[192,1024]{1,0:T(8,128)(2,1)}, bf16[192,1024]{1,0:T(8,128)(2,1)S(1)}, u32[]{:S(2)}, u32[]{:S(2)}) collective-permute-start(bf16[192,1024]{1,0:T(8,128)(2,1)} %collective-permute-done.3.refs_1_), channel_id=1, source_target_pairs={{0,7},{1,0},{2,1},{3,2},{4,3},{5,4},{6,5},{7,6},{8,15},{9,8},{10,9... | collective-permute-start | bytes 1179656 | tf_op jit(solution)/shard_map/ppermute | solution.py:22
  30.0 15.7 %collective-permute-start.6 = (bf16[192,1024]{1,0:T(8,128)(2,1)}, bf16[192,1024]{1,0:T(8,128)(2,1)S(1)}, u32[]{:S(2)}, u32[]{:S(2)}) collective-permute-start(bf16[192,1024]{1,0:T(8,128)(2,1)} %collective-permute-done.3.refs_1_), channel_id=1, source_target_pairs={{0,8},{1,9},{2,10},{3,11},{4,12},{5,13},{6,14},{7,15},{8,0},{9,1},... | collective-permute-start | bytes 1179656 | tf_op jit(solution)/shard_map/ppermute | solution.py:22
  30.6 15.1 %collective-permute-start.7 = (bf16[192,1024]{1,0:T(8,128)(2,1)S(1)}, bf16[192,1024]{1,0:T(8,128)(2,1)S(1)}, u32[]{:S(2)}, u32[]{:S(2)}) collective-permute-start(bf16[192,1024]{1,0:T(8,128)(2,1)S(1)} %collective-permute-done), channel_id=1, source_target_pairs={{0,32},{1,33},{2,34},{3,35},{4,36},{5,37},{6,38},{7,39},{8,40},{9,... | collective-permute-start | bytes 1179656 | tf_op jit(solution)/shard_map/ppermute | solution.py:22
  31.1 14.6 %collective-permute-start.8 = (bf16[192,1024]{1,0:T(8,128)(2,1)S(1)}, bf16[192,1024]{1,0:T(8,128)(2,1)S(1)}, u32[]{:S(2)}, u32[]{:S(2)}) collective-permute-start(bf16[192,1024]{1,0:T(8,128)(2,1)S(1)} %collective-permute-done), channel_id=1, source_target_pairs={{0,96},{1,97},{2,98},{3,99},{4,100},{5,101},{6,102},{7,103},{8,104... | collective-permute-start | bytes 1179656 | tf_op jit(solution)/shard_map/ppermute | solution.py:22
  34.5 11.2 %all-to-all-start.1 = ((f32[16,2,192]{2,1,0:T(2,128)}), f32[16,2,192]{2,1,0:T(2,128)S(1)}, u32[]{:S(2)}, u32[]{:S(2)}) async-start(f32[16,2,192]{2,1,0:T(2,128)} %broadcast_in_dim.20), calls=%async_computation.1 | async-start | bytes 65536 | tf_op jit(solution)/shard_map/all_to_all | solution.py:41
  41.5 13.0 %collective-permute-start.12 = (bf16[192,1024]{1,0:T(8,128)(2,1)}, bf16[192,1024]{1,0:T(8,128)(2,1)}, u32[]{:S(2)}, u32[]{:S(2)}) collective-permute-start(bf16[192,1024]{1,0:T(8,128)(2,1)} %collective-permute-done.1), channel_id=1, source_target_pairs={{0,32},{1,33},{2,34},{3,35},{4,36},{5,37},{6,38},{7,39},{8,40},{9,... | collective-permute-start | bytes 1179656 | tf_op jit(solution)/shard_map/ppermute | solution.py:22
  45.9 14.7 %collective-permute-start.10 = (bf16[272,1024]{1,0:T(8,128)(2,1)S(1)}, bf16[272,1024]{1,0:T(8,128)(2,1)S(1)}, u32[]{:S(2)}, u32[]{:S(2)}) collective-permute-start(bf16[272,1024]{1,0:T(8,128)(2,1)S(1)} %get-tuple-element.60), channel_id=1, source_target_pairs={{0,7},{1,0},{2,1},{3,2},{4,3},{5,4},{6,5},{7,6},{8,15},{9,8},{10,9... | collective-permute-start | bytes 1671176 | tf_op jit(solution)/shard_map/ppermute | solution.py:22
  47.4 15.3 %collective-permute-start.9 = (bf16[272,1024]{1,0:T(8,128)(2,1)S(1)}, bf16[272,1024]{1,0:T(8,128)(2,1)S(1)}, u32[]{:S(2)}, u32[]{:S(2)}) collective-permute-start(bf16[272,1024]{1,0:T(8,128)(2,1)S(1)} %get-tuple-element.61), channel_id=1, source_target_pairs={{0,1},{1,2},{2,3},{3,4},{4,5},{5,6},{6,7},{7,0},{8,9},{9,10},{10,1... | collective-permute-start | bytes 1671176 | tf_op jit(solution)/shard_map/ppermute | solution.py:22
  48.1 12.1 %collective-permute-start.11 = (bf16[224,1024]{1,0:T(8,128)(2,1)S(1)}, bf16[224,1024]{1,0:T(8,128)(2,1)S(1)}, u32[]{:S(2)}, u32[]{:S(2)}) collective-permute-start(bf16[224,1024]{1,0:T(8,128)(2,1)S(1)} %pad_maximum_fusion.2), channel_id=1, source_target_pairs={{0,8},{1,9},{2,10},{3,11},{4,12},{5,13},{6,14},{7,15},{8,0},{9,1},... | collective-permute-start | bytes 1376264 | tf_op jit(solution)/shard_map/ppermute | solution.py:22
  65.5 16.3 %collective-permute-start.14 = (bf16[272,1024]{1,0:T(8,128)(2,1)S(1)}, bf16[272,1024]{1,0:T(8,128)(2,1)S(1)}, u32[]{:S(2)}, u32[]{:S(2)}) collective-permute-start(bf16[272,1024]{1,0:T(8,128)(2,1)S(1)} %collective-permute-done.9.refs_6_), channel_id=1, source_target_pairs={{0,1},{1,2},{2,3},{3,4},{4,5},{5,6},{6,7},{7,0},{8,9},{9,10},{10,1... | collective-permute-start | bytes 1671176 | tf_op jit(solution)/shard_map/ppermute | solution.py:22
  66.3 15.9 %collective-permute-start.15 = (bf16[272,1024]{1,0:T(8,128)(2,1)S(1)}, bf16[272,1024]{1,0:T(8,128)(2,1)S(1)}, u32[]{:S(2)}, u32[]{:S(2)}) collective-permute-start(bf16[272,1024]{1,0:T(8,128)(2,1)S(1)} %collective-permute-done.10.refs_7_), channel_id=1, source_target_pairs={{0,7},{1,0},{2,1},{3,2},{4,3},{5,4},{6,5},{7,6},{8,15},{9,8},{10,9... | collective-permute-start | bytes 1671176 | tf_op jit(solution)/shard_map/ppermute | solution.py:22
  69.4 11.7 %collective-permute-start.16 = (bf16[112,1024]{1,0:T(8,128)(2,1)S(1)}, bf16[112,1024]{1,0:T(8,128)(2,1)S(1)}, u32[]{:S(2)}, u32[]{:S(2)}) collective-permute-start(bf16[112,1024]{1,0:T(8,128)(2,1)S(1)} %slice.47), channel_id=1, source_target_pairs={{0,8},{1,9},{2,10},{3,11},{4,12},{5,13},{6,14},{7,15},{8,0},{9,1},... | collective-permute-start | bytes 688136 | tf_op jit(solution)/shard_map/ppermute | solution.py:22
  70.8 11.1 %collective-permute-start.17 = (bf16[112,1024]{1,0:T(8,128)(2,1)S(1)}, bf16[112,1024]{1,0:T(8,128)(2,1)S(1)}, u32[]{:S(2)}, u32[]{:S(2)}) collective-permute-start(bf16[112,1024]{1,0:T(8,128)(2,1)S(1)} %slice.48), channel_id=1, source_target_pairs={{0,8},{1,9},{2,10},{3,11},{4,12},{5,13},{6,14},{7,15},{8,0},{9,1},... | collective-permute-start | bytes 688136 | tf_op jit(solution)/shard_map/ppermute | solution.py:22
  82.2 14.9 %collective-permute-start.20 = (bf16[192,1024]{1,0:T(8,128)(2,1)S(1)}, bf16[192,1024]{1,0:T(8,128)(2,1)S(1)}, u32[]{:S(2)}, u32[]{:S(2)}) collective-permute-start(bf16[192,1024]{1,0:T(8,128)(2,1)S(1)} %slice.52), channel_id=1, source_target_pairs={{0,7},{1,0},{2,1},{3,2},{4,3},{5,4},{6,5},{7,6},{8,15},{9,8},{10,9... | collective-permute-start | bytes 1179656 | tf_op jit(solution)/shard_map/ppermute | solution.py:22
  84.7 12.4 %collective-permute-start.19 = (bf16[160,1024]{1,0:T(8,128)(2,1)S(1)}, bf16[160,1024]{1,0:T(8,128)(2,1)S(1)}, u32[]{:S(2)}, u32[]{:S(2)}) collective-permute-start(bf16[160,1024]{1,0:T(8,128)(2,1)S(1)} %slice.51), channel_id=1, source_target_pairs={{0,1},{1,2},{2,3},{3,4},{4,5},{5,6},{6,7},{7,0},{8,9},{9,10},{10,1... | collective-permute-start | bytes 983048 | tf_op jit(solution)/shard_map/ppermute | solution.py:22
  85.4 11.3 %collective-permute-start.21 = (bf16[112,1024]{1,0:T(8,128)(2,1)S(1)}, bf16[112,1024]{1,0:T(8,128)(2,1)S(1)}, u32[]{:S(2)}, u32[]{:S(2)}) collective-permute-start(bf16[112,1024]{1,0:T(8,128)(2,1)S(1)} %slice.53), channel_id=1, source_target_pairs={{0,8},{1,9},{2,10},{3,11},{4,12},{5,13},{6,14},{7,15},{8,0},{9,1},... | collective-permute-start | bytes 688136 | tf_op jit(solution)/shard_map/ppermute | solution.py:22
  86.1 10.9 %collective-permute-start.22 = (bf16[112,1024]{1,0:T(8,128)(2,1)S(1)}, bf16[112,1024]{1,0:T(8,128)(2,1)S(1)}, u32[]{:S(2)}, u32[]{:S(2)}) collective-permute-start(bf16[112,1024]{1,0:T(8,128)(2,1)S(1)} %slice.54), channel_id=1, source_target_pairs={{0,8},{1,9},{2,10},{3,11},{4,12},{5,13},{6,14},{7,15},{8,0},{9,1},... | collective-permute-start | bytes 688136 | tf_op jit(solution)/shard_map/ppermute | solution.py:22
  97.1 11.1 %collective-permute-start.24 = (bf16[112,1024]{1,0:T(8,128)(2,1)S(1)}, bf16[112,1024]{1,0:T(8,128)(2,1)S(1)}, u32[]{:S(2)}, u32[]{:S(2)}) collective-permute-start(bf16[112,1024]{1,0:T(8,128)(2,1)S(1)} %slice.56), channel_id=1, source_target_pairs={{0,8},{1,9},{2,10},{3,11},{4,12},{5,13},{6,14},{7,15},{8,0},{9,1},... | collective-permute-start | bytes 688136 | tf_op jit(solution)/shard_map/ppermute | solution.py:22
  (21 other events, 214.0 us)

commit v4 on v3

--- a/solution.py
+++ b/solution.py
@@ -112,7 +112,7 @@
     )(slot, row, same, other, weight, residual, prior, point)
 
 
-def gram_kernel(slots, first, n, count, has_acc, has_diag, *refs):
+def gram_kernel(slots, first, n, count, cuts, has_acc, has_diag, *refs):
     left_ref = refs[0]
     pieces = refs[1 : 1 + count]
     rest = refs[1 + count :]
@@ -120,56 +120,68 @@
         acc_ref, rest = rest[0], rest[1:]
     if has_diag:
         diag_ref, rest = rest[0], rest[1:]
-    out_ref, lbuf, rbuf, obuf, lsem, rsem, asem, osem = rest
+    out_ref, lbuf, rbuf, tbuf, abuf, obuf, lsem, rsem, asem, osem = rest
     width = obuf.shape[0]
-    depth = rbuf.shape[0]
     tile = min(256, width)
     tiles = width // tile
-    copies = []
+    spans = list(zip(cuts[:-1], cuts[1:]))
+    copies = [[] for _ in spans]
     for i, (slot, offset, operand, source, rows) in enumerate(slots):
-        copies.append(
+        at = (slot - first) * n + offset
+        span = [k for k, (lo, hi) in enumerate(spans) if lo <= at < hi][0]
+        copies[span].append(
             pltpu.make_async_copy(
                 pieces[operand].at[pl.ds(source, rows)],
-                rbuf.at[pl.ds((slot - first) * n + offset, rows)],
+                rbuf.at[pl.ds(at, rows)],
                 rsem.at[i],
             )
         )
     lefts, accs, outs = [], [], []
     for m in range(tiles):
         ms = pl.ds(m * tile, tile)
-        lefts.append(
-            pltpu.make_async_copy(
-                left_ref.at[ms, pl.ds(first * n, depth)], lbuf.at[ms], lsem.at[m]
-            )
-        )
+        for k, (lo, hi) in enumerate(spans):
+            lefts.append(
+                pltpu.make_async_copy(
+                    left_ref.at[ms, pl.ds(first * n + lo, hi - lo)],
+                    lbuf.at[ms, pl.ds(lo, hi - lo)],
+                    lsem.at[m * len(spans) + k],
+                )
+            )
         if has_acc:
-            accs.append(pltpu.make_async_copy(acc_ref.at[ms], obuf.at[ms], asem.at[m]))
+            accs.append(pltpu.make_async_copy(acc_ref.at[ms], abuf.at[ms], asem.at[m]))
         outs.append(pltpu.make_async_copy(obuf.at[ms], out_ref.at[ms], osem.at[m]))
-    lefts[0].start()
-    for c in copies:
+    for k in range(len(spans)):
+        lefts[k].start()
+        for c in copies[k]:
+            c.start()
+        for m in range(1, tiles):
+            lefts[m * len(spans) + k].start()
+    for c in accs:
         c.start()
-    for m in range(tiles):
-        if m:
-            lefts[m].start()
-        if has_acc:
-            accs[m].start()
-    for c in copies:
-        c.wait()
-    for m in range(tiles):
-        ms = pl.ds(m * tile, tile)
-        lefts[m].wait()
-        part = jnp.dot(lbuf[ms, :], rbuf[...], preferred_element_type=jnp.float32)
-        if has_acc:
-            accs[m].wait()
-            obuf[ms, :] = obuf[ms, :] + part
-        else:
-            obuf[ms, :] = part
-        if has_diag:
-            row = lax.broadcasted_iota(jnp.int32, (tile, tile), 0)
-            col = lax.broadcasted_iota(jnp.int32, (tile, tile), 1)
-            extra = jnp.where(row == col, diag_ref[:, ms], 0.0)
-            obuf[ms, ms] = obuf[ms, ms] + extra
-        outs[m].start()
+    for k, (lo, hi) in enumerate(spans):
+        for c in copies[k]:
+            c.wait()
+        for m in range(tiles):
+            ms = pl.ds(m * tile, tile)
+            lefts[m * len(spans) + k].wait()
+            part = jnp.dot(
+                lbuf[ms, lo:hi], rbuf[lo:hi, :], preferred_element_type=jnp.float32
+            )
+            if k:
+                part = part + tbuf[ms, :]
+            if k < len(spans) - 1:
+                tbuf[ms, :] = part
+                continue
+            if has_acc:
+                accs[m].wait()
+                part = part + abuf[ms, :].astype(jnp.float32)
+            obuf[ms, :] = part.astype(obuf.dtype)
+            if has_diag:
+                row = lax.broadcasted_iota(jnp.int32, (tile, tile), 0)
+                col = lax.broadcasted_iota(jnp.int32, (tile, tile), 1)
+                extra = jnp.where(row == col, diag_ref[:, ms], 0.0)
+                obuf[ms, ms] = obuf[ms, ms] + extra
+            outs[m].start()
     for c in outs:
         c.wait()
 
@@ -179,33 +191,37 @@
     n = left.shape[1] // 16
     first = min(slot[0] for slot in slots)
     depth = n * (1 + max(slot[0] for slot in slots) - first)
+    cuts = [0, 6 * n, depth] if depth > 6 * n else [0, depth]
     used = sorted({slot[2] for slot in slots})
     slots = [(s, o, used.index(p), r, k) for s, o, p, r, k in slots]
     pieces = [pieces[p] for p in used]
     has_acc, has_diag = acc is not None, diag is not None
+    kind = jnp.float32 if has_diag else jnp.bfloat16
     tiles = width // min(256, width)
     anywhere = pl.BlockSpec(memory_space=pl.ANY)
     operands = [left, *pieces]
-    far = pl.BlockSpec(memory_space=pltpu.HBM)
-    in_specs = [far] + [anywhere] * len(pieces)
+    in_specs = [anywhere] * len(operands)
     if has_acc:
         operands.append(acc)
-        in_specs.append(far)
+        in_specs.append(anywhere)
     if has_diag:
         operands.append(diag)
         in_specs.append(pl.BlockSpec(memory_space=pltpu.VMEM))
-    sems = [pltpu.SemaphoreType.DMA((k,)) for k in [tiles, len(slots)]]
-    sems += [pltpu.SemaphoreType.DMA((tiles,))] * 2
+    sems = [tiles * (len(cuts) - 1), len(slots), tiles, tiles]
     return pl.pallas_call(
-        lambda *refs: gram_kernel(slots, first, n, len(pieces), has_acc, has_diag, *refs),
-        out_shape=jax.ShapeDtypeStruct((width, width), jnp.float32),
+        lambda *refs: gram_kernel(
+            slots, first, n, len(pieces), cuts, has_acc, has_diag, *refs
+        ),
+        out_shape=jax.ShapeDtypeStruct((width, width), kind),
         in_specs=in_specs,
-        out_specs=far,
+        out_specs=anywhere,
         scratch_shapes=[
             pltpu.VMEM((width, depth), jnp.bfloat16),
             pltpu.VMEM((depth, width), jnp.bfloat16),
-            pltpu.VMEM((width, width), jnp.float32),
-            *sems,
+            pltpu.VMEM((width if len(cuts) > 2 else 8, width), jnp.float32),
+            pltpu.VMEM((width if has_acc else 16, width), jnp.bfloat16),
+            pltpu.VMEM((width, width), kind),
+            *[pltpu.SemaphoreType.DMA((k,)) for k in sems],
         ],
         compiler_params=pltpu.CompilerParams(vmem_limit_bytes=60 * 2**20),
         cost_estimate=pl.CostEstimate(flops=1, bytes_accessed=1, transcendentals=0),
@@ -265,6 +281,10 @@
     up1, down1, mine_y, left2, right2, facts = together(
         up1, down1, mine_y, left2, right2, facts
     )
+    chance = jax.nn.sigmoid(facts[:, :1])
+    weight = (chance * (1.0 - chance)).astype(jnp.bfloat16).astype(jnp.float32)
+    residual = (facts[:, 1:] - chance).astype(jnp.bfloat16)
+    diag = jnp.where(row_index == feat_index, prior_prec, 0.0)[None, :]
     put(mine, (0, 0, 0, n))
     put(mine_y, (1, 0, 0, n))
 
@@ -273,9 +293,10 @@
     down2 = shift(jnp.concatenate([down1, other_a]), "z", -1)
     swapped1 = swap(jnp.concatenate([up1[a:], down1[a:]]), "yl")
     twice_own, twice_far = shift(left1, "x", 1), shift(right2, "x", -1)
-    up2, down2, swapped1, twice_own, twice_far = together(
-        up2, down2, swapped1, twice_own, twice_far
-    )
+    up2, down2, swapped1, twice_own, twice_far, *small = together(
+        up2, down2, swapped1, twice_own, twice_far, weight, residual, diag, slot, row
+    )
+    weight, residual, diag, slot, row = small
     put(up1, (2, 0, 0, n))
     put(down1, (4, 0, 0, n))
     put(swapped1, (3, a, 0, b), (5, a, b, b))
@@ -285,9 +306,6 @@
     same = [features, right1, left1, across, right2, left2, twice_own, twice_far]
     same = jnp.stack(same)
     other = swap(same, "c")
-    chance = jax.nn.sigmoid(facts[:, :1])
-    weight = (chance * (1.0 - chance)).astype(jnp.bfloat16).astype(jnp.float32)
-    residual = (facts[:, 1:] - chance).astype(jnp.bfloat16)
     left, gradient = prepare(
         slot, row, same, other, weight, residual, prior_prec[None], posterior[None]
     )
@@ -316,7 +334,6 @@
     put(up5, (15, 0, 0, a))
     put(swapped4, (15, a, 0, b))
 
-    diag = jnp.where(row_index == feat_index, prior_prec, 0.0)[None, :]
     last = [slot for slot in slots if slot[0] >= 14]
     hessian = gram(left, last, pieces, acc, diag)
     return (hessian, gradient[0])

time: 117 us -> 116 us (level)
  Pallas kernels: 30.3 us -> 28.3 us
  local copies, waits for them, and re-layouts: 14.1 us -> 15.8 us
    pallas_call x3, Pallas kernels: 22 us -> 20.1 us  [gram(): pl.pallas_call(lambda *refs: gram_kernel(slots, first, n, len(pieces), cu...]
    unnamed x44, local copies, waits for them, and re-layouts: 10.1 us -> 11.7 us
  transfers between devices with their start and end apart: 27 -> 27, of which waited for: 10 -> 11; matrix products, arithmetic and copies ran while one was open for 12% -> 14% of each run, Pallas kernels for 21% -> 20%
where the time goes in v4:
time: 116 us; the launch traced here: 115 us
  starting transfers between devices  47.8 us (41%)
  Pallas kernels  28.3 us (24%)
  waiting for transfers between devices  17.6 us (15%)
  local copies, waits for them, and re-layouts  15.8 us (14%)
  other arithmetic  2.7 us (2%)
  matrix products  1.19 us (1%)
    ppermute x25, starting transfers between devices, permuted(): return lax.ppermute(x, ('rows', 'feat'), pairs)  34.4 us
    pallas_call x3, Pallas kernels, gram(): pl.pallas_call(lambda *refs: gram_kernel(slots, first, n, len(pieces), cu...  20.1 us
    all_to_all x2, starting transfers between devices, from_all(): return lax.all_to_all(copies, axis, split_axis=0, concat_axis=0, tiled=True)  13.4 us
    ppermute x25, waiting for transfers between devices, permuted(): return lax.ppermute(x, ('rows', 'feat'), pairs)  12.3 us
    unnamed x44, local copies, waits for them, and re-layouts  11.7 us
    pallas_call x1, Pallas kernels, prepare(): pl.pallas_call(prepare_kernel, in_specs=[smem, smem] + [anywhere] * 2 + [...  8.27 us
    all_to_all x2, waiting for transfers between devices, from_all(): return lax.all_to_all(copies, axis, split_axis=0, concat_axis=0, tiled=True)  5.32 us
  transfers between devices with their start and end apart: 27, of which 11 were waited for; matrix products, arithmetic and copies ran while one was open for 14% of the time, Pallas kernels for 20%

profile of v4, /device:TPU:64, one launch (start us, length us, event | category | flops | bytes accessed | tf_op | source)
XLA Modules:
  0.0 114.6 jit_solution(5707594082125558902)
XLA Ops:
  0.6 3.3 %collective-permute-start = (bf16[192,1024]{1,0:T(8,128)(2,1)}, bf16[192,1024]{1,0:T(8,128)(2,1)S(1)}, u32[]{:S(2)}, u32[]{:S(2)}) collective-permute-start(bf16[192,1024]{1,0:T(8,128)(2,1)} %param.4), channel_id=1, source_target_pairs={{0,128},{1,129},{2,130},{3,131},{4,132},{5,133},{6,134},{7,135},{8... | collective-permute-start | bytes 1179656 | tf_op jit(solution)/shard_map/ppermute | solution.py:22
  3.9 1.5 %collective-permute-start.1 = (bf16[192,1024]{1,0:T(8,128)(2,1)}, bf16[192,1024]{1,0:T(8,128)(2,1)S(1)}, u32[]{:S(2)}, u32[]{:S(2)}) collective-permute-start(bf16[192,1024]{1,0:T(8,128)(2,1)} %param.4), channel_id=1, source_target_pairs={{0,32},{1,33},{2,34},{3,35},{4,36},{5,37},{6,38},{7,39},{8,40},{9,... | collective-permute-start | bytes 1179656 | tf_op jit(solution)/shard_map/ppermute | solution.py:22
  5.4 1.7 %collective-permute-start.2 = (bf16[192,1024]{1,0:T(8,128)(2,1)}, bf16[192,1024]{1,0:T(8,128)(2,1)S(1)}, u32[]{:S(2)}, u32[]{:S(2)}) collective-permute-start(bf16[192,1024]{1,0:T(8,128)(2,1)} %param.4), channel_id=1, source_target_pairs={{0,96},{1,97},{2,98},{3,99},{4,100},{5,101},{6,102},{7,103},{8,104... | collective-permute-start | bytes 1179656 | tf_op jit(solution)/shard_map/ppermute | solution.py:22
  7.1 2.2 %collective-permute-start.3 = (bf16[192,1024]{1,0:T(8,128)(2,1)}, bf16[192,1024]{1,0:T(8,128)(2,1)S(1)}, u32[]{:S(2)}, u32[]{:S(2)}) collective-permute-start(bf16[192,1024]{1,0:T(8,128)(2,1)} %param.4), channel_id=1, source_target_pairs={{0,0},{1,17},{2,34},{3,51},{4,68},{5,85},{6,102},{7,119},{8,128},{... | collective-permute-start | bytes 1179656 | tf_op jit(solution)/shard_map/ppermute | solution.py:22
  11.8 9.7 %all-to-all-start = ((f32[16,1,192]{2,1,0:T(1,128)}), f32[16,1,192]{2,1,0:T(1,128)S(1)}, u32[]{:S(2)}, u32[]{:S(2)}) async-start(f32[16,1,192]{2,1,0:T(1,128)} %broadcast_in_dim.19), calls=%async_computation | async-start | bytes 32768 | tf_op jit(solution)/shard_map/all_to_all | solution.py:41
  22.1 1.8 %bitcast_dynamic-update-slice_fusion.7 = bf16[8,192,1024]{2,1,0:T(8,128)(2,1)} fusion(bf16[192,1024]{1,0:T(8,128)(2,1)} %param.4), kind=kLoop, calls=%fused_computation.10 | loop fusion | bytes 786432
  25.8 2.0 %all-to-all-done = f32[16,1,192]{2,1,0:T(1,128)S(1)} async-done(((f32[16,1,192]{2,1,0:T(1,128)}), f32[16,1,192]{2,1,0:T(1,128)S(1)}, u32[]{:S(2)}, u32[]{:S(2)}) %all-to-all-start) | async-done | bytes 12320 | tf_op jit(solution)/shard_map/all_to_all | solution.py:41
  31.1 2.7 %collective-permute-start.8 = (bf16[192,1024]{1,0:T(8,128)(2,1)S(1)}, bf16[192,1024]{1,0:T(8,128)(2,1)}, u32[]{:S(2)}, u32[]{:S(2)}) collective-permute-start(bf16[192,1024]{1,0:T(8,128)(2,1)S(1)} %collective-permute-done), channel_id=1, source_target_pairs={{0,96},{1,97},{2,98},{3,99},{4,100},{5,101},{6,102},{7,103},{8,104... | collective-permute-start | bytes 1179656 | tf_op jit(solution)/shard_map/ppermute | solution.py:22
  34.5 3.8 %all-to-all-start.1 = ((f32[16,2,192]{2,1,0:T(2,128)}), f32[16,2,192]{2,1,0:T(2,128)S(1)}, u32[]{:S(2)}, u32[]{:S(2)}) async-start(f32[16,2,192]{2,1,0:T(2,128)} %broadcast_in_dim.20), calls=%async_computation.1 | async-start | bytes 65536 | tf_op jit(solution)/shard_map/all_to_all | solution.py:41
  40.6 1.9 %collective-permute-start.12 = (bf16[192,1024]{1,0:T(8,128)(2,1)S(1)}, bf16[192,1024]{1,0:T(8,128)(2,1)}, u32[]{:S(2)}, u32[]{:S(2)}) collective-permute-start(bf16[192,1024]{1,0:T(8,128)(2,1)S(1)} %collective-permute-done.1), channel_id=1, source_target_pairs={{0,32},{1,33},{2,34},{3,35},{4,36},{5,37},{6,38},{7,39},{8,40},{9,... | collective-permute-start | bytes 1179656 | tf_op jit(solution)/shard_map/ppermute | solution.py:22
  42.5 3.4 %all-to-all-done.1 = f32[16,2,192]{2,1,0:T(2,128)S(1)} async-done(((f32[16,2,192]{2,1,0:T(2,128)}), f32[16,2,192]{2,1,0:T(2,128)S(1)}, u32[]{:S(2)}, u32[]{:S(2)}) %all-to-all-start.1) | async-done | bytes 24608 | tf_op jit(solution)/shard_map/all_to_all | solution.py:41
  46.1 1.5 %collective-permute-start.10 = (bf16[272,1024]{1,0:T(8,128)(2,1)S(1)}, bf16[272,1024]{1,0:T(8,128)(2,1)S(1)}, u32[]{:S(2)}, u32[]{:S(2)}) collective-permute-start(bf16[272,1024]{1,0:T(8,128)(2,1)S(1)} %get-tuple-element.70), channel_id=1, source_target_pairs={{0,7},{1,0},{2,1},{3,2},{4,3},{5,4},{6,5},{7,6},{8,15},{9,8},{10,9... | collective-permute-start | bytes 1671176 | tf_op jit(solution)/shard_map/ppermute | solution.py:22
  50.6 1.8 %bitcast_dynamic-update-slice_fusion.3 = bf16[8,192,1024]{2,1,0:T(8,128)(2,1)} fusion(bf16[8,192,1024]{2,1,0:T(8,128)(2,1)} %bitcast_dynamic-update-slice_fusion.4, bf16[192,1024]{1,0:T(8,128)(2,1)} %collective-permute-done.8), kind=kLoop, calls=%fused_computation.6 | loop fusion | bytes 786432
  53.7 1.8 %bitcast_dynamic-update-slice_fusion.2 = bf16[8,192,1024]{2,1,0:T(8,128)(2,1)} fusion(bf16[8,192,1024]{2,1,0:T(8,128)(2,1)} %bitcast_dynamic-update-slice_fusion.3, bf16[192,1024]{1,0:T(8,128)(2,1)} %collective-permute-done.7), kind=kLoop, calls=%fused_computation.5 | loop fusion | bytes 786432
  55.4 4.5 %collective-permute-done.13 = bf16[192,1024]{1,0:T(8,128)(2,1)S(1)} collective-permute-done((bf16[192,1024]{1,0:T(8,128)(2,1)}, bf16[192,1024]{1,0:T(8,128)(2,1)S(1)}, u32[]{:S(2)}, u32[]{:S(2)}) %collective-permute-start.13) | collective-permute-done | bytes 393248 | tf_op jit(solution)/shard_map/ppermute | solution.py:22
  60.8 2.1 %collective-permute-done.9.refs_6_ = bf16[272,1024]{1,0:T(8,128)(2,1)S(1)} collective-permute-done((bf16[272,1024]{1,0:T(8,128)(2,1)S(1)}, bf16[272,1024]{1,0:T(8,128)(2,1)S(1)}, u32[]{:S(2)}, u32[]{:S(2)}) %collective-permute-start.9) | collective-permute-done | bytes 557088 | tf_op jit(solution)/shard_map/ppermute | solution.py:22
  62.9 2.0 %bitcast_dynamic-update-slice_fusion.1 = bf16[8,192,1024]{2,1,0:T(8,128)(2,1)} fusion(bf16[8,192,1024]{2,1,0:T(8,128)(2,1)} %bitcast_dynamic-update-slice_fusion.2, bf16[192,1024]{1,0:T(8,128)(2,1)} %collective-permute-done.12), kind=kLoop, calls=%fused_computation.4 | loop fusion | bytes 786432
  71.7 8.3 %prepare.1 = (bf16[1024,3072]{1,0:T(8,128)(2,1)}, f32[1,1024]{1,0:T(1,128)}) custom-call(s32[16]{0:T(128)} %stack.157.slot_ref, s32[16]{0:T(128)} %stack.174.row_ref, bf16[8,192,1024]{2,1,0:T(8,128)(2,1)} %bitcast_dynamic-update-slice_fusion.refs_0_, bf16[8,192,1024]{2,1,0:T(8,128)(2,1)} %collective-permute-done.18.refs_1_, f32[16,1,192]{2,1,0:T(1,128)} %fusion.1.refs_2_, ...), custom_call_target="tpu_custom_call" | custom-call | flops 1 | bytes 1 | tf_op jit(solution)/shard_map/prepare/pallas_call | solution.py:95
  80.7 1.7 %collective-permute-done.15.refs_11_.refs_2_ = bf16[272,1024]{1,0:T(8,128)(2,1)S(1)} collective-permute-done((bf16[272,1024]{1,0:T(8,128)(2,1)S(1)}, bf16[272,1024]{1,0:T(8,128)(2,1)S(1)}, u32[]{:S(2)}, u32[]{:S(2)}) %collective-permute-start.15) | collective-permute-done | bytes 557088 | tf_op jit(solution)/shard_map/ppermute | solution.py:22
  83.6 2.0 %collective-permute-start.19 = (bf16[160,1024]{1,0:T(8,128)(2,1)S(1)}, bf16[160,1024]{1,0:T(8,128)(2,1)S(1)}, u32[]{:S(2)}, u32[]{:S(2)}) collective-permute-start(bf16[160,1024]{1,0:T(8,128)(2,1)S(1)} %slice.51), channel_id=1, source_target_pairs={{0,1},{1,2},{2,3},{3,4},{4,5},{5,6},{6,7},{7,0},{8,9},{9,10},{10,1... | collective-permute-start | bytes 983048 | tf_op jit(solution)/shard_map/ppermute | solution.py:22
  87.7 8.3 %gram.3.refs_7_ = bf16[1024,1024]{1,0:T(8,128)(2,1)} custom-call(bf16[1024,3072]{1,0:T(8,128)(2,1)} %get-tuple-element.55.refs_0_, bf16[192,1024]{1,0:T(8,128)(2,1)} %copy-done.10, bf16[192,1024]{1,0:T(8,128)(2,1)} %copy-done.8, bf16[192,1024]{1,0:T(8,128)(2,1)} %copy-done.5, bf16[192,1024]{1,0:T(8,128)(2,1)} %copy-done.3, bf16[224,1024]{1,0:T(8,128)(2,1)} %copy-done.9, ...), custom_call_target="tpu_custom_call" | custom-call | flops 1 | bytes 1 | tf_op jit(solution)/shard_map/gram/pallas_call | solution.py:211
  98.2 3.0 %collective-permute-start.23 = (bf16[80,1024]{1,0:T(8,128)(2,1)S(1)}, bf16[80,1024]{1,0:T(8,128)(2,1)S(1)}, u32[]{:S(2)}, u32[]{:S(2)}) collective-permute-start(bf16[80,1024]{1,0:T(8,128)(2,1)S(1)} %slice.55), channel_id=1, source_target_pairs={{0,1},{1,2},{2,3},{3,4},{4,5},{5,6},{6,7},{7,0},{8,9},{9,10},{10,1... | collective-permute-start | bytes 491528 | tf_op jit(solution)/shard_map/ppermute | solution.py:22
  101.3 6.1 %gram.4.refs_5_ = bf16[1024,1024]{1,0:T(8,128)(2,1)} custom-call(bf16[1024,3072]{1,0:T(8,128)(2,1)} %get-tuple-element.55.refs_0_, bf16[272,1024]{1,0:T(8,128)(2,1)} %copy-done.1, bf16[272,1024]{1,0:T(8,128)(2,1)} %copy-done, bf16[112,1024]{1,0:T(8,128)(2,1)} %copy-done.13, bf16[112,1024]{1,0:T(8,128)(2,1)} %copy-done.14, bf16[160,1024]{1,0:T(8,128)(2,1)} %copy-done.4, ...), custom_call_target="tpu_custom_call" | custom-call | flops 1 | bytes 1 | tf_op jit(solution)/shard_map/gram/pallas_call | solution.py:211
  108.8 5.6 %gram.5 = f32[1024,1024]{1,0:T(8,128)} custom-call(bf16[1024,3072]{1,0:T(8,128)(2,1)} %get-tuple-element.55.refs_0_, bf16[160,1024]{1,0:T(8,128)(2,1)} %copy-done.4, bf16[192,1024]{1,0:T(8,128)(2,1)} %copy-done.2, bf16[80,1024]{1,0:T(8,128)(2,1)} %copy-done.16, bf16[112,1024]{1,0:T(8,128)(2,1)} %copy-done.15, bf16[1024,1024]{1,0:T(8,128)(2,1)} %gram.4.refs_5_, ...), custom_call_target="tpu_custom_call" | custom-call | flops 1 | bytes 1 | tf_op jit(solution)/shard_map/gram/pallas_call | solution.py:211
  (105 shorter events, 31.0 us)
Async XLA Ops:
  0.6 27.2 %collective-permute-start = (bf16[192,1024]{1,0:T(8,128)(2,1)}, bf16[192,1024]{1,0:T(8,128)(2,1)S(1)}, u32[]{:S(2)}, u32[]{:S(2)}) collective-permute-start(bf16[192,1024]{1,0:T(8,128)(2,1)} %param.4), channel_id=1, source_target_pairs={{0,128},{1,129},{2,130},{3,131},{4,132},{5,133},{6,134},{7,135},{8... | collective-permute-start | bytes 1179656 | tf_op jit(solution)/shard_map/ppermute | solution.py:22
  3.9 23.9 %collective-permute-start.1 = (bf16[192,1024]{1,0:T(8,128)(2,1)}, bf16[192,1024]{1,0:T(8,128)(2,1)S(1)}, u32[]{:S(2)}, u32[]{:S(2)}) collective-permute-start(bf16[192,1024]{1,0:T(8,128)(2,1)} %param.4), channel_id=1, source_target_pairs={{0,32},{1,33},{2,34},{3,35},{4,36},{5,37},{6,38},{7,39},{8,40},{9,... | collective-permute-start | bytes 1179656 | tf_op jit(solution)/shard_map/ppermute | solution.py:22
  5.4 22.4 %collective-permute-start.2 = (bf16[192,1024]{1,0:T(8,128)(2,1)}, bf16[192,1024]{1,0:T(8,128)(2,1)S(1)}, u32[]{:S(2)}, u32[]{:S(2)}) collective-permute-start(bf16[192,1024]{1,0:T(8,128)(2,1)} %param.4), channel_id=1, source_target_pairs={{0,96},{1,97},{2,98},{3,99},{4,100},{5,101},{6,102},{7,103},{8,104... | collective-permute-start | bytes 1179656 | tf_op jit(solution)/shard_map/ppermute | solution.py:22
  7.1 20.7 %collective-permute-start.3 = (bf16[192,1024]{1,0:T(8,128)(2,1)}, bf16[192,1024]{1,0:T(8,128)(2,1)S(1)}, u32[]{:S(2)}, u32[]{:S(2)}) collective-permute-start(bf16[192,1024]{1,0:T(8,128)(2,1)} %param.4), channel_id=1, source_target_pairs={{0,0},{1,17},{2,34},{3,51},{4,68},{5,85},{6,102},{7,119},{8,128},{... | collective-permute-start | bytes 1179656 | tf_op jit(solution)/shard_map/ppermute | solution.py:22
  11.8 16.0 %all-to-all-start = ((f32[16,1,192]{2,1,0:T(1,128)}), f32[16,1,192]{2,1,0:T(1,128)S(1)}, u32[]{:S(2)}, u32[]{:S(2)}) async-start(f32[16,1,192]{2,1,0:T(1,128)} %broadcast_in_dim.19), calls=%async_computation | async-start | bytes 32768 | tf_op jit(solution)/shard_map/all_to_all | solution.py:41
  27.9 12.7 %collective-permute-start.4 = (bf16[192,1024]{1,0:T(8,128)(2,1)S(1)}, bf16[192,1024]{1,0:T(8,128)(2,1)S(1)}, u32[]{:S(2)}, u32[]{:S(2)}) collective-permute-start(bf16[192,1024]{1,0:T(8,128)(2,1)S(1)} %collective-permute-done.3.refs_1_), channel_id=1, source_target_pairs={{0,1},{1,2},{2,3},{3,4},{4,5},{5,6},{6,7},{7,0},{8,9},{9,10},{10,1... | collective-permute-start | bytes 1179656 | tf_op jit(solution)/shard_map/ppermute | solution.py:22
  28.6 17.2 %collective-permute-start.5 = (bf16[192,1024]{1,0:T(8,128)(2,1)S(1)}, bf16[192,1024]{1,0:T(8,128)(2,1)S(1)}, u32[]{:S(2)}, u32[]{:S(2)}) collective-permute-start(bf16[192,1024]{1,0:T(8,128)(2,1)S(1)} %collective-permute-done.3.refs_1_), channel_id=1, source_target_pairs={{0,7},{1,0},{2,1},{3,2},{4,3},{5,4},{6,5},{7,6},{8,15},{9,8},{10,9... | collective-permute-start | bytes 1179656 | tf_op jit(solution)/shard_map/ppermute | solution.py:22
  30.0 15.9 %collective-permute-start.6 = (bf16[192,1024]{1,0:T(8,128)(2,1)S(1)}, bf16[192,1024]{1,0:T(8,128)(2,1)S(1)}, u32[]{:S(2)}, u32[]{:S(2)}) collective-permute-start(bf16[192,1024]{1,0:T(8,128)(2,1)S(1)} %collective-permute-done.3.refs_1_), channel_id=1, source_target_pairs={{0,8},{1,9},{2,10},{3,11},{4,12},{5,13},{6,14},{7,15},{8,0},{9,1},... | collective-permute-start | bytes 1179656 | tf_op jit(solution)/shard_map/ppermute | solution.py:22
  30.6 15.3 %collective-permute-start.7 = (bf16[192,1024]{1,0:T(8,128)(2,1)S(1)}, bf16[192,1024]{1,0:T(8,128)(2,1)}, u32[]{:S(2)}, u32[]{:S(2)}) collective-permute-start(bf16[192,1024]{1,0:T(8,128)(2,1)S(1)} %collective-permute-done), channel_id=1, source_target_pairs={{0,32},{1,33},{2,34},{3,35},{4,36},{5,37},{6,38},{7,39},{8,40},{9,... | collective-permute-start | bytes 1179656 | tf_op jit(solution)/shard_map/ppermute | solution.py:22
  31.1 14.8 %collective-permute-start.8 = (bf16[192,1024]{1,0:T(8,128)(2,1)S(1)}, bf16[192,1024]{1,0:T(8,128)(2,1)}, u32[]{:S(2)}, u32[]{:S(2)}) collective-permute-start(bf16[192,1024]{1,0:T(8,128)(2,1)S(1)} %collective-permute-done), channel_id=1, source_target_pairs={{0,96},{1,97},{2,98},{3,99},{4,100},{5,101},{6,102},{7,103},{8,104... | collective-permute-start | bytes 1179656 | tf_op jit(solution)/shard_map/ppermute | solution.py:22
  34.5 11.4 %all-to-all-start.1 = ((f32[16,2,192]{2,1,0:T(2,128)}), f32[16,2,192]{2,1,0:T(2,128)S(1)}, u32[]{:S(2)}, u32[]{:S(2)}) async-start(f32[16,2,192]{2,1,0:T(2,128)} %broadcast_in_dim.20), calls=%async_computation.1 | async-start | bytes 65536 | tf_op jit(solution)/shard_map/all_to_all | solution.py:41
  40.6 14.8 %collective-permute-start.12 = (bf16[192,1024]{1,0:T(8,128)(2,1)S(1)}, bf16[192,1024]{1,0:T(8,128)(2,1)}, u32[]{:S(2)}, u32[]{:S(2)}) collective-permute-start(bf16[192,1024]{1,0:T(8,128)(2,1)S(1)} %collective-permute-done.1), channel_id=1, source_target_pairs={{0,32},{1,33},{2,34},{3,35},{4,36},{5,37},{6,38},{7,39},{8,40},{9,... | collective-permute-start | bytes 1179656 | tf_op jit(solution)/shard_map/ppermute | solution.py:22
  46.1 14.7 %collective-permute-start.10 = (bf16[272,1024]{1,0:T(8,128)(2,1)S(1)}, bf16[272,1024]{1,0:T(8,128)(2,1)S(1)}, u32[]{:S(2)}, u32[]{:S(2)}) collective-permute-start(bf16[272,1024]{1,0:T(8,128)(2,1)S(1)} %get-tuple-element.70), channel_id=1, source_target_pairs={{0,7},{1,0},{2,1},{3,2},{4,3},{5,4},{6,5},{7,6},{8,15},{9,8},{10,9... | collective-permute-start | bytes 1671176 | tf_op jit(solution)/shard_map/ppermute | solution.py:22
  47.6 15.3 %collective-permute-start.9 = (bf16[272,1024]{1,0:T(8,128)(2,1)S(1)}, bf16[272,1024]{1,0:T(8,128)(2,1)S(1)}, u32[]{:S(2)}, u32[]{:S(2)}) collective-permute-start(bf16[272,1024]{1,0:T(8,128)(2,1)S(1)} %get-tuple-element.71), channel_id=1, source_target_pairs={{0,1},{1,2},{2,3},{3,4},{4,5},{5,6},{6,7},{7,0},{8,9},{9,10},{10,1... | collective-permute-start | bytes 1671176 | tf_op jit(solution)/shard_map/ppermute | solution.py:22
  48.2 12.1 %collective-permute-start.11 = (bf16[224,1024]{1,0:T(8,128)(2,1)S(1)}, bf16[224,1024]{1,0:T(8,128)(2,1)S(1)}, u32[]{:S(2)}, u32[]{:S(2)}) collective-permute-start(bf16[224,1024]{1,0:T(8,128)(2,1)S(1)} %pad_maximum_fusion.2), channel_id=1, source_target_pairs={{0,8},{1,9},{2,10},{3,11},{4,12},{5,13},{6,14},{7,15},{8,0},{9,1},... | collective-permute-start | bytes 1376264 | tf_op jit(solution)/shard_map/ppermute | solution.py:22
  49.4 10.5 %collective-permute-start.13 = (bf16[192,1024]{1,0:T(8,128)(2,1)}, bf16[192,1024]{1,0:T(8,128)(2,1)S(1)}, u32[]{:S(2)}, u32[]{:S(2)}) collective-permute-start(bf16[192,1024]{1,0:T(8,128)(2,1)} %collective-permute-done.8), channel_id=1, source_target_pairs={{0,96},{1,97},{2,98},{3,99},{4,100},{5,101},{6,102},{7,103},{8,104... | collective-permute-start | bytes 1179656 | tf_op jit(solution)/shard_map/ppermute | solution.py:22
  65.7 15.0 %collective-permute-start.14 = (bf16[272,1024]{1,0:T(8,128)(2,1)S(1)}, bf16[272,1024]{1,0:T(8,128)(2,1)S(1)}, u32[]{:S(2)}, u32[]{:S(2)}) collective-permute-start(bf16[272,1024]{1,0:T(8,128)(2,1)S(1)} %collective-permute-done.9.refs_6_), channel_id=1, source_target_pairs={{0,1},{1,2},{2,3},{3,4},{4,5},{5,6},{6,7},{7,0},{8,9},{9,10},{10,1... | collective-permute-start | bytes 1671176 | tf_op jit(solution)/shard_map/ppermute | solution.py:22
  66.4 15.9 %collective-permute-start.15 = (bf16[272,1024]{1,0:T(8,128)(2,1)S(1)}, bf16[272,1024]{1,0:T(8,128)(2,1)S(1)}, u32[]{:S(2)}, u32[]{:S(2)}) collective-permute-start(bf16[272,1024]{1,0:T(8,128)(2,1)S(1)} %collective-permute-done.10.refs_7_), channel_id=1, source_target_pairs={{0,7},{1,0},{2,1},{3,2},{4,3},{5,4},{6,5},{7,6},{8,15},{9,8},{10,9... | collective-permute-start | bytes 1671176 | tf_op jit(solution)/shard_map/ppermute | solution.py:22
  67.7 12.2 %collective-permute-start.16 = (bf16[112,1024]{1,0:T(8,128)(2,1)S(1)}, bf16[112,1024]{1,0:T(8,128)(2,1)S(1)}, u32[]{:S(2)}, u32[]{:S(2)}) collective-permute-start(bf16[112,1024]{1,0:T(8,128)(2,1)S(1)} %slice.49), channel_id=1, source_target_pairs={{0,8},{1,9},{2,10},{3,11},{4,12},{5,13},{6,14},{7,15},{8,0},{9,1},... | collective-permute-start | bytes 688136 | tf_op jit(solution)/shard_map/ppermute | solution.py:22
  69.1 11.1 %collective-permute-start.17 = (bf16[112,1024]{1,0:T(8,128)(2,1)S(1)}, bf16[112,1024]{1,0:T(8,128)(2,1)S(1)}, u32[]{:S(2)}, u32[]{:S(2)}) collective-permute-start(bf16[112,1024]{1,0:T(8,128)(2,1)S(1)} %slice.50), channel_id=1, source_target_pairs={{0,8},{1,9},{2,10},{3,11},{4,12},{5,13},{6,14},{7,15},{8,0},{9,1},... | collective-permute-start | bytes 688136 | tf_op jit(solution)/shard_map/ppermute | solution.py:22
  82.4 14.8 %collective-permute-start.20 = (bf16[192,1024]{1,0:T(8,128)(2,1)S(1)}, bf16[192,1024]{1,0:T(8,128)(2,1)S(1)}, u32[]{:S(2)}, u32[]{:S(2)}) collective-permute-start(bf16[192,1024]{1,0:T(8,128)(2,1)S(1)} %slice.52), channel_id=1, source_target_pairs={{0,7},{1,0},{2,1},{3,2},{4,3},{5,4},{6,5},{7,6},{8,15},{9,8},{10,9... | collective-permute-start | bytes 1179656 | tf_op jit(solution)/shard_map/ppermute | solution.py:22
  83.6 13.7 %collective-permute-start.19 = (bf16[160,1024]{1,0:T(8,128)(2,1)S(1)}, bf16[160,1024]{1,0:T(8,128)(2,1)S(1)}, u32[]{:S(2)}, u32[]{:S(2)}) collective-permute-start(bf16[160,1024]{1,0:T(8,128)(2,1)S(1)} %slice.51), channel_id=1, source_target_pairs={{0,1},{1,2},{2,3},{3,4},{4,5},{5,6},{6,7},{7,0},{8,9},{9,10},{10,1... | collective-permute-start | bytes 983048 | tf_op jit(solution)/shard_map/ppermute | solution.py:22
  85.6 10.4 %collective-permute-start.21 = (bf16[112,1024]{1,0:T(8,128)(2,1)S(1)}, bf16[112,1024]{1,0:T(8,128)(2,1)S(1)}, u32[]{:S(2)}, u32[]{:S(2)}) collective-permute-start(bf16[112,1024]{1,0:T(8,128)(2,1)S(1)} %slice.53), channel_id=1, source_target_pairs={{0,8},{1,9},{2,10},{3,11},{4,12},{5,13},{6,14},{7,15},{8,0},{9,1},... | collective-permute-start | bytes 688136 | tf_op jit(solution)/shard_map/ppermute | solution.py:22
  86.3 10.9 %collective-permute-start.22 = (bf16[112,1024]{1,0:T(8,128)(2,1)S(1)}, bf16[112,1024]{1,0:T(8,128)(2,1)S(1)}, u32[]{:S(2)}, u32[]{:S(2)}) collective-permute-start(bf16[112,1024]{1,0:T(8,128)(2,1)S(1)} %slice.54), channel_id=1, source_target_pairs={{0,8},{1,9},{2,10},{3,11},{4,12},{5,13},{6,14},{7,15},{8,0},{9,1},... | collective-permute-start | bytes 688136 | tf_op jit(solution)/shard_map/ppermute | solution.py:22
  (21 other events, 219.6 us)

commit v5 on v4

--- a/solution.py
+++ b/solution.py
@@ -278,9 +278,11 @@
     left2, right2 = shift(across, "x", 1), shift(across, "x", -1)
     facts = jnp.stack([margins, labels.astype(jnp.float32)])
     facts = from_all(facts, "rows")
-    up1, down1, mine_y, left2, right2, facts = together(
-        up1, down1, mine_y, left2, right2, facts
-    )
+    held = (features, across, left1, right1, prior_prec)
+    up1, down1, mine_y, left2, right2, facts, *held = together(
+        up1, down1, mine_y, left2, right2, facts, *held
+    )
+    features, across, left1, right1, prior_prec = held
     chance = jax.nn.sigmoid(facts[:, :1])
     weight = (chance * (1.0 - chance)).astype(jnp.bfloat16).astype(jnp.float32)
     residual = (facts[:, 1:] - chance).astype(jnp.bfloat16)

time: 116 us -> 114 us (0.983)
  blocking collectives: 0 us -> 15.8 us
  local copies, waits for them, and re-layouts: 15.8 us -> 8.31 us
  starting transfers between devices: 47.8 us -> 40.7 us
  waiting for transfers between devices: 17.6 us -> 13 us
    all_to_all x0 -> x1, blocking collectives: none -> 15.8 us  [from_all(): return lax.all_to_all(copies, axis, split_axis=0, concat_axis=0, tiled=True)]
    all_to_all x2 -> x1, starting transfers between devices: 13.4 us -> 4.13 us  [from_all(): return lax.all_to_all(copies, axis, split_axis=0, concat_axis=0, tiled=True)]
    unnamed x44 -> x60, local copies, waits for them, and re-layouts: 11.7 us -> 5.5 us
    ppermute x25, waiting for transfers between devices: 12.3 us -> 7.38 us  [permuted(): return lax.ppermute(x, ('rows', 'feat'), pairs)]
    ppermute x25, starting transfers between devices: 34.4 us -> 36.6 us  [permuted(): return lax.ppermute(x, ('rows', 'feat'), pairs)]
    all_to_all x2 -> x1, waiting for transfers between devices: 5.32 us -> 5.58 us  [from_all(): return lax.all_to_all(copies, axis, split_axis=0, concat_axis=0, tiled=True)]
  transfers between devices with their start and end apart: 27 -> 26, of which waited for: 11 -> 5; matrix products, arithmetic and copies ran while one was open for 14% -> 7% of each run, Pallas kernels for 20% -> 20%
where the time goes in v5:
time: 114 us; the launch traced here: 113 us
  starting transfers between devices  40.7 us (36%)
  Pallas kernels  28.4 us (25%)
  blocking collectives  15.8 us (14%)
  waiting for transfers between devices  13 us (11%)
  local copies, waits for them, and re-layouts  8.31 us (7%)
  other arithmetic  3.59 us (3%)
  between operations  2.02 us (2%)
  matrix products  1.19 us (1%)
    ppermute x25, starting transfers between devices, permuted(): return lax.ppermute(x, ('rows', 'feat'), pairs)  36.6 us
    pallas_call x3, Pallas kernels, gram(): pl.pallas_call(lambda *refs: gram_kernel(slots, first, n, len(pieces), cu...  20 us
    all_to_all x1, blocking collectives, from_all(): return lax.all_to_all(copies, axis, split_axis=0, concat_axis=0, tiled=True)  15.8 us
    pallas_call x1, Pallas kernels, prepare(): pl.pallas_call(prepare_kernel, in_specs=[smem, smem] + [anywhere] * 2 + [...  8.44 us
    ppermute x25, waiting for transfers between devices, permuted(): return lax.ppermute(x, ('rows', 'feat'), pairs)  7.38 us
    all_to_all x1, waiting for transfers between devices, from_all(): return lax.all_to_all(copies, axis, split_axis=0, concat_axis=0, tiled=True)  5.58 us
    unnamed x60, local copies, waits for them, and re-layouts  5.5 us
    all_to_all x1, starting transfers between devices, from_all(): return lax.all_to_all(copies, axis, split_axis=0, concat_axis=0, tiled=True)  4.13 us
  transfers between devices with their start and end apart: 26, of which 5 were waited for; matrix products, arithmetic and copies ran while one was open for 7% of the time, Pallas kernels for 20%

profile of v5, /device:TPU:64, one launch (start us, length us, event | category | flops | bytes accessed | tf_op | source)
XLA Modules:
  0.0 113.0 jit_solution(13820984266137302110)
XLA Ops:
  0.6 3.3 %collective-permute-start = (bf16[192,1024]{1,0:T(8,128)(2,1)}, bf16[192,1024]{1,0:T(8,128)(2,1)S(1)}, u32[]{:S(2)}, u32[]{:S(2)}) collective-permute-start(bf16[192,1024]{1,0:T(8,128)(2,1)} %param.4), channel_id=1, source_target_pairs={{0,128},{1,129},{2,130},{3,131},{4,132},{5,133},{6,134},{7,135},{8... | collective-permute-start | bytes 1179656 | tf_op jit(solution)/shard_map/ppermute | solution.py:22
  3.9 1.5 %collective-permute-start.1 = (bf16[192,1024]{1,0:T(8,128)(2,1)}, bf16[192,1024]{1,0:T(8,128)(2,1)S(1)}, u32[]{:S(2)}, u32[]{:S(2)}) collective-permute-start(bf16[192,1024]{1,0:T(8,128)(2,1)} %param.4), channel_id=1, source_target_pairs={{0,32},{1,33},{2,34},{3,35},{4,36},{5,37},{6,38},{7,39},{8,40},{9,... | collective-permute-start | bytes 1179656 | tf_op jit(solution)/shard_map/ppermute | solution.py:22
  5.4 1.7 %collective-permute-start.2 = (bf16[192,1024]{1,0:T(8,128)(2,1)}, bf16[192,1024]{1,0:T(8,128)(2,1)S(1)}, u32[]{:S(2)}, u32[]{:S(2)}) collective-permute-start(bf16[192,1024]{1,0:T(8,128)(2,1)} %param.4), channel_id=1, source_target_pairs={{0,96},{1,97},{2,98},{3,99},{4,100},{5,101},{6,102},{7,103},{8,104... | collective-permute-start | bytes 1179656 | tf_op jit(solution)/shard_map/ppermute | solution.py:22
  7.1 2.2 %collective-permute-start.3 = (bf16[192,1024]{1,0:T(8,128)(2,1)}, bf16[192,1024]{1,0:T(8,128)(2,1)S(1)}, u32[]{:S(2)}, u32[]{:S(2)}) collective-permute-start(bf16[192,1024]{1,0:T(8,128)(2,1)} %param.4), channel_id=1, source_target_pairs={{0,0},{1,17},{2,34},{3,51},{4,68},{5,85},{6,102},{7,119},{8,128},{... | collective-permute-start | bytes 1179656 | tf_op jit(solution)/shard_map/ppermute | solution.py:22
  11.2 15.8 %all_to_all.11 = f32[16,1,192]{2,1,0:T(1,128)S(1)} all-to-all(f32[16,1,192]{2,1,0:T(1,128)S(1)} %broadcast_in_dim.19), channel_id=1, replica_groups=mesh['rows'=16,'feat'=16] {'feat'}, dimensions={0} | all-to-all | bytes 24576 | tf_op jit(solution)/shard_map/all_to_all | solution.py:41
  29.3 1.3 %collective-permute-start.6 = (bf16[192,1024]{1,0:T(8,128)(2,1)S(1)}, bf16[192,1024]{1,0:T(8,128)(2,1)S(1)}, u32[]{:S(2)}, u32[]{:S(2)}) collective-permute-start(bf16[192,1024]{1,0:T(8,128)(2,1)S(1)} %collective-permute-done.3.refs_1_), channel_id=1, source_target_pairs={{0,8},{1,9},{2,10},{3,11},{4,12},{5,13},{6,14},{7,15},{8,0},{9,1},... | collective-permute-start | bytes 1179656 | tf_op jit(solution)/shard_map/ppermute | solution.py:22
  30.6 3.2 %collective-permute-start.8 = (bf16[192,1024]{1,0:T(8,128)(2,1)S(1)}, bf16[192,1024]{1,0:T(8,128)(2,1)S(1)}, u32[]{:S(2)}, u32[]{:S(2)}) collective-permute-start(bf16[192,1024]{1,0:T(8,128)(2,1)S(1)} %collective-permute-done), channel_id=1, source_target_pairs={{0,96},{1,97},{2,98},{3,99},{4,100},{5,101},{6,102},{7,103},{8,104... | collective-permute-start | bytes 1179656 | tf_op jit(solution)/shard_map/ppermute | solution.py:22
  35.2 4.1 %all-to-all-start.1 = ((f32[16,2,192]{2,1,0:T(2,128)}), f32[16,2,192]{2,1,0:T(2,128)}, u32[]{:S(2)}, u32[]{:S(2)}) async-start(f32[16,2,192]{2,1,0:T(2,128)} %broadcast_in_dim.20), calls=%async_computation.1 | async-start | bytes 65536 | tf_op jit(solution)/shard_map/all_to_all | solution.py:41
  41.4 5.6 %all-to-all-done.1 = f32[16,2,192]{2,1,0:T(2,128)} async-done(((f32[16,2,192]{2,1,0:T(2,128)}), f32[16,2,192]{2,1,0:T(2,128)}, u32[]{:S(2)}, u32[]{:S(2)}) %all-to-all-start.1) | async-done | bytes 24608 | tf_op jit(solution)/shard_map/all_to_all | solution.py:41
  50.7 2.7 %collective-permute-start.13 = (bf16[192,1024]{1,0:T(8,128)(2,1)S(1)}, bf16[192,1024]{1,0:T(8,128)(2,1)S(1)}, u32[]{:S(2)}, u32[]{:S(2)}) collective-permute-start(bf16[192,1024]{1,0:T(8,128)(2,1)S(1)} %collective-permute-done.8), channel_id=1, source_target_pairs={{0,96},{1,97},{2,98},{3,99},{4,100},{5,101},{6,102},{7,103},{8,104... | collective-permute-start | bytes 1179656 | tf_op jit(solution)/shard_map/ppermute | solution.py:22
  53.4 1.5 %subtract_convert_fusion = (bf16[16,1,192]{2,1,0:T(2,128)(2,1)}, f32[16,1,192]{2,1,0:T(1,128)S(1)}) fusion(f32[16,2,192]{2,1,0:T(2,128)} %all-to-all-done.1), kind=kLoop, calls=%fused_computation.14 | loop fusion | flops 15360 | bytes 43008 | tf_op jit(solution)/shard_map/convert_element_type | solution.py:288
  56.3 5.3 %collective-permute-done.12 = bf16[192,1024]{1,0:T(8,128)(2,1)S(1)} collective-permute-done((bf16[192,1024]{1,0:T(8,128)(2,1)S(1)}, bf16[192,1024]{1,0:T(8,128)(2,1)S(1)}, u32[]{:S(2)}, u32[]{:S(2)}) %collective-permute-start.12) | collective-permute-done | bytes 393248 | tf_op jit(solution)/shard_map/ppermute | solution.py:22
  62.0 1.6 %collective-permute-done.9.refs_6_ = bf16[272,1024]{1,0:T(8,128)(2,1)S(1)} collective-permute-done((bf16[272,1024]{1,0:T(8,128)(2,1)S(1)}, bf16[272,1024]{1,0:T(8,128)(2,1)S(1)}, u32[]{:S(2)}, u32[]{:S(2)}) %collective-permute-start.9) | collective-permute-done | bytes 557088 | tf_op jit(solution)/shard_map/ppermute | solution.py:22
  63.9 1.4 %copy-done.2 = bf16[8,192,1024]{2,1,0:T(8,128)(2,1)} copy-done((bf16[8,192,1024]{2,1,0:T(8,128)(2,1)}, bf16[8,192,1024]{2,1,0:T(8,128)(2,1)S(1)}, u32[]{:S(2)}) %copy-start.2) | copy-done | bytes 3145752
  65.4 1.9 %collective-permute-start.14 = (bf16[272,1024]{1,0:T(8,128)(2,1)S(1)}, bf16[272,1024]{1,0:T(8,128)(2,1)S(1)}, u32[]{:S(2)}, u32[]{:S(2)}) collective-permute-start(bf16[272,1024]{1,0:T(8,128)(2,1)S(1)} %collective-permute-done.9.refs_6_), channel_id=1, source_target_pairs={{0,1},{1,2},{2,3},{3,4},{4,5},{5,6},{6,7},{7,0},{8,9},{9,10},{10,1... | collective-permute-start | bytes 1671176 | tf_op jit(solution)/shard_map/ppermute | solution.py:22
  70.1 1.7 %copy-done.3 = bf16[8,192,1024]{2,1,0:T(8,128)(2,1)} copy-done((bf16[8,192,1024]{2,1,0:T(8,128)(2,1)}, bf16[8,192,1024]{2,1,0:T(8,128)(2,1)S(1)}, u32[]{:S(2)}) %copy-start.3) | copy-done | bytes 3145752
  71.9 8.4 %prepare.1 = (bf16[1024,3072]{1,0:T(8,128)(2,1)}, f32[1,1024]{1,0:T(1,128)}) custom-call(s32[16]{0:T(128)} %stack.157.slot_ref, s32[16]{0:T(128)} %stack.174.row_ref, bf16[8,192,1024]{2,1,0:T(8,128)(2,1)} %copy-done.2, bf16[8,192,1024]{2,1,0:T(8,128)(2,1)} %copy-done.3, f32[16,1,192]{2,1,0:T(1,128)} %fusion.1.refs_2_, ...), custom_call_target="tpu_custom_call" | custom-call | flops 1 | bytes 1 | tf_op jit(solution)/shard_map/prepare/pallas_call | solution.py:95
  80.5 2.6 %collective-permute-start.20 = (bf16[192,1024]{1,0:T(8,128)(2,1)S(1)}, bf16[192,1024]{1,0:T(8,128)(2,1)S(1)}, u32[]{:S(2)}, u32[]{:S(2)}) collective-permute-start(bf16[192,1024]{1,0:T(8,128)(2,1)S(1)} %slice.52), channel_id=1, source_target_pairs={{0,7},{1,0},{2,1},{3,2},{4,3},{5,4},{6,5},{7,6},{8,15},{9,8},{10,9... | collective-permute-start | bytes 1179656 | tf_op jit(solution)/shard_map/ppermute | solution.py:22
  83.6 2.1 %collective-permute-start.21 = (bf16[112,1024]{1,0:T(8,128)(2,1)S(1)}, bf16[112,1024]{1,0:T(8,128)(2,1)S(1)}, u32[]{:S(2)}, u32[]{:S(2)}) collective-permute-start(bf16[112,1024]{1,0:T(8,128)(2,1)S(1)} %slice.53), channel_id=1, source_target_pairs={{0,8},{1,9},{2,10},{3,11},{4,12},{5,13},{6,14},{7,15},{8,0},{9,1},... | collective-permute-start | bytes 688136 | tf_op jit(solution)/shard_map/ppermute | solution.py:22
  85.8 8.3 %gram.3.refs_7_ = bf16[1024,1024]{1,0:T(8,128)(2,1)} custom-call(bf16[1024,3072]{1,0:T(8,128)(2,1)} %get-tuple-element.65.refs_0_, bf16[192,1024]{1,0:T(8,128)(2,1)} %copy-done.13, bf16[192,1024]{1,0:T(8,128)(2,1)} %copy-done.11, bf16[192,1024]{1,0:T(8,128)(2,1)} %copy-done.7, bf16[192,1024]{1,0:T(8,128)(2,1)} %copy-done.5, bf16[224,1024]{1,0:T(8,128)(2,1)} %copy-done.12, ...), custom_call_target="tpu_custom_call" | custom-call | flops 1 | bytes 1 | tf_op jit(solution)/shard_map/gram/pallas_call | solution.py:211
  94.3 2.1 %collective-permute-start.24 = (bf16[112,1024]{1,0:T(8,128)(2,1)S(1)}, bf16[112,1024]{1,0:T(8,128)(2,1)S(1)}, u32[]{:S(2)}, u32[]{:S(2)}) collective-permute-start(bf16[112,1024]{1,0:T(8,128)(2,1)S(1)} %slice.56), channel_id=1, source_target_pairs={{0,8},{1,9},{2,10},{3,11},{4,12},{5,13},{6,14},{7,15},{8,0},{9,1},... | collective-permute-start | bytes 688136 | tf_op jit(solution)/shard_map/ppermute | solution.py:22
  96.5 3.3 %collective-permute-start.23 = (bf16[80,1024]{1,0:T(8,128)(2,1)S(1)}, bf16[80,1024]{1,0:T(8,128)(2,1)S(1)}, u32[]{:S(2)}, u32[]{:S(2)}) collective-permute-start(bf16[80,1024]{1,0:T(8,128)(2,1)S(1)} %slice.55), channel_id=1, source_target_pairs={{0,1},{1,2},{2,3},{3,4},{4,5},{5,6},{6,7},{7,0},{8,9},{9,10},{10,1... | collective-permute-start | bytes 491528 | tf_op jit(solution)/shard_map/ppermute | solution.py:22
  99.8 6.1 %gram.4.refs_5_ = bf16[1024,1024]{1,0:T(8,128)(2,1)} custom-call(bf16[1024,3072]{1,0:T(8,128)(2,1)} %get-tuple-element.65.refs_0_, bf16[272,1024]{1,0:T(8,128)(2,1)} %copy-done.1, bf16[272,1024]{1,0:T(8,128)(2,1)} %copy-done, bf16[112,1024]{1,0:T(8,128)(2,1)} %copy-done.20, bf16[112,1024]{1,0:T(8,128)(2,1)} %copy-done.21, bf16[160,1024]{1,0:T(8,128)(2,1)} %copy-done.6, ...), custom_call_target="tpu_custom_call" | custom-call | flops 1 | bytes 1 | tf_op jit(solution)/shard_map/gram/pallas_call | solution.py:211
  107.2 5.6 %gram.5 = f32[1024,1024]{1,0:T(8,128)} custom-call(bf16[1024,3072]{1,0:T(8,128)(2,1)} %get-tuple-element.65.refs_0_, bf16[160,1024]{1,0:T(8,128)(2,1)} %copy-done.6, bf16[192,1024]{1,0:T(8,128)(2,1)} %copy-done.4, bf16[80,1024]{1,0:T(8,128)(2,1)} %copy-done.23, bf16[112,1024]{1,0:T(8,128)(2,1)} %copy-done.22, bf16[1024,1024]{1,0:T(8,128)(2,1)} %gram.4.refs_5_, ...), custom_call_target="tpu_custom_call" | custom-call | flops 1 | bytes 1 | tf_op jit(solution)/shard_map/gram/pallas_call | solution.py:211
  (120 shorter events, 17.6 us)
Async XLA Ops:
  0.6 26.5 %collective-permute-start = (bf16[192,1024]{1,0:T(8,128)(2,1)}, bf16[192,1024]{1,0:T(8,128)(2,1)S(1)}, u32[]{:S(2)}, u32[]{:S(2)}) collective-permute-start(bf16[192,1024]{1,0:T(8,128)(2,1)} %param.4), channel_id=1, source_target_pairs={{0,128},{1,129},{2,130},{3,131},{4,132},{5,133},{6,134},{7,135},{8... | collective-permute-start | bytes 1179656 | tf_op jit(solution)/shard_map/ppermute | solution.py:22
  3.9 23.2 %collective-permute-start.1 = (bf16[192,1024]{1,0:T(8,128)(2,1)}, bf16[192,1024]{1,0:T(8,128)(2,1)S(1)}, u32[]{:S(2)}, u32[]{:S(2)}) collective-permute-start(bf16[192,1024]{1,0:T(8,128)(2,1)} %param.4), channel_id=1, source_target_pairs={{0,32},{1,33},{2,34},{3,35},{4,36},{5,37},{6,38},{7,39},{8,40},{9,... | collective-permute-start | bytes 1179656 | tf_op jit(solution)/shard_map/ppermute | solution.py:22
  5.4 21.7 %collective-permute-start.2 = (bf16[192,1024]{1,0:T(8,128)(2,1)}, bf16[192,1024]{1,0:T(8,128)(2,1)S(1)}, u32[]{:S(2)}, u32[]{:S(2)}) collective-permute-start(bf16[192,1024]{1,0:T(8,128)(2,1)} %param.4), channel_id=1, source_target_pairs={{0,96},{1,97},{2,98},{3,99},{4,100},{5,101},{6,102},{7,103},{8,104... | collective-permute-start | bytes 1179656 | tf_op jit(solution)/shard_map/ppermute | solution.py:22
  7.1 20.0 %collective-permute-start.3 = (bf16[192,1024]{1,0:T(8,128)(2,1)}, bf16[192,1024]{1,0:T(8,128)(2,1)S(1)}, u32[]{:S(2)}, u32[]{:S(2)}) collective-permute-start(bf16[192,1024]{1,0:T(8,128)(2,1)} %param.4), channel_id=1, source_target_pairs={{0,0},{1,17},{2,34},{3,51},{4,68},{5,85},{6,102},{7,119},{8,128},{... | collective-permute-start | bytes 1179656 | tf_op jit(solution)/shard_map/ppermute | solution.py:22
  27.2 19.8 %collective-permute-start.4 = (bf16[192,1024]{1,0:T(8,128)(2,1)S(1)}, bf16[192,1024]{1,0:T(8,128)(2,1)S(1)}, u32[]{:S(2)}, u32[]{:S(2)}) collective-permute-start(bf16[192,1024]{1,0:T(8,128)(2,1)S(1)} %collective-permute-done.3.refs_1_), channel_id=1, source_target_pairs={{0,1},{1,2},{2,3},{3,4},{4,5},{5,6},{6,7},{7,0},{8,9},{9,10},{10,1... | collective-permute-start | bytes 1179656 | tf_op jit(solution)/shard_map/ppermute | solution.py:22
  28.2 18.8 %collective-permute-start.5 = (bf16[192,1024]{1,0:T(8,128)(2,1)S(1)}, bf16[192,1024]{1,0:T(8,128)(2,1)S(1)}, u32[]{:S(2)}, u32[]{:S(2)}) collective-permute-start(bf16[192,1024]{1,0:T(8,128)(2,1)S(1)} %collective-permute-done.3.refs_1_), channel_id=1, source_target_pairs={{0,7},{1,0},{2,1},{3,2},{4,3},{5,4},{6,5},{7,6},{8,15},{9,8},{10,9... | collective-permute-start | bytes 1179656 | tf_op jit(solution)/shard_map/ppermute | solution.py:22
  29.3 17.7 %collective-permute-start.6 = (bf16[192,1024]{1,0:T(8,128)(2,1)S(1)}, bf16[192,1024]{1,0:T(8,128)(2,1)S(1)}, u32[]{:S(2)}, u32[]{:S(2)}) collective-permute-start(bf16[192,1024]{1,0:T(8,128)(2,1)S(1)} %collective-permute-done.3.refs_1_), channel_id=1, source_target_pairs={{0,8},{1,9},{2,10},{3,11},{4,12},{5,13},{6,14},{7,15},{8,0},{9,1},... | collective-permute-start | bytes 1179656 | tf_op jit(solution)/shard_map/ppermute | solution.py:22
  30.6 16.4 %collective-permute-start.7 = (bf16[192,1024]{1,0:T(8,128)(2,1)S(1)}, bf16[192,1024]{1,0:T(8,128)(2,1)S(1)}, u32[]{:S(2)}, u32[]{:S(2)}) collective-permute-start(bf16[192,1024]{1,0:T(8,128)(2,1)S(1)} %collective-permute-done), channel_id=1, source_target_pairs={{0,32},{1,33},{2,34},{3,35},{4,36},{5,37},{6,38},{7,39},{8,40},{9,... | collective-permute-start | bytes 1179656 | tf_op jit(solution)/shard_map/ppermute | solution.py:22
  30.6 16.4 %collective-permute-start.8 = (bf16[192,1024]{1,0:T(8,128)(2,1)S(1)}, bf16[192,1024]{1,0:T(8,128)(2,1)S(1)}, u32[]{:S(2)}, u32[]{:S(2)}) collective-permute-start(bf16[192,1024]{1,0:T(8,128)(2,1)S(1)} %collective-permute-done), channel_id=1, source_target_pairs={{0,96},{1,97},{2,98},{3,99},{4,100},{5,101},{6,102},{7,103},{8,104... | collective-permute-start | bytes 1179656 | tf_op jit(solution)/shard_map/ppermute | solution.py:22
  35.2 11.7 %all-to-all-start.1 = ((f32[16,2,192]{2,1,0:T(2,128)}), f32[16,2,192]{2,1,0:T(2,128)}, u32[]{:S(2)}, u32[]{:S(2)}) async-start(f32[16,2,192]{2,1,0:T(2,128)} %broadcast_in_dim.20), calls=%async_computation.1 | async-start | bytes 65536 | tf_op jit(solution)/shard_map/all_to_all | solution.py:41
  47.3 14.7 %collective-permute-start.10 = (bf16[272,1024]{1,0:T(8,128)(2,1)S(1)}, bf16[272,1024]{1,0:T(8,128)(2,1)S(1)}, u32[]{:S(2)}, u32[]{:S(2)}) collective-permute-start(bf16[272,1024]{1,0:T(8,128)(2,1)S(1)} %get-tuple-element.80), channel_id=1, source_target_pairs={{0,7},{1,0},{2,1},{3,2},{4,3},{5,4},{6,5},{7,6},{8,15},{9,8},{10,9... | collective-permute-start | bytes 1671176 | tf_op jit(solution)/shard_map/ppermute | solution.py:22
  48.0 15.5 %collective-permute-start.9 = (bf16[272,1024]{1,0:T(8,128)(2,1)S(1)}, bf16[272,1024]{1,0:T(8,128)(2,1)S(1)}, u32[]{:S(2)}, u32[]{:S(2)}) collective-permute-start(bf16[272,1024]{1,0:T(8,128)(2,1)S(1)} %get-tuple-element.81), channel_id=1, source_target_pairs={{0,1},{1,2},{2,3},{3,4},{4,5},{5,6},{6,7},{7,0},{8,9},{9,10},{10,1... | collective-permute-start | bytes 1671176 | tf_op jit(solution)/shard_map/ppermute | solution.py:22
  49.4 12.3 %collective-permute-start.11 = (bf16[224,1024]{1,0:T(8,128)(2,1)S(1)}, bf16[224,1024]{1,0:T(8,128)(2,1)S(1)}, u32[]{:S(2)}, u32[]{:S(2)}) collective-permute-start(bf16[224,1024]{1,0:T(8,128)(2,1)S(1)} %pad_maximum_fusion.2), channel_id=1, source_target_pairs={{0,8},{1,9},{2,10},{3,11},{4,12},{5,13},{6,14},{7,15},{8,0},{9,1},... | collective-permute-start | bytes 1376264 | tf_op jit(solution)/shard_map/ppermute | solution.py:22
  50.2 11.5 %collective-permute-start.12 = (bf16[192,1024]{1,0:T(8,128)(2,1)S(1)}, bf16[192,1024]{1,0:T(8,128)(2,1)S(1)}, u32[]{:S(2)}, u32[]{:S(2)}) collective-permute-start(bf16[192,1024]{1,0:T(8,128)(2,1)S(1)} %copy-done.15), channel_id=1, source_target_pairs={{0,32},{1,33},{2,34},{3,35},{4,36},{5,37},{6,38},{7,39},{8,40},{9,... | collective-permute-start | bytes 1179656 | tf_op jit(solution)/shard_map/ppermute | solution.py:22
  50.7 10.9 %collective-permute-start.13 = (bf16[192,1024]{1,0:T(8,128)(2,1)S(1)}, bf16[192,1024]{1,0:T(8,128)(2,1)S(1)}, u32[]{:S(2)}, u32[]{:S(2)}) collective-permute-start(bf16[192,1024]{1,0:T(8,128)(2,1)S(1)} %collective-permute-done.8), channel_id=1, source_target_pairs={{0,96},{1,97},{2,98},{3,99},{4,100},{5,101},{6,102},{7,103},{8,104... | collective-permute-start | bytes 1179656 | tf_op jit(solution)/shard_map/ppermute | solution.py:22
  65.4 15.0 %collective-permute-start.14 = (bf16[272,1024]{1,0:T(8,128)(2,1)S(1)}, bf16[272,1024]{1,0:T(8,128)(2,1)S(1)}, u32[]{:S(2)}, u32[]{:S(2)}) collective-permute-start(bf16[272,1024]{1,0:T(8,128)(2,1)S(1)} %collective-permute-done.9.refs_6_), channel_id=1, source_target_pairs={{0,1},{1,2},{2,3},{3,4},{4,5},{5,6},{6,7},{7,0},{8,9},{9,10},{10,1... | collective-permute-start | bytes 1671176 | tf_op jit(solution)/shard_map/ppermute | solution.py:22
  67.3 13.2 %collective-permute-start.15 = (bf16[272,1024]{1,0:T(8,128)(2,1)S(1)}, bf16[272,1024]{1,0:T(8,128)(2,1)S(1)}, u32[]{:S(2)}, u32[]{:S(2)}) collective-permute-start(bf16[272,1024]{1,0:T(8,128)(2,1)S(1)} %collective-permute-done.10.refs_7_), channel_id=1, source_target_pairs={{0,7},{1,0},{2,1},{3,2},{4,3},{5,4},{6,5},{7,6},{8,15},{9,8},{10,9... | collective-permute-start | bytes 1671176 | tf_op jit(solution)/shard_map/ppermute | solution.py:22
  67.4 12.9 %collective-permute-start.16 = (bf16[112,1024]{1,0:T(8,128)(2,1)S(1)}, bf16[112,1024]{1,0:T(8,128)(2,1)S(1)}, u32[]{:S(2)}, u32[]{:S(2)}) collective-permute-start(bf16[112,1024]{1,0:T(8,128)(2,1)S(1)} %slice.49), channel_id=1, source_target_pairs={{0,8},{1,9},{2,10},{3,11},{4,12},{5,13},{6,14},{7,15},{8,0},{9,1},... | collective-permute-start | bytes 688136 | tf_op jit(solution)/shard_map/ppermute | solution.py:22
  68.7 11.6 %collective-permute-start.17 = (bf16[112,1024]{1,0:T(8,128)(2,1)S(1)}, bf16[112,1024]{1,0:T(8,128)(2,1)S(1)}, u32[]{:S(2)}, u32[]{:S(2)}) collective-permute-start(bf16[112,1024]{1,0:T(8,128)(2,1)S(1)} %slice.50), channel_id=1, source_target_pairs={{0,8},{1,9},{2,10},{3,11},{4,12},{5,13},{6,14},{7,15},{8,0},{9,1},... | collective-permute-start | bytes 688136 | tf_op jit(solution)/shard_map/ppermute | solution.py:22
  80.5 13.8 %collective-permute-start.20 = (bf16[192,1024]{1,0:T(8,128)(2,1)S(1)}, bf16[192,1024]{1,0:T(8,128)(2,1)S(1)}, u32[]{:S(2)}, u32[]{:S(2)}) collective-permute-start(bf16[192,1024]{1,0:T(8,128)(2,1)S(1)} %slice.52), channel_id=1, source_target_pairs={{0,7},{1,0},{2,1},{3,2},{4,3},{5,4},{6,5},{7,6},{8,15},{9,8},{10,9... | collective-permute-start | bytes 1179656 | tf_op jit(solution)/shard_map/ppermute | solution.py:22
  83.1 11.2 %collective-permute-start.19 = (bf16[160,1024]{1,0:T(8,128)(2,1)S(1)}, bf16[160,1024]{1,0:T(8,128)(2,1)S(1)}, u32[]{:S(2)}, u32[]{:S(2)}) collective-permute-start(bf16[160,1024]{1,0:T(8,128)(2,1)S(1)} %slice.51), channel_id=1, source_target_pairs={{0,1},{1,2},{2,3},{3,4},{4,5},{5,6},{6,7},{7,0},{8,9},{9,10},{10,1... | collective-permute-start | bytes 983048 | tf_op jit(solution)/shard_map/ppermute | solution.py:22
  83.6 10.5 %collective-permute-start.21 = (bf16[112,1024]{1,0:T(8,128)(2,1)S(1)}, bf16[112,1024]{1,0:T(8,128)(2,1)S(1)}, u32[]{:S(2)}, u32[]{:S(2)}) collective-permute-start(bf16[112,1024]{1,0:T(8,128)(2,1)S(1)} %slice.53), channel_id=1, source_target_pairs={{0,8},{1,9},{2,10},{3,11},{4,12},{5,13},{6,14},{7,15},{8,0},{9,1},... | collective-permute-start | bytes 688136 | tf_op jit(solution)/shard_map/ppermute | solution.py:22
  94.3 11.6 %collective-permute-start.24 = (bf16[112,1024]{1,0:T(8,128)(2,1)S(1)}, bf16[112,1024]{1,0:T(8,128)(2,1)S(1)}, u32[]{:S(2)}, u32[]{:S(2)}) collective-permute-start(bf16[112,1024]{1,0:T(8,128)(2,1)S(1)} %slice.56), channel_id=1, source_target_pairs={{0,8},{1,9},{2,10},{3,11},{4,12},{5,13},{6,14},{7,15},{8,0},{9,1},... | collective-permute-start | bytes 688136 | tf_op jit(solution)/shard_map/ppermute | solution.py:22
  96.5 9.4 %collective-permute-start.23 = (bf16[80,1024]{1,0:T(8,128)(2,1)S(1)}, bf16[80,1024]{1,0:T(8,128)(2,1)S(1)}, u32[]{:S(2)}, u32[]{:S(2)}) collective-permute-start(bf16[80,1024]{1,0:T(8,128)(2,1)S(1)} %slice.55), channel_id=1, source_target_pairs={{0,1},{1,2},{2,3},{3,4},{4,5},{5,6},{6,7},{7,0},{8,9},{9,10},{10,1... | collective-permute-start | bytes 491528 | tf_op jit(solution)/shard_map/ppermute | solution.py:22
  (28 other events, 226.8 us)

commit v6 on v5

--- a/solution.py
+++ b/solution.py
@@ -269,14 +269,15 @@
     across = swap(features, "yh")
     left1, right1 = shift(features, "x", 1), shift(features, "x", -1)
     margins = from_all(partial, "feat").sum(axis=0)
-    across, left1, right1, margins, mine = together(
-        across, left1, right1, margins, mine
+    marks = labels.astype(jnp.float32)
+    across, left1, right1, margins, marks, mine = together(
+        across, left1, right1, margins, marks, mine
     )
 
     up1, down1 = shift(mine, "z", 1), shift(mine, "z", -1)
     mine_y = swap(mine, "yl")
     left2, right2 = shift(across, "x", 1), shift(across, "x", -1)
-    facts = jnp.stack([margins, labels.astype(jnp.float32)])
+    facts = jnp.stack([margins, marks])
     facts = from_all(facts, "rows")
     held = (features, across, left1, right1, prior_prec)
     up1, down1, mine_y, left2, right2, facts, *held = together(

time: 114 us -> 113 us (level)
  blocking collectives: 15.8 us -> 0 us
  starting transfers between devices: 40.7 us -> 49.8 us
  waiting for transfers between devices: 13 us -> 18.9 us
    all_to_all x1 -> x0, blocking collectives: 15.8 us -> none  [from_all(): return lax.all_to_all(copies, axis, split_axis=0, concat_axis=0, tiled=True)]
    all_to_all x1 -> x2, starting transfers between devices: 4.13 us -> 13.8 us  [from_all(): return lax.all_to_all(copies, axis, split_axis=0, concat_axis=0, tiled=True)]
    all_to_all x1 -> x2, waiting for transfers between devices: 5.58 us -> 11.3 us  [from_all(): return lax.all_to_all(copies, axis, split_axis=0, concat_axis=0, tiled=True)]
    unnamed x60 -> x68, local copies, waits for them, and re-layouts: 5.5 us -> 5.46 us
  transfers between devices with their start and end apart: 26 -> 27, of which waited for: 5 -> 5; matrix products, arithmetic and copies ran while one was open for 7% -> 8% of each run, Pallas kernels for 20% -> 20%
where the time goes in v6:
time: 113 us
  starting transfers between devices  49.8 us (44%)
  Pallas kernels  28.4 us (25%)
  waiting for transfers between devices  18.9 us (17%)
  local copies, waits for them, and re-layouts  8.83 us (8%)
  other arithmetic  3.54 us (3%)
  between operations  2.07 us (2%)
  matrix products  1.19 us (1%)
    ppermute x25, starting transfers between devices, permuted(): return lax.ppermute(x, ('rows', 'feat'), pairs)  36 us
    pallas_call x3, Pallas kernels, gram(): pl.pallas_call(lambda *refs: gram_kernel(slots, first, n, len(pieces), cu...  20.1 us
    all_to_all x2, starting transfers between devices, from_all(): return lax.all_to_all(copies, axis, split_axis=0, concat_axis=0, tiled=True)  13.8 us
    all_to_all x2, waiting for transfers between devices, from_all(): return lax.all_to_all(copies, axis, split_axis=0, concat_axis=0, tiled=True)  11.3 us
    pallas_call x1, Pallas kernels, prepare(): pl.pallas_call(prepare_kernel, in_specs=[smem, smem] + [anywhere] * 2 + [...  8.32 us
    ppermute x25, waiting for transfers between devices, permuted(): return lax.ppermute(x, ('rows', 'feat'), pairs)  7.59 us
    unnamed x68, local copies, waits for them, and re-layouts  5.46 us
  transfers between devices with their start and end apart: 27, of which 5 were waited for; matrix products, arithmetic and copies ran while one was open for 8% of the time, Pallas kernels for 20%

profile of v6, /device:TPU:64, one launch (start us, length us, event | category | flops | bytes accessed | tf_op | source)
XLA Modules:
  0.0 112.8 jit_solution(13112932038447613885)
XLA Ops:
  0.6 3.3 %collective-permute-start = (bf16[192,1024]{1,0:T(8,128)(2,1)}, bf16[192,1024]{1,0:T(8,128)(2,1)S(1)}, u32[]{:S(2)}, u32[]{:S(2)}) collective-permute-start(bf16[192,1024]{1,0:T(8,128)(2,1)} %param.4), channel_id=1, source_target_pairs={{0,128},{1,129},{2,130},{3,131},{4,132},{5,133},{6,134},{7,135},{8... | collective-permute-start | bytes 1179656 | tf_op jit(solution)/shard_map/ppermute | solution.py:22
  3.9 1.5 %collective-permute-start.1 = (bf16[192,1024]{1,0:T(8,128)(2,1)}, bf16[192,1024]{1,0:T(8,128)(2,1)S(1)}, u32[]{:S(2)}, u32[]{:S(2)}) collective-permute-start(bf16[192,1024]{1,0:T(8,128)(2,1)} %param.4), channel_id=1, source_target_pairs={{0,32},{1,33},{2,34},{3,35},{4,36},{5,37},{6,38},{7,39},{8,40},{9,... | collective-permute-start | bytes 1179656 | tf_op jit(solution)/shard_map/ppermute | solution.py:22
  5.4 1.7 %collective-permute-start.2 = (bf16[192,1024]{1,0:T(8,128)(2,1)}, bf16[192,1024]{1,0:T(8,128)(2,1)S(1)}, u32[]{:S(2)}, u32[]{:S(2)}) collective-permute-start(bf16[192,1024]{1,0:T(8,128)(2,1)} %param.4), channel_id=1, source_target_pairs={{0,96},{1,97},{2,98},{3,99},{4,100},{5,101},{6,102},{7,103},{8,104... | collective-permute-start | bytes 1179656 | tf_op jit(solution)/shard_map/ppermute | solution.py:22
  7.1 2.2 %collective-permute-start.3 = (bf16[192,1024]{1,0:T(8,128)(2,1)}, bf16[192,1024]{1,0:T(8,128)(2,1)S(1)}, u32[]{:S(2)}, u32[]{:S(2)}) collective-permute-start(bf16[192,1024]{1,0:T(8,128)(2,1)} %param.4), channel_id=1, source_target_pairs={{0,0},{1,17},{2,34},{3,51},{4,68},{5,85},{6,102},{7,119},{8,128},{... | collective-permute-start | bytes 1179656 | tf_op jit(solution)/shard_map/ppermute | solution.py:22
  11.9 9.7 %all-to-all-start = ((f32[16,1,192]{2,1,0:T(1,128)}), f32[16,1,192]{2,1,0:T(1,128)S(1)}, u32[]{:S(2)}, u32[]{:S(2)}) async-start(f32[16,1,192]{2,1,0:T(1,128)} %broadcast_in_dim.19), calls=%async_computation | async-start | bytes 32768 | tf_op jit(solution)/shard_map/all_to_all | solution.py:41
  22.2 5.7 %all-to-all-done = f32[16,1,192]{2,1,0:T(1,128)S(1)} async-done(((f32[16,1,192]{2,1,0:T(1,128)}), f32[16,1,192]{2,1,0:T(1,128)S(1)}, u32[]{:S(2)}, u32[]{:S(2)}) %all-to-all-start) | async-done | bytes 12320 | tf_op jit(solution)/shard_map/all_to_all | solution.py:41
  31.2 2.7 %collective-permute-start.8 = (bf16[192,1024]{1,0:T(8,128)(2,1)S(1)}, bf16[192,1024]{1,0:T(8,128)(2,1)S(1)}, u32[]{:S(2)}, u32[]{:S(2)}) collective-permute-start(bf16[192,1024]{1,0:T(8,128)(2,1)S(1)} %collective-permute-done), channel_id=1, source_target_pairs={{0,96},{1,97},{2,98},{3,99},{4,100},{5,101},{6,102},{7,103},{8,104... | collective-permute-start | bytes 1179656 | tf_op jit(solution)/shard_map/ppermute | solution.py:22
  34.5 4.1 %all-to-all-start.1 = ((f32[16,2,192]{2,1,0:T(2,128)}), f32[16,2,192]{2,1,0:T(2,128)}, u32[]{:S(2)}, u32[]{:S(2)}) async-start(f32[16,2,192]{2,1,0:T(2,128)} %broadcast_in_dim.20), calls=%async_computation.1 | async-start | bytes 65536 | tf_op jit(solution)/shard_map/all_to_all | solution.py:41
  40.6 5.6 %all-to-all-done.1 = f32[16,2,192]{2,1,0:T(2,128)} async-done(((f32[16,2,192]{2,1,0:T(2,128)}), f32[16,2,192]{2,1,0:T(2,128)}, u32[]{:S(2)}, u32[]{:S(2)}) %all-to-all-start.1) | async-done | bytes 24608 | tf_op jit(solution)/shard_map/all_to_all | solution.py:41
  46.6 1.5 %collective-permute-start.10 = (bf16[272,1024]{1,0:T(8,128)(2,1)S(1)}, bf16[272,1024]{1,0:T(8,128)(2,1)S(1)}, u32[]{:S(2)}, u32[]{:S(2)}) collective-permute-start(bf16[272,1024]{1,0:T(8,128)(2,1)S(1)} %get-tuple-element.82), channel_id=1, source_target_pairs={{0,7},{1,0},{2,1},{3,2},{4,3},{5,4},{6,5},{7,6},{8,15},{9,8},{10,9... | collective-permute-start | bytes 1671176 | tf_op jit(solution)/shard_map/ppermute | solution.py:22
  48.8 1.5 %collective-permute-start.11 = (bf16[224,1024]{1,0:T(8,128)(2,1)S(1)}, bf16[224,1024]{1,0:T(8,128)(2,1)S(1)}, u32[]{:S(2)}, u32[]{:S(2)}) collective-permute-start(bf16[224,1024]{1,0:T(8,128)(2,1)S(1)} %pad_maximum_fusion.2), channel_id=1, source_target_pairs={{0,8},{1,9},{2,10},{3,11},{4,12},{5,13},{6,14},{7,15},{8,0},{9,1},... | collective-permute-start | bytes 1376264 | tf_op jit(solution)/shard_map/ppermute | solution.py:22
  50.9 2.7 %collective-permute-start.13 = (bf16[192,1024]{1,0:T(8,128)(2,1)}, bf16[192,1024]{1,0:T(8,128)(2,1)S(1)}, u32[]{:S(2)}, u32[]{:S(2)}) collective-permute-start(bf16[192,1024]{1,0:T(8,128)(2,1)} %copy-done.18), channel_id=1, source_target_pairs={{0,96},{1,97},{2,98},{3,99},{4,100},{5,101},{6,102},{7,103},{8,104... | collective-permute-start | bytes 1179656 | tf_op jit(solution)/shard_map/ppermute | solution.py:22
  53.6 1.5 %subtract_convert_fusion = (bf16[16,1,192]{2,1,0:T(2,128)(2,1)}, f32[16,1,192]{2,1,0:T(1,128)S(1)}) fusion(f32[16,2,192]{2,1,0:T(2,128)} %all-to-all-done.1), kind=kLoop, calls=%fused_computation.14 | loop fusion | flops 15360 | bytes 43008 | tf_op jit(solution)/shard_map/convert_element_type | solution.py:289
  56.5 5.3 %collective-permute-done.12 = bf16[192,1024]{1,0:T(8,128)(2,1)S(1)} collective-permute-done((bf16[192,1024]{1,0:T(8,128)(2,1)S(1)}, bf16[192,1024]{1,0:T(8,128)(2,1)S(1)}, u32[]{:S(2)}, u32[]{:S(2)}) %collective-permute-start.12) | collective-permute-done | bytes 393248 | tf_op jit(solution)/shard_map/ppermute | solution.py:22
  61.9 1.9 %collective-permute-done.9.refs_6_ = bf16[272,1024]{1,0:T(8,128)(2,1)S(1)} collective-permute-done((bf16[272,1024]{1,0:T(8,128)(2,1)S(1)}, bf16[272,1024]{1,0:T(8,128)(2,1)S(1)}, u32[]{:S(2)}, u32[]{:S(2)}) %collective-permute-start.9) | collective-permute-done | bytes 557088 | tf_op jit(solution)/shard_map/ppermute | solution.py:22
  70.4 1.7 %copy-done.3 = bf16[8,192,1024]{2,1,0:T(8,128)(2,1)} copy-done((bf16[8,192,1024]{2,1,0:T(8,128)(2,1)}, bf16[8,192,1024]{2,1,0:T(8,128)(2,1)S(1)}, u32[]{:S(2)}) %copy-start.3) | copy-done | bytes 3145752
  72.1 8.3 %prepare.1 = (bf16[1024,3072]{1,0:T(8,128)(2,1)}, f32[1,1024]{1,0:T(1,128)}) custom-call(s32[16]{0:T(128)} %stack.157.slot_ref, s32[16]{0:T(128)} %stack.174.row_ref, bf16[8,192,1024]{2,1,0:T(8,128)(2,1)} %copy-done.2, bf16[8,192,1024]{2,1,0:T(8,128)(2,1)} %copy-done.3, f32[16,1,192]{2,1,0:T(1,128)} %fusion.1.refs_2_, ...), custom_call_target="tpu_custom_call" | custom-call | flops 1 | bytes 1 | tf_op jit(solution)/shard_map/prepare/pallas_call | solution.py:95
  80.8 1.6 %collective-permute-start.20 = (bf16[192,1024]{1,0:T(8,128)(2,1)S(1)}, bf16[192,1024]{1,0:T(8,128)(2,1)S(1)}, u32[]{:S(2)}, u32[]{:S(2)}) collective-permute-start(bf16[192,1024]{1,0:T(8,128)(2,1)S(1)} %slice.52), channel_id=1, source_target_pairs={{0,7},{1,0},{2,1},{3,2},{4,3},{5,4},{6,5},{7,6},{8,15},{9,8},{10,9... | collective-permute-start | bytes 1179656 | tf_op jit(solution)/shard_map/ppermute | solution.py:22
  82.5 1.5 %collective-permute-start.19 = (bf16[160,1024]{1,0:T(8,128)(2,1)S(1)}, bf16[160,1024]{1,0:T(8,128)(2,1)S(1)}, u32[]{:S(2)}, u32[]{:S(2)}) collective-permute-start(bf16[160,1024]{1,0:T(8,128)(2,1)S(1)} %slice.51), channel_id=1, source_target_pairs={{0,1},{1,2},{2,3},{3,4},{4,5},{5,6},{6,7},{7,0},{8,9},{9,10},{10,1... | collective-permute-start | bytes 983048 | tf_op jit(solution)/shard_map/ppermute | solution.py:22
  86.2 8.3 %gram.3.refs_7_ = bf16[1024,1024]{1,0:T(8,128)(2,1)} custom-call(bf16[1024,3072]{1,0:T(8,128)(2,1)} %get-tuple-element.67.refs_0_, bf16[192,1024]{1,0:T(8,128)(2,1)} %copy-done.13, bf16[192,1024]{1,0:T(8,128)(2,1)} %copy-done.11, bf16[192,1024]{1,0:T(8,128)(2,1)} %copy-done.7, bf16[192,1024]{1,0:T(8,128)(2,1)} %copy-done.5, bf16[224,1024]{1,0:T(8,128)(2,1)} %copy-done.12, ...), custom_call_target="tpu_custom_call" | custom-call | flops 1 | bytes 1 | tf_op jit(solution)/shard_map/gram/pallas_call | solution.py:211
  94.6 1.5 %collective-permute-start.24 = (bf16[112,1024]{1,0:T(8,128)(2,1)S(1)}, bf16[112,1024]{1,0:T(8,128)(2,1)S(1)}, u32[]{:S(2)}, u32[]{:S(2)}) collective-permute-start(bf16[112,1024]{1,0:T(8,128)(2,1)S(1)} %slice.56), channel_id=1, source_target_pairs={{0,8},{1,9},{2,10},{3,11},{4,12},{5,13},{6,14},{7,15},{8,0},{9,1},... | collective-permute-start | bytes 688136 | tf_op jit(solution)/shard_map/ppermute | solution.py:22
  96.1 3.3 %collective-permute-start.23 = (bf16[80,1024]{1,0:T(8,128)(2,1)S(1)}, bf16[80,1024]{1,0:T(8,128)(2,1)S(1)}, u32[]{:S(2)}, u32[]{:S(2)}) collective-permute-start(bf16[80,1024]{1,0:T(8,128)(2,1)S(1)} %slice.55), channel_id=1, source_target_pairs={{0,1},{1,2},{2,3},{3,4},{4,5},{5,6},{6,7},{7,0},{8,9},{9,10},{10,1... | collective-permute-start | bytes 491528 | tf_op jit(solution)/shard_map/ppermute | solution.py:22
  99.4 6.1 %gram.4.refs_5_ = bf16[1024,1024]{1,0:T(8,128)(2,1)} custom-call(bf16[1024,3072]{1,0:T(8,128)(2,1)} %get-tuple-element.67.refs_0_, bf16[272,1024]{1,0:T(8,128)(2,1)} %copy-done.1, bf16[272,1024]{1,0:T(8,128)(2,1)} %copy-done, bf16[112,1024]{1,0:T(8,128)(2,1)} %copy-done.24, bf16[112,1024]{1,0:T(8,128)(2,1)} %copy-done.25, bf16[160,1024]{1,0:T(8,128)(2,1)} %copy-done.6, ...), custom_call_target="tpu_custom_call" | custom-call | flops 1 | bytes 1 | tf_op jit(solution)/shard_map/gram/pallas_call | solution.py:211
  106.9 5.7 %gram.5 = f32[1024,1024]{1,0:T(8,128)} custom-call(bf16[1024,3072]{1,0:T(8,128)(2,1)} %get-tuple-element.67.refs_0_, bf16[160,1024]{1,0:T(8,128)(2,1)} %copy-done.6, bf16[192,1024]{1,0:T(8,128)(2,1)} %copy-done.4, bf16[80,1024]{1,0:T(8,128)(2,1)} %copy-done.27, bf16[112,1024]{1,0:T(8,128)(2,1)} %copy-done.26, bf16[1024,1024]{1,0:T(8,128)(2,1)} %gram.4.refs_5_, ...), custom_call_target="tpu_custom_call" | custom-call | flops 1 | bytes 1 | tf_op jit(solution)/shard_map/gram/pallas_call | solution.py:211
  (129 shorter events, 21.7 us)
Async XLA Ops:
  0.6 27.3 %collective-permute-start = (bf16[192,1024]{1,0:T(8,128)(2,1)}, bf16[192,1024]{1,0:T(8,128)(2,1)S(1)}, u32[]{:S(2)}, u32[]{:S(2)}) collective-permute-start(bf16[192,1024]{1,0:T(8,128)(2,1)} %param.4), channel_id=1, source_target_pairs={{0,128},{1,129},{2,130},{3,131},{4,132},{5,133},{6,134},{7,135},{8... | collective-permute-start | bytes 1179656 | tf_op jit(solution)/shard_map/ppermute | solution.py:22
  3.9 24.0 %collective-permute-start.1 = (bf16[192,1024]{1,0:T(8,128)(2,1)}, bf16[192,1024]{1,0:T(8,128)(2,1)S(1)}, u32[]{:S(2)}, u32[]{:S(2)}) collective-permute-start(bf16[192,1024]{1,0:T(8,128)(2,1)} %param.4), channel_id=1, source_target_pairs={{0,32},{1,33},{2,34},{3,35},{4,36},{5,37},{6,38},{7,39},{8,40},{9,... | collective-permute-start | bytes 1179656 | tf_op jit(solution)/shard_map/ppermute | solution.py:22
  5.4 22.5 %collective-permute-start.2 = (bf16[192,1024]{1,0:T(8,128)(2,1)}, bf16[192,1024]{1,0:T(8,128)(2,1)S(1)}, u32[]{:S(2)}, u32[]{:S(2)}) collective-permute-start(bf16[192,1024]{1,0:T(8,128)(2,1)} %param.4), channel_id=1, source_target_pairs={{0,96},{1,97},{2,98},{3,99},{4,100},{5,101},{6,102},{7,103},{8,104... | collective-permute-start | bytes 1179656 | tf_op jit(solution)/shard_map/ppermute | solution.py:22
  7.1 20.8 %collective-permute-start.3 = (bf16[192,1024]{1,0:T(8,128)(2,1)}, bf16[192,1024]{1,0:T(8,128)(2,1)S(1)}, u32[]{:S(2)}, u32[]{:S(2)}) collective-permute-start(bf16[192,1024]{1,0:T(8,128)(2,1)} %param.4), channel_id=1, source_target_pairs={{0,0},{1,17},{2,34},{3,51},{4,68},{5,85},{6,102},{7,119},{8,128},{... | collective-permute-start | bytes 1179656 | tf_op jit(solution)/shard_map/ppermute | solution.py:22
  11.9 16.0 %all-to-all-start = ((f32[16,1,192]{2,1,0:T(1,128)}), f32[16,1,192]{2,1,0:T(1,128)S(1)}, u32[]{:S(2)}, u32[]{:S(2)}) async-start(f32[16,1,192]{2,1,0:T(1,128)} %broadcast_in_dim.19), calls=%async_computation | async-start | bytes 32768 | tf_op jit(solution)/shard_map/all_to_all | solution.py:41
  28.0 18.3 %collective-permute-start.4 = (bf16[192,1024]{1,0:T(8,128)(2,1)S(1)}, bf16[192,1024]{1,0:T(8,128)(2,1)S(1)}, u32[]{:S(2)}, u32[]{:S(2)}) collective-permute-start(bf16[192,1024]{1,0:T(8,128)(2,1)S(1)} %collective-permute-done.3.refs_1_), channel_id=1, source_target_pairs={{0,1},{1,2},{2,3},{3,4},{4,5},{5,6},{6,7},{7,0},{8,9},{9,10},{10,1... | collective-permute-start | bytes 1179656 | tf_op jit(solution)/shard_map/ppermute | solution.py:22
  28.6 17.7 %collective-permute-start.5 = (bf16[192,1024]{1,0:T(8,128)(2,1)S(1)}, bf16[192,1024]{1,0:T(8,128)(2,1)S(1)}, u32[]{:S(2)}, u32[]{:S(2)}) collective-permute-start(bf16[192,1024]{1,0:T(8,128)(2,1)S(1)} %collective-permute-done.3.refs_1_), channel_id=1, source_target_pairs={{0,7},{1,0},{2,1},{3,2},{4,3},{5,4},{6,5},{7,6},{8,15},{9,8},{10,9... | collective-permute-start | bytes 1179656 | tf_op jit(solution)/shard_map/ppermute | solution.py:22
  30.1 16.2 %collective-permute-start.6 = (bf16[192,1024]{1,0:T(8,128)(2,1)S(1)}, bf16[192,1024]{1,0:T(8,128)(2,1)S(1)}, u32[]{:S(2)}, u32[]{:S(2)}) collective-permute-start(bf16[192,1024]{1,0:T(8,128)(2,1)S(1)} %collective-permute-done.3.refs_1_), channel_id=1, source_target_pairs={{0,8},{1,9},{2,10},{3,11},{4,12},{5,13},{6,14},{7,15},{8,0},{9,1},... | collective-permute-start | bytes 1179656 | tf_op jit(solution)/shard_map/ppermute | solution.py:22
  30.7 15.6 %collective-permute-start.7 = (bf16[192,1024]{1,0:T(8,128)(2,1)S(1)}, bf16[192,1024]{1,0:T(8,128)(2,1)S(1)}, u32[]{:S(2)}, u32[]{:S(2)}) collective-permute-start(bf16[192,1024]{1,0:T(8,128)(2,1)S(1)} %collective-permute-done), channel_id=1, source_target_pairs={{0,32},{1,33},{2,34},{3,35},{4,36},{5,37},{6,38},{7,39},{8,40},{9,... | collective-permute-start | bytes 1179656 | tf_op jit(solution)/shard_map/ppermute | solution.py:22
  31.2 15.1 %collective-permute-start.8 = (bf16[192,1024]{1,0:T(8,128)(2,1)S(1)}, bf16[192,1024]{1,0:T(8,128)(2,1)S(1)}, u32[]{:S(2)}, u32[]{:S(2)}) collective-permute-start(bf16[192,1024]{1,0:T(8,128)(2,1)S(1)} %collective-permute-done), channel_id=1, source_target_pairs={{0,96},{1,97},{2,98},{3,99},{4,100},{5,101},{6,102},{7,103},{8,104... | collective-permute-start | bytes 1179656 | tf_op jit(solution)/shard_map/ppermute | solution.py:22
  34.5 11.7 %all-to-all-start.1 = ((f32[16,2,192]{2,1,0:T(2,128)}), f32[16,2,192]{2,1,0:T(2,128)}, u32[]{:S(2)}, u32[]{:S(2)}) async-start(f32[16,2,192]{2,1,0:T(2,128)} %broadcast_in_dim.20), calls=%async_computation.1 | async-start | bytes 65536 | tf_op jit(solution)/shard_map/all_to_all | solution.py:41
  46.6 15.3 %collective-permute-start.10 = (bf16[272,1024]{1,0:T(8,128)(2,1)S(1)}, bf16[272,1024]{1,0:T(8,128)(2,1)S(1)}, u32[]{:S(2)}, u32[]{:S(2)}) collective-permute-start(bf16[272,1024]{1,0:T(8,128)(2,1)S(1)} %get-tuple-element.82), channel_id=1, source_target_pairs={{0,7},{1,0},{2,1},{3,2},{4,3},{5,4},{6,5},{7,6},{8,15},{9,8},{10,9... | collective-permute-start | bytes 1671176 | tf_op jit(solution)/shard_map/ppermute | solution.py:22
  48.1 15.6 %collective-permute-start.9 = (bf16[272,1024]{1,0:T(8,128)(2,1)S(1)}, bf16[272,1024]{1,0:T(8,128)(2,1)S(1)}, u32[]{:S(2)}, u32[]{:S(2)}) collective-permute-start(bf16[272,1024]{1,0:T(8,128)(2,1)S(1)} %get-tuple-element.83), channel_id=1, source_target_pairs={{0,1},{1,2},{2,3},{3,4},{4,5},{5,6},{6,7},{7,0},{8,9},{9,10},{10,1... | collective-permute-start | bytes 1671176 | tf_op jit(solution)/shard_map/ppermute | solution.py:22
  48.8 13.0 %collective-permute-start.11 = (bf16[224,1024]{1,0:T(8,128)(2,1)S(1)}, bf16[224,1024]{1,0:T(8,128)(2,1)S(1)}, u32[]{:S(2)}, u32[]{:S(2)}) collective-permute-start(bf16[224,1024]{1,0:T(8,128)(2,1)S(1)} %pad_maximum_fusion.2), channel_id=1, source_target_pairs={{0,8},{1,9},{2,10},{3,11},{4,12},{5,13},{6,14},{7,15},{8,0},{9,1},... | collective-permute-start | bytes 1376264 | tf_op jit(solution)/shard_map/ppermute | solution.py:22
  50.3 11.5 %collective-permute-start.12 = (bf16[192,1024]{1,0:T(8,128)(2,1)S(1)}, bf16[192,1024]{1,0:T(8,128)(2,1)S(1)}, u32[]{:S(2)}, u32[]{:S(2)}) collective-permute-start(bf16[192,1024]{1,0:T(8,128)(2,1)S(1)} %copy-done.15), channel_id=1, source_target_pairs={{0,32},{1,33},{2,34},{3,35},{4,36},{5,37},{6,38},{7,39},{8,40},{9,... | collective-permute-start | bytes 1179656 | tf_op jit(solution)/shard_map/ppermute | solution.py:22
  50.9 10.9 %collective-permute-start.13 = (bf16[192,1024]{1,0:T(8,128)(2,1)}, bf16[192,1024]{1,0:T(8,128)(2,1)S(1)}, u32[]{:S(2)}, u32[]{:S(2)}) collective-permute-start(bf16[192,1024]{1,0:T(8,128)(2,1)} %copy-done.18), channel_id=1, source_target_pairs={{0,96},{1,97},{2,98},{3,99},{4,100},{5,101},{6,102},{7,103},{8,104... | collective-permute-start | bytes 1179656 | tf_op jit(solution)/shard_map/ppermute | solution.py:22
  65.6 14.9 %collective-permute-start.14 = (bf16[272,1024]{1,0:T(8,128)(2,1)S(1)}, bf16[272,1024]{1,0:T(8,128)(2,1)S(1)}, u32[]{:S(2)}, u32[]{:S(2)}) collective-permute-start(bf16[272,1024]{1,0:T(8,128)(2,1)S(1)} %collective-permute-done.9.refs_6_), channel_id=1, source_target_pairs={{0,1},{1,2},{2,3},{3,4},{4,5},{5,6},{6,7},{7,0},{8,9},{9,10},{10,1... | collective-permute-start | bytes 1671176 | tf_op jit(solution)/shard_map/ppermute | solution.py:22
  66.9 13.9 %collective-permute-start.15 = (bf16[272,1024]{1,0:T(8,128)(2,1)S(1)}, bf16[272,1024]{1,0:T(8,128)(2,1)S(1)}, u32[]{:S(2)}, u32[]{:S(2)}) collective-permute-start(bf16[272,1024]{1,0:T(8,128)(2,1)S(1)} %collective-permute-done.10.refs_7_), channel_id=1, source_target_pairs={{0,7},{1,0},{2,1},{3,2},{4,3},{5,4},{6,5},{7,6},{8,15},{9,8},{10,9... | collective-permute-start | bytes 1671176 | tf_op jit(solution)/shard_map/ppermute | solution.py:22
  67.6 12.8 %collective-permute-start.16 = (bf16[112,1024]{1,0:T(8,128)(2,1)S(1)}, bf16[112,1024]{1,0:T(8,128)(2,1)S(1)}, u32[]{:S(2)}, u32[]{:S(2)}) collective-permute-start(bf16[112,1024]{1,0:T(8,128)(2,1)S(1)} %slice.49), channel_id=1, source_target_pairs={{0,8},{1,9},{2,10},{3,11},{4,12},{5,13},{6,14},{7,15},{8,0},{9,1},... | collective-permute-start | bytes 688136 | tf_op jit(solution)/shard_map/ppermute | solution.py:22
  69.0 11.4 %collective-permute-start.17 = (bf16[112,1024]{1,0:T(8,128)(2,1)S(1)}, bf16[112,1024]{1,0:T(8,128)(2,1)S(1)}, u32[]{:S(2)}, u32[]{:S(2)}) collective-permute-start(bf16[112,1024]{1,0:T(8,128)(2,1)S(1)} %slice.50), channel_id=1, source_target_pairs={{0,8},{1,9},{2,10},{3,11},{4,12},{5,13},{6,14},{7,15},{8,0},{9,1},... | collective-permute-start | bytes 688136 | tf_op jit(solution)/shard_map/ppermute | solution.py:22
  80.8 13.7 %collective-permute-start.20 = (bf16[192,1024]{1,0:T(8,128)(2,1)S(1)}, bf16[192,1024]{1,0:T(8,128)(2,1)S(1)}, u32[]{:S(2)}, u32[]{:S(2)}) collective-permute-start(bf16[192,1024]{1,0:T(8,128)(2,1)S(1)} %slice.52), channel_id=1, source_target_pairs={{0,7},{1,0},{2,1},{3,2},{4,3},{5,4},{6,5},{7,6},{8,15},{9,8},{10,9... | collective-permute-start | bytes 1179656 | tf_op jit(solution)/shard_map/ppermute | solution.py:22
  82.5 12.0 %collective-permute-start.19 = (bf16[160,1024]{1,0:T(8,128)(2,1)S(1)}, bf16[160,1024]{1,0:T(8,128)(2,1)S(1)}, u32[]{:S(2)}, u32[]{:S(2)}) collective-permute-start(bf16[160,1024]{1,0:T(8,128)(2,1)S(1)} %slice.51), channel_id=1, source_target_pairs={{0,1},{1,2},{2,3},{3,4},{4,5},{5,6},{6,7},{7,0},{8,9},{9,10},{10,1... | collective-permute-start | bytes 983048 | tf_op jit(solution)/shard_map/ppermute | solution.py:22
  84.0 10.4 %collective-permute-start.21 = (bf16[112,1024]{1,0:T(8,128)(2,1)S(1)}, bf16[112,1024]{1,0:T(8,128)(2,1)S(1)}, u32[]{:S(2)}, u32[]{:S(2)}) collective-permute-start(bf16[112,1024]{1,0:T(8,128)(2,1)S(1)} %slice.53), channel_id=1, source_target_pairs={{0,8},{1,9},{2,10},{3,11},{4,12},{5,13},{6,14},{7,15},{8,0},{9,1},... | collective-permute-start | bytes 688136 | tf_op jit(solution)/shard_map/ppermute | solution.py:22
  94.6 11.0 %collective-permute-start.24 = (bf16[112,1024]{1,0:T(8,128)(2,1)S(1)}, bf16[112,1024]{1,0:T(8,128)(2,1)S(1)}, u32[]{:S(2)}, u32[]{:S(2)}) collective-permute-start(bf16[112,1024]{1,0:T(8,128)(2,1)S(1)} %slice.56), channel_id=1, source_target_pairs={{0,8},{1,9},{2,10},{3,11},{4,12},{5,13},{6,14},{7,15},{8,0},{9,1},... | collective-permute-start | bytes 688136 | tf_op jit(solution)/shard_map/ppermute | solution.py:22
  (33 other events, 252.1 us)

commit v7 on v6

--- a/solution.py
+++ b/solution.py
@@ -296,10 +296,11 @@
     down2 = shift(jnp.concatenate([down1, other_a]), "z", -1)
     swapped1 = swap(jnp.concatenate([up1[a:], down1[a:]]), "yl")
     twice_own, twice_far = shift(left1, "x", 1), shift(right2, "x", -1)
+    small = (weight, residual, diag, slot, row, prior_prec[None], posterior[None])
     up2, down2, swapped1, twice_own, twice_far, *small = together(
-        up2, down2, swapped1, twice_own, twice_far, weight, residual, diag, slot, row
-    )
-    weight, residual, diag, slot, row = small
+        up2, down2, swapped1, twice_own, twice_far, *small
+    )
+    weight, residual, diag, slot, row, prior, point = small
     put(up1, (2, 0, 0, n))
     put(down1, (4, 0, 0, n))
     put(swapped1, (3, a, 0, b), (5, a, b, b))
@@ -310,7 +311,7 @@
     same = jnp.stack(same)
     other = swap(same, "c")
     left, gradient = prepare(
-        slot, row, same, other, weight, residual, prior_prec[None], posterior[None]
+        slot, row, same, other, weight, residual, prior, point
     )
     up3, down3, swap_u2, swap_d2, left = together(up3, down3, swap_u2, swap_d2, left)
     put(up2, (6, 0, 0, a), (3, 0, a, a), (6, a, 2 * a, b))

time: 113 us -> 113 us (level)
  waiting for transfers between devices: 18.9 us -> 20.2 us
    ppermute x25, waiting for transfers between devices: 7.59 us -> 9.94 us  [permuted(): return lax.ppermute(x, ('rows', 'feat'), pairs)]
    unnamed x68 -> x64, local copies, waits for them, and re-layouts: 5.46 us -> 3.76 us
  transfers between devices with their start and end apart: 27 -> 27, of which waited for: 5 -> 8; matrix products, arithmetic and copies ran while one was open for 8% -> 8% of each run, Pallas kernels for 20% -> 20%
where the time goes in v7:
time: 113 us
  starting transfers between devices  49.9 us (44%)
  Pallas kernels  28.5 us (25%)
  waiting for transfers between devices  20.2 us (18%)
  local copies, waits for them, and re-layouts  7.82 us (7%)
  other arithmetic  3.53 us (3%)
  between operations  1.81 us (2%)
  matrix products  1.19 us (1%)
    ppermute x25, starting transfers between devices, permuted(): return lax.ppermute(x, ('rows', 'feat'), pairs)  36.1 us
    pallas_call x3, Pallas kernels, gram(): pl.pallas_call(lambda *refs: gram_kernel(slots, first, n, len(pieces), cu...  20.2 us
    all_to_all x2, starting transfers between devices, from_all(): return lax.all_to_all(copies, axis, split_axis=0, concat_axis=0, tiled=True)  13.8 us
    all_to_all x2, waiting for transfers between devices, from_all(): return lax.all_to_all(copies, axis, split_axis=0, concat_axis=0, tiled=True)  10.2 us
    ppermute x25, waiting for transfers between devices, permuted(): return lax.ppermute(x, ('rows', 'feat'), pairs)  9.94 us
    pallas_call x1, Pallas kernels, prepare(): pl.pallas_call(prepare_kernel, in_specs=[smem, smem] + [anywhere] * 2 + [...  8.28 us
    unnamed x64, local copies, waits for them, and re-layouts  3.76 us
  transfers between devices with their start and end apart: 27, of which 8 were waited for; matrix products, arithmetic and copies ran while one was open for 8% of the time, Pallas kernels for 20%

profile of v7, /device:TPU:64, one launch (start us, length us, event | category | flops | bytes accessed | tf_op | source)
XLA Modules:
  0.0 112.9 jit_solution(464650959512307958)
XLA Ops:
  0.6 3.3 %collective-permute-start = (bf16[192,1024]{1,0:T(8,128)(2,1)}, bf16[192,1024]{1,0:T(8,128)(2,1)S(1)}, u32[]{:S(2)}, u32[]{:S(2)}) collective-permute-start(bf16[192,1024]{1,0:T(8,128)(2,1)} %param.4), channel_id=1, source_target_pairs={{0,128},{1,129},{2,130},{3,131},{4,132},{5,133},{6,134},{7,135},{8... | collective-permute-start | bytes 1179656 | tf_op jit(solution)/shard_map/ppermute | solution.py:22
  3.9 1.5 %collective-permute-start.1 = (bf16[192,1024]{1,0:T(8,128)(2,1)}, bf16[192,1024]{1,0:T(8,128)(2,1)S(1)}, u32[]{:S(2)}, u32[]{:S(2)}) collective-permute-start(bf16[192,1024]{1,0:T(8,128)(2,1)} %param.4), channel_id=1, source_target_pairs={{0,32},{1,33},{2,34},{3,35},{4,36},{5,37},{6,38},{7,39},{8,40},{9,... | collective-permute-start | bytes 1179656 | tf_op jit(solution)/shard_map/ppermute | solution.py:22
  5.4 1.7 %collective-permute-start.2 = (bf16[192,1024]{1,0:T(8,128)(2,1)}, bf16[192,1024]{1,0:T(8,128)(2,1)S(1)}, u32[]{:S(2)}, u32[]{:S(2)}) collective-permute-start(bf16[192,1024]{1,0:T(8,128)(2,1)} %param.4), channel_id=1, source_target_pairs={{0,96},{1,97},{2,98},{3,99},{4,100},{5,101},{6,102},{7,103},{8,104... | collective-permute-start | bytes 1179656 | tf_op jit(solution)/shard_map/ppermute | solution.py:22
  7.1 2.2 %collective-permute-start.3 = (bf16[192,1024]{1,0:T(8,128)(2,1)}, bf16[192,1024]{1,0:T(8,128)(2,1)S(1)}, u32[]{:S(2)}, u32[]{:S(2)}) collective-permute-start(bf16[192,1024]{1,0:T(8,128)(2,1)} %param.4), channel_id=1, source_target_pairs={{0,0},{1,17},{2,34},{3,51},{4,68},{5,85},{6,102},{7,119},{8,128},{... | collective-permute-start | bytes 1179656 | tf_op jit(solution)/shard_map/ppermute | solution.py:22
  11.9 9.7 %all-to-all-start = ((f32[16,1,192]{2,1,0:T(1,128)}), f32[16,1,192]{2,1,0:T(1,128)S(1)}, u32[]{:S(2)}, u32[]{:S(2)}) async-start(f32[16,1,192]{2,1,0:T(1,128)} %broadcast_in_dim.19), calls=%async_computation | async-start | bytes 32768 | tf_op jit(solution)/shard_map/all_to_all | solution.py:41
  22.2 5.7 %all-to-all-done = f32[16,1,192]{2,1,0:T(1,128)S(1)} async-done(((f32[16,1,192]{2,1,0:T(1,128)}), f32[16,1,192]{2,1,0:T(1,128)S(1)}, u32[]{:S(2)}, u32[]{:S(2)}) %all-to-all-start) | async-done | bytes 12320 | tf_op jit(solution)/shard_map/all_to_all | solution.py:41
  28.6 1.5 %collective-permute-start.5 = (bf16[192,1024]{1,0:T(8,128)(2,1)S(1)}, bf16[192,1024]{1,0:T(8,128)(2,1)S(1)}, u32[]{:S(2)}, u32[]{:S(2)}) collective-permute-start(bf16[192,1024]{1,0:T(8,128)(2,1)S(1)} %collective-permute-done.3.refs_1_), channel_id=1, source_target_pairs={{0,7},{1,0},{2,1},{3,2},{4,3},{5,4},{6,5},{7,6},{8,15},{9,8},{10,9... | collective-permute-start | bytes 1179656 | tf_op jit(solution)/shard_map/ppermute | solution.py:22
  31.2 2.7 %collective-permute-start.8 = (bf16[192,1024]{1,0:T(8,128)(2,1)S(1)}, bf16[192,1024]{1,0:T(8,128)(2,1)S(1)}, u32[]{:S(2)}, u32[]{:S(2)}) collective-permute-start(bf16[192,1024]{1,0:T(8,128)(2,1)S(1)} %collective-permute-done), channel_id=1, source_target_pairs={{0,96},{1,97},{2,98},{3,99},{4,100},{5,101},{6,102},{7,103},{8,104... | collective-permute-start | bytes 1179656 | tf_op jit(solution)/shard_map/ppermute | solution.py:22
  34.5 4.1 %all-to-all-start.1 = ((f32[16,2,192]{2,1,0:T(2,128)}), f32[16,2,192]{2,1,0:T(2,128)}, u32[]{:S(2)}, u32[]{:S(2)}) async-start(f32[16,2,192]{2,1,0:T(2,128)} %broadcast_in_dim.20), calls=%async_computation.1 | async-start | bytes 65536 | tf_op jit(solution)/shard_map/all_to_all | solution.py:41
  41.7 4.6 %all-to-all-done.1 = f32[16,2,192]{2,1,0:T(2,128)} async-done(((f32[16,2,192]{2,1,0:T(2,128)}), f32[16,2,192]{2,1,0:T(2,128)}, u32[]{:S(2)}, u32[]{:S(2)}) %all-to-all-start.1) | async-done | bytes 24608 | tf_op jit(solution)/shard_map/all_to_all | solution.py:41
  46.6 1.5 %collective-permute-start.10 = (bf16[272,1024]{1,0:T(8,128)(2,1)S(1)}, bf16[272,1024]{1,0:T(8,128)(2,1)S(1)}, u32[]{:S(2)}, u32[]{:S(2)}) collective-permute-start(bf16[272,1024]{1,0:T(8,128)(2,1)S(1)} %get-tuple-element.86), channel_id=1, source_target_pairs={{0,7},{1,0},{2,1},{3,2},{4,3},{5,4},{6,5},{7,6},{8,15},{9,8},{10,9... | collective-permute-start | bytes 1671176 | tf_op jit(solution)/shard_map/ppermute | solution.py:22
  48.8 1.5 %collective-permute-start.11 = (bf16[224,1024]{1,0:T(8,128)(2,1)S(1)}, bf16[224,1024]{1,0:T(8,128)(2,1)S(1)}, u32[]{:S(2)}, u32[]{:S(2)}) collective-permute-start(bf16[224,1024]{1,0:T(8,128)(2,1)S(1)} %pad_maximum_fusion.2), channel_id=1, source_target_pairs={{0,8},{1,9},{2,10},{3,11},{4,12},{5,13},{6,14},{7,15},{8,0},{9,1},... | collective-permute-start | bytes 1376264 | tf_op jit(solution)/shard_map/ppermute | solution.py:22
  50.9 2.7 %collective-permute-start.13 = (bf16[192,1024]{1,0:T(8,128)(2,1)}, bf16[192,1024]{1,0:T(8,128)(2,1)S(1)}, u32[]{:S(2)}, u32[]{:S(2)}) collective-permute-start(bf16[192,1024]{1,0:T(8,128)(2,1)} %copy-done.17), channel_id=1, source_target_pairs={{0,96},{1,97},{2,98},{3,99},{4,100},{5,101},{6,102},{7,103},{8,104... | collective-permute-start | bytes 1179656 | tf_op jit(solution)/shard_map/ppermute | solution.py:22
  53.6 1.5 %subtract_convert_fusion = (bf16[16,1,192]{2,1,0:T(2,128)(2,1)}, f32[16,1,192]{2,1,0:T(1,128)S(1)}) fusion(f32[16,2,192]{2,1,0:T(2,128)} %all-to-all-done.1), kind=kLoop, calls=%fused_computation.14 | loop fusion | flops 15360 | bytes 43008 | tf_op jit(solution)/shard_map/convert_element_type | solution.py:289
  56.5 5.3 %collective-permute-done.12 = bf16[192,1024]{1,0:T(8,128)(2,1)S(1)} collective-permute-done((bf16[192,1024]{1,0:T(8,128)(2,1)S(1)}, bf16[192,1024]{1,0:T(8,128)(2,1)S(1)}, u32[]{:S(2)}, u32[]{:S(2)}) %collective-permute-start.12) | collective-permute-done | bytes 393248 | tf_op jit(solution)/shard_map/ppermute | solution.py:22
  61.9 1.9 %collective-permute-done.9.refs_6_ = bf16[272,1024]{1,0:T(8,128)(2,1)S(1)} collective-permute-done((bf16[272,1024]{1,0:T(8,128)(2,1)S(1)}, bf16[272,1024]{1,0:T(8,128)(2,1)S(1)}, u32[]{:S(2)}, u32[]{:S(2)}) %collective-permute-start.9) | collective-permute-done | bytes 557088 | tf_op jit(solution)/shard_map/ppermute | solution.py:22
  64.2 1.4 %copy-done.2 = bf16[8,192,1024]{2,1,0:T(8,128)(2,1)} copy-done((bf16[8,192,1024]{2,1,0:T(8,128)(2,1)}, bf16[8,192,1024]{2,1,0:T(8,128)(2,1)S(1)}, u32[]{:S(2)}) %copy-start.2) | copy-done | bytes 3145752
  69.9 8.3 %prepare.1 = (bf16[1024,3072]{1,0:T(8,128)(2,1)}, f32[1,1024]{1,0:T(1,128)}) custom-call(s32[16]{0:T(128)} %stack.157.slot_ref, s32[16]{0:T(128)} %stack.174.row_ref, bf16[8,192,1024]{2,1,0:T(8,128)(2,1)} %copy-done.2, bf16[8,192,1024]{2,1,0:T(8,128)(2,1)} %collective-permute-done.18.refs_1_, f32[16,1,192]{2,1,0:T(1,128)} %fusion.1.refs_2_, ...), custom_call_target="tpu_custom_call" | custom-call | flops 1 | bytes 1 | tf_op jit(solution)/shard_map/prepare/pallas_call | solution.py:95
  81.4 2.5 %collective-permute-start.19 = (bf16[160,1024]{1,0:T(8,128)(2,1)S(1)}, bf16[160,1024]{1,0:T(8,128)(2,1)S(1)}, u32[]{:S(2)}, u32[]{:S(2)}) collective-permute-start(bf16[160,1024]{1,0:T(8,128)(2,1)S(1)} %slice.51), channel_id=1, source_target_pairs={{0,1},{1,2},{2,3},{3,4},{4,5},{5,6},{6,7},{7,0},{8,9},{9,10},{10,1... | collective-permute-start | bytes 983048 | tf_op jit(solution)/shard_map/ppermute | solution.py:22
  86.1 8.4 %gram.3.refs_7_ = bf16[1024,1024]{1,0:T(8,128)(2,1)} custom-call(bf16[1024,3072]{1,0:T(8,128)(2,1)} %get-tuple-element.71.refs_0_, bf16[192,1024]{1,0:T(8,128)(2,1)} %copy-done.12, bf16[192,1024]{1,0:T(8,128)(2,1)} %copy-done.10, bf16[192,1024]{1,0:T(8,128)(2,1)} %copy-done.6, bf16[192,1024]{1,0:T(8,128)(2,1)} %copy-done.4, bf16[224,1024]{1,0:T(8,128)(2,1)} %copy-done.11, ...), custom_call_target="tpu_custom_call" | custom-call | flops 1 | bytes 1 | tf_op jit(solution)/shard_map/gram/pallas_call | solution.py:211
  94.7 1.6 %collective-permute-start.24 = (bf16[112,1024]{1,0:T(8,128)(2,1)S(1)}, bf16[112,1024]{1,0:T(8,128)(2,1)S(1)}, u32[]{:S(2)}, u32[]{:S(2)}) collective-permute-start(bf16[112,1024]{1,0:T(8,128)(2,1)S(1)} %slice.56), channel_id=1, source_target_pairs={{0,8},{1,9},{2,10},{3,11},{4,12},{5,13},{6,14},{7,15},{8,0},{9,1},... | collective-permute-start | bytes 688136 | tf_op jit(solution)/shard_map/ppermute | solution.py:22
  96.2 3.3 %collective-permute-start.23 = (bf16[80,1024]{1,0:T(8,128)(2,1)S(1)}, bf16[80,1024]{1,0:T(8,128)(2,1)S(1)}, u32[]{:S(2)}, u32[]{:S(2)}) collective-permute-start(bf16[80,1024]{1,0:T(8,128)(2,1)S(1)} %slice.55), channel_id=1, source_target_pairs={{0,1},{1,2},{2,3},{3,4},{4,5},{5,6},{6,7},{7,0},{8,9},{9,10},{10,1... | collective-permute-start | bytes 491528 | tf_op jit(solution)/shard_map/ppermute | solution.py:22
  99.5 6.1 %gram.4.refs_5_ = bf16[1024,1024]{1,0:T(8,128)(2,1)} custom-call(bf16[1024,3072]{1,0:T(8,128)(2,1)} %get-tuple-element.71.refs_0_, bf16[272,1024]{1,0:T(8,128)(2,1)} %copy-done.1, bf16[272,1024]{1,0:T(8,128)(2,1)} %copy-done, bf16[112,1024]{1,0:T(8,128)(2,1)} %copy-done.23, bf16[112,1024]{1,0:T(8,128)(2,1)} %copy-done.24, bf16[160,1024]{1,0:T(8,128)(2,1)} %copy-done.5, ...), custom_call_target="tpu_custom_call" | custom-call | flops 1 | bytes 1 | tf_op jit(solution)/shard_map/gram/pallas_call | solution.py:211
  107.0 5.6 %gram.5 = f32[1024,1024]{1,0:T(8,128)} custom-call(bf16[1024,3072]{1,0:T(8,128)(2,1)} %get-tuple-element.71.refs_0_, bf16[160,1024]{1,0:T(8,128)(2,1)} %copy-done.5, bf16[192,1024]{1,0:T(8,128)(2,1)} %copy-done.3, bf16[80,1024]{1,0:T(8,128)(2,1)} %copy-done.26, bf16[112,1024]{1,0:T(8,128)(2,1)} %copy-done.25, bf16[1024,1024]{1,0:T(8,128)(2,1)} %gram.4.refs_5_, ...), custom_call_target="tpu_custom_call" | custom-call | flops 1 | bytes 1 | tf_op jit(solution)/shard_map/gram/pallas_call | solution.py:211
  (125 shorter events, 22.4 us)
Async XLA Ops:
  0.6 27.3 %collective-permute-start = (bf16[192,1024]{1,0:T(8,128)(2,1)}, bf16[192,1024]{1,0:T(8,128)(2,1)S(1)}, u32[]{:S(2)}, u32[]{:S(2)}) collective-permute-start(bf16[192,1024]{1,0:T(8,128)(2,1)} %param.4), channel_id=1, source_target_pairs={{0,128},{1,129},{2,130},{3,131},{4,132},{5,133},{6,134},{7,135},{8... | collective-permute-start | bytes 1179656 | tf_op jit(solution)/shard_map/ppermute | solution.py:22
  3.9 24.0 %collective-permute-start.1 = (bf16[192,1024]{1,0:T(8,128)(2,1)}, bf16[192,1024]{1,0:T(8,128)(2,1)S(1)}, u32[]{:S(2)}, u32[]{:S(2)}) collective-permute-start(bf16[192,1024]{1,0:T(8,128)(2,1)} %param.4), channel_id=1, source_target_pairs={{0,32},{1,33},{2,34},{3,35},{4,36},{5,37},{6,38},{7,39},{8,40},{9,... | collective-permute-start | bytes 1179656 | tf_op jit(solution)/shard_map/ppermute | solution.py:22
  5.4 22.5 %collective-permute-start.2 = (bf16[192,1024]{1,0:T(8,128)(2,1)}, bf16[192,1024]{1,0:T(8,128)(2,1)S(1)}, u32[]{:S(2)}, u32[]{:S(2)}) collective-permute-start(bf16[192,1024]{1,0:T(8,128)(2,1)} %param.4), channel_id=1, source_target_pairs={{0,96},{1,97},{2,98},{3,99},{4,100},{5,101},{6,102},{7,103},{8,104... | collective-permute-start | bytes 1179656 | tf_op jit(solution)/shard_map/ppermute | solution.py:22
  7.1 20.8 %collective-permute-start.3 = (bf16[192,1024]{1,0:T(8,128)(2,1)}, bf16[192,1024]{1,0:T(8,128)(2,1)S(1)}, u32[]{:S(2)}, u32[]{:S(2)}) collective-permute-start(bf16[192,1024]{1,0:T(8,128)(2,1)} %param.4), channel_id=1, source_target_pairs={{0,0},{1,17},{2,34},{3,51},{4,68},{5,85},{6,102},{7,119},{8,128},{... | collective-permute-start | bytes 1179656 | tf_op jit(solution)/shard_map/ppermute | solution.py:22
  11.9 16.0 %all-to-all-start = ((f32[16,1,192]{2,1,0:T(1,128)}), f32[16,1,192]{2,1,0:T(1,128)S(1)}, u32[]{:S(2)}, u32[]{:S(2)}) async-start(f32[16,1,192]{2,1,0:T(1,128)} %broadcast_in_dim.19), calls=%async_computation | async-start | bytes 32768 | tf_op jit(solution)/shard_map/all_to_all | solution.py:41
  28.0 18.3 %collective-permute-start.4 = (bf16[192,1024]{1,0:T(8,128)(2,1)S(1)}, bf16[192,1024]{1,0:T(8,128)(2,1)S(1)}, u32[]{:S(2)}, u32[]{:S(2)}) collective-permute-start(bf16[192,1024]{1,0:T(8,128)(2,1)S(1)} %collective-permute-done.3.refs_1_), channel_id=1, source_target_pairs={{0,1},{1,2},{2,3},{3,4},{4,5},{5,6},{6,7},{7,0},{8,9},{9,10},{10,1... | collective-permute-start | bytes 1179656 | tf_op jit(solution)/shard_map/ppermute | solution.py:22
  28.6 17.7 %collective-permute-start.5 = (bf16[192,1024]{1,0:T(8,128)(2,1)S(1)}, bf16[192,1024]{1,0:T(8,128)(2,1)S(1)}, u32[]{:S(2)}, u32[]{:S(2)}) collective-permute-start(bf16[192,1024]{1,0:T(8,128)(2,1)S(1)} %collective-permute-done.3.refs_1_), channel_id=1, source_target_pairs={{0,7},{1,0},{2,1},{3,2},{4,3},{5,4},{6,5},{7,6},{8,15},{9,8},{10,9... | collective-permute-start | bytes 1179656 | tf_op jit(solution)/shard_map/ppermute | solution.py:22
  30.1 16.2 %collective-permute-start.6 = (bf16[192,1024]{1,0:T(8,128)(2,1)S(1)}, bf16[192,1024]{1,0:T(8,128)(2,1)S(1)}, u32[]{:S(2)}, u32[]{:S(2)}) collective-permute-start(bf16[192,1024]{1,0:T(8,128)(2,1)S(1)} %collective-permute-done.3.refs_1_), channel_id=1, source_target_pairs={{0,8},{1,9},{2,10},{3,11},{4,12},{5,13},{6,14},{7,15},{8,0},{9,1},... | collective-permute-start | bytes 1179656 | tf_op jit(solution)/shard_map/ppermute | solution.py:22
  30.7 15.7 %collective-permute-start.7 = (bf16[192,1024]{1,0:T(8,128)(2,1)S(1)}, bf16[192,1024]{1,0:T(8,128)(2,1)S(1)}, u32[]{:S(2)}, u32[]{:S(2)}) collective-permute-start(bf16[192,1024]{1,0:T(8,128)(2,1)S(1)} %collective-permute-done), channel_id=1, source_target_pairs={{0,32},{1,33},{2,34},{3,35},{4,36},{5,37},{6,38},{7,39},{8,40},{9,... | collective-permute-start | bytes 1179656 | tf_op jit(solution)/shard_map/ppermute | solution.py:22
  31.2 15.2 %collective-permute-start.8 = (bf16[192,1024]{1,0:T(8,128)(2,1)S(1)}, bf16[192,1024]{1,0:T(8,128)(2,1)S(1)}, u32[]{:S(2)}, u32[]{:S(2)}) collective-permute-start(bf16[192,1024]{1,0:T(8,128)(2,1)S(1)} %collective-permute-done), channel_id=1, source_target_pairs={{0,96},{1,97},{2,98},{3,99},{4,100},{5,101},{6,102},{7,103},{8,104... | collective-permute-start | bytes 1179656 | tf_op jit(solution)/shard_map/ppermute | solution.py:22
  34.5 11.7 %all-to-all-start.1 = ((f32[16,2,192]{2,1,0:T(2,128)}), f32[16,2,192]{2,1,0:T(2,128)}, u32[]{:S(2)}, u32[]{:S(2)}) async-start(f32[16,2,192]{2,1,0:T(2,128)} %broadcast_in_dim.20), calls=%async_computation.1 | async-start | bytes 65536 | tf_op jit(solution)/shard_map/all_to_all | solution.py:41
  46.6 15.3 %collective-permute-start.10 = (bf16[272,1024]{1,0:T(8,128)(2,1)S(1)}, bf16[272,1024]{1,0:T(8,128)(2,1)S(1)}, u32[]{:S(2)}, u32[]{:S(2)}) collective-permute-start(bf16[272,1024]{1,0:T(8,128)(2,1)S(1)} %get-tuple-element.86), channel_id=1, source_target_pairs={{0,7},{1,0},{2,1},{3,2},{4,3},{5,4},{6,5},{7,6},{8,15},{9,8},{10,9... | collective-permute-start | bytes 1671176 | tf_op jit(solution)/shard_map/ppermute | solution.py:22
  48.2 15.6 %collective-permute-start.9 = (bf16[272,1024]{1,0:T(8,128)(2,1)S(1)}, bf16[272,1024]{1,0:T(8,128)(2,1)S(1)}, u32[]{:S(2)}, u32[]{:S(2)}) collective-permute-start(bf16[272,1024]{1,0:T(8,128)(2,1)S(1)} %get-tuple-element.87), channel_id=1, source_target_pairs={{0,1},{1,2},{2,3},{3,4},{4,5},{5,6},{6,7},{7,0},{8,9},{9,10},{10,1... | collective-permute-start | bytes 1671176 | tf_op jit(solution)/shard_map/ppermute | solution.py:22
  48.8 13.0 %collective-permute-start.11 = (bf16[224,1024]{1,0:T(8,128)(2,1)S(1)}, bf16[224,1024]{1,0:T(8,128)(2,1)S(1)}, u32[]{:S(2)}, u32[]{:S(2)}) collective-permute-start(bf16[224,1024]{1,0:T(8,128)(2,1)S(1)} %pad_maximum_fusion.2), channel_id=1, source_target_pairs={{0,8},{1,9},{2,10},{3,11},{4,12},{5,13},{6,14},{7,15},{8,0},{9,1},... | collective-permute-start | bytes 1376264 | tf_op jit(solution)/shard_map/ppermute | solution.py:22
  50.4 11.5 %collective-permute-start.12 = (bf16[192,1024]{1,0:T(8,128)(2,1)S(1)}, bf16[192,1024]{1,0:T(8,128)(2,1)S(1)}, u32[]{:S(2)}, u32[]{:S(2)}) collective-permute-start(bf16[192,1024]{1,0:T(8,128)(2,1)S(1)} %copy-done.14), channel_id=1, source_target_pairs={{0,32},{1,33},{2,34},{3,35},{4,36},{5,37},{6,38},{7,39},{8,40},{9,... | collective-permute-start | bytes 1179656 | tf_op jit(solution)/shard_map/ppermute | solution.py:22
  50.9 10.9 %collective-permute-start.13 = (bf16[192,1024]{1,0:T(8,128)(2,1)}, bf16[192,1024]{1,0:T(8,128)(2,1)S(1)}, u32[]{:S(2)}, u32[]{:S(2)}) collective-permute-start(bf16[192,1024]{1,0:T(8,128)(2,1)} %copy-done.17), channel_id=1, source_target_pairs={{0,96},{1,97},{2,98},{3,99},{4,100},{5,101},{6,102},{7,103},{8,104... | collective-permute-start | bytes 1179656 | tf_op jit(solution)/shard_map/ppermute | solution.py:22
  65.6 13.8 %collective-permute-start.14 = (bf16[272,1024]{1,0:T(8,128)(2,1)S(1)}, bf16[272,1024]{1,0:T(8,128)(2,1)S(1)}, u32[]{:S(2)}, u32[]{:S(2)}) collective-permute-start(bf16[272,1024]{1,0:T(8,128)(2,1)S(1)} %collective-permute-done.9.refs_6_), channel_id=1, source_target_pairs={{0,1},{1,2},{2,3},{3,4},{4,5},{5,6},{6,7},{7,0},{8,9},{9,10},{10,1... | collective-permute-start | bytes 1671176 | tf_op jit(solution)/shard_map/ppermute | solution.py:22
  66.9 13.9 %collective-permute-start.15 = (bf16[272,1024]{1,0:T(8,128)(2,1)S(1)}, bf16[272,1024]{1,0:T(8,128)(2,1)S(1)}, u32[]{:S(2)}, u32[]{:S(2)}) collective-permute-start(bf16[272,1024]{1,0:T(8,128)(2,1)S(1)} %collective-permute-done.10.refs_7_), channel_id=1, source_target_pairs={{0,7},{1,0},{2,1},{3,2},{4,3},{5,4},{6,5},{7,6},{8,15},{9,8},{10,9... | collective-permute-start | bytes 1671176 | tf_op jit(solution)/shard_map/ppermute | solution.py:22
  67.7 10.6 %collective-permute-start.16 = (bf16[112,1024]{1,0:T(8,128)(2,1)S(1)}, bf16[112,1024]{1,0:T(8,128)(2,1)S(1)}, u32[]{:S(2)}, u32[]{:S(2)}) collective-permute-start(bf16[112,1024]{1,0:T(8,128)(2,1)S(1)} %slice.49), channel_id=1, source_target_pairs={{0,8},{1,9},{2,10},{3,11},{4,12},{5,13},{6,14},{7,15},{8,0},{9,1},... | collective-permute-start | bytes 688136 | tf_op jit(solution)/shard_map/ppermute | solution.py:22
  69.1 9.8 %collective-permute-start.17 = (bf16[112,1024]{1,0:T(8,128)(2,1)S(1)}, bf16[112,1024]{1,0:T(8,128)(2,1)S(1)}, u32[]{:S(2)}, u32[]{:S(2)}) collective-permute-start(bf16[112,1024]{1,0:T(8,128)(2,1)S(1)} %slice.50), channel_id=1, source_target_pairs={{0,8},{1,9},{2,10},{3,11},{4,12},{5,13},{6,14},{7,15},{8,0},{9,1},... | collective-permute-start | bytes 688136 | tf_op jit(solution)/shard_map/ppermute | solution.py:22
  80.8 13.8 %collective-permute-start.20 = (bf16[192,1024]{1,0:T(8,128)(2,1)S(1)}, bf16[192,1024]{1,0:T(8,128)(2,1)S(1)}, u32[]{:S(2)}, u32[]{:S(2)}) collective-permute-start(bf16[192,1024]{1,0:T(8,128)(2,1)S(1)} %slice.52), channel_id=1, source_target_pairs={{0,7},{1,0},{2,1},{3,2},{4,3},{5,4},{6,5},{7,6},{8,15},{9,8},{10,9... | collective-permute-start | bytes 1179656 | tf_op jit(solution)/shard_map/ppermute | solution.py:22
  81.4 13.1 %collective-permute-start.19 = (bf16[160,1024]{1,0:T(8,128)(2,1)S(1)}, bf16[160,1024]{1,0:T(8,128)(2,1)S(1)}, u32[]{:S(2)}, u32[]{:S(2)}) collective-permute-start(bf16[160,1024]{1,0:T(8,128)(2,1)S(1)} %slice.51), channel_id=1, source_target_pairs={{0,1},{1,2},{2,3},{3,4},{4,5},{5,6},{6,7},{7,0},{8,9},{9,10},{10,1... | collective-permute-start | bytes 983048 | tf_op jit(solution)/shard_map/ppermute | solution.py:22
  84.0 10.5 %collective-permute-start.21 = (bf16[112,1024]{1,0:T(8,128)(2,1)S(1)}, bf16[112,1024]{1,0:T(8,128)(2,1)S(1)}, u32[]{:S(2)}, u32[]{:S(2)}) collective-permute-start(bf16[112,1024]{1,0:T(8,128)(2,1)S(1)} %slice.53), channel_id=1, source_target_pairs={{0,8},{1,9},{2,10},{3,11},{4,12},{5,13},{6,14},{7,15},{8,0},{9,1},... | collective-permute-start | bytes 688136 | tf_op jit(solution)/shard_map/ppermute | solution.py:22
  94.7 11.1 %collective-permute-start.24 = (bf16[112,1024]{1,0:T(8,128)(2,1)S(1)}, bf16[112,1024]{1,0:T(8,128)(2,1)S(1)}, u32[]{:S(2)}, u32[]{:S(2)}) collective-permute-start(bf16[112,1024]{1,0:T(8,128)(2,1)S(1)} %slice.56), channel_id=1, source_target_pairs={{0,8},{1,9},{2,10},{3,11},{4,12},{5,13},{6,14},{7,15},{8,0},{9,1},... | collective-permute-start | bytes 688136 | tf_op jit(solution)/shard_map/ppermute | solution.py:22
  (31 other events, 234.8 us)
